TPU v7x, 256 devices: a whole 4x4x8 slice. The times are simulated.
256 devices in a mesh: slab: 16 (over z_lo, y), front: 16 (over x, z_hi, core).
Axes of the slice: x: 4, y: 4, z: 8 (z_hi: 2, z_lo: 4; z = z_hi * 4 + z_lo), core: 2. Of those that a mesh axis runs over, the one named last changes fastest.
Arguments:
- sources: float32 [2, 16, 16384, 128], P(None, 'slab', 'front'), may hold values from -6 to 6
- front_inv: float32 [16, 16384, 512], P('slab', 'front'), may hold values from -0.25 to 0.25
- pattern: int32 [16, 256, 4], P('slab', 'front'), may hold values from 0 to 15, all different within a row
- tree: int32 [16, 16, 4], P('slab', 'front'), may hold values from 0 to 15, all different within a row
- lift: float32 [16, 8192, 256], P('slab', 'front'), may hold values from -0.1875 to 0.1875
- spread: float32 [16, 2048, 1024], P('slab', 'front'), may hold values from -0.1875 to 0.1875
- couple: float32 [16, 2048, 256], P('slab', 'front'), may hold values from -0.375 to 0.375
- sep_inv: float32 [16, 2048, 4096], P('slab', 'front'), may hold values from -0.09375 to 0.09375
- inflow: float32 [16, 2048, 128], P('slab', 'front'), may hold values from -6 to 6
Outputs:
- leaf_field: float32 [2, 16, 16384, 128], P(None, 'slab', 'front')
Inputs may be any that keep to these rules, and one draw needn't show every extreme that they name: `pattern`: each block row names 4 different block columns. `tree`: each leaf names 4 different separator blocks.
All inputs are finite; a program needn't handle non-finite values.
Results may differ from a plain program's by a relative error of at most 0.0001.
Values sent between devices are 32-bit elements; how exact they have to be, the bound alone decides.
No kernel may reach another device: no remote copies, remote signals or barrier semaphores. Data moves between devices by JAX's collectives and lax.ppermute only.
A program may use at most 128 MiB of HBM per device.

v0:
```python
import functools

import jax
import jax.numpy as jnp
from jax import lax
from jax.experimental import pallas as pl
from jax.experimental.pallas import tpu as pltpu
from jax.sharding import Mesh
from jax.sharding import PartitionSpec as P

BEATS = 2
LEAF = 1024
SEP = 2048
BLK = 64
NB = 4
BND = 128
P_SIZE = 4
BROWS = LEAF // BLK
FRONT = ("front_0", "front_1", "front_2")
X, Z, C = FRONT
NX = 4
HALF = SEP // 2
QUARTER = HALF // NX
F32 = jnp.float32
BF16 = jnp.bfloat16


def twist(field):
    half = field.shape[-1] // 2
    lane = lax.broadcasted_iota(jnp.int32, field.shape, len(field.shape) - 1)
    turned = pltpu.roll(field, half, len(field.shape) - 1)
    return jnp.where(lane < half, -turned, turned)


def split(a):
    high = a.astype(BF16)
    low = (a - high.astype(F32)).astype(BF16)
    return high, low


def mm(a, b):
    return jnp.dot(a, b, preferred_element_type=F32)


def rows_split(a):
    return jnp.concatenate(split(a), axis=0)


def cols_split(b):
    return jnp.concatenate(split(b), axis=1)


def product(stacked, paired):
    rows, cols = stacked.shape[0] // 2, paired.shape[1] // 2
    full = mm(stacked, paired)
    return full[:rows, :cols] + (full[:rows, cols:] + full[rows:, :cols])


def packed(matrix, field):
    both = jnp.concatenate([field, twist(field)], axis=0)
    return product(rows_split(matrix), cols_split(both))


def front_rows(g, field):
    gh, gl = split(g)
    fh, fl = split(field)
    rows = g.shape[0]
    first = mm(jnp.concatenate([gh, gl], axis=0), fh)
    return first[:rows] + (first[rows:] + mm(gh, fl))


def gathered(patt_ref, row, take):
    both = []
    for k in range(NB):
        a, b = take(patt_ref[k, row])
        both.append(jnp.concatenate([a, b], axis=1))
        both.append(jnp.concatenate([twist(a), twist(b)], axis=1))
    return jnp.concatenate(both, axis=0)


def tail_columns(g, patt_ref, row):
    parts = []
    for block in (BROWS - 2, BROWS - 1):
        total = jnp.zeros((BLK, 2 * BLK), F32)
        for k in range(NB):
            held = (patt_ref[k, row] == block).astype(F32)
            total = total + held * g[:, k * 2 * BLK : (k + 1) * 2 * BLK]
        parts.append(total)
    return jnp.concatenate(parts, axis=1)


def tail_field(z):
    tz = twist(z)
    return jnp.concatenate([z[:BLK], tz[:BLK], z[BLK:], tz[BLK:]], axis=0)


def start_kernel(
    patt_ref, src_ref, g_ref, couple_ref, wave_ref, y_ref, drive_ref, g_out, blocks, held, couple, wave, sems
):
    copies = [
        pltpu.make_async_copy(g_ref.at[0, pl.ds(LEAF - BND, BND), :], held, sems.at[0]),
        pltpu.make_async_copy(couple_ref.at[0], couple, sems.at[1]),
        pltpu.make_async_copy(wave_ref.at[0], wave, sems.at[2]),
    ]
    for i in range(2):
        for k in range(NB):
            at = pl.ds(pl.multiple_of(patt_ref[k, BROWS - 2 + i] * BLK, BLK), BLK)
            n = i * NB + k
            copies.append(
                pltpu.make_async_copy(src_ref.at[:, 0, at, :], blocks.at[n], sems.at[3 + n])
            )
    for copy in copies:
        copy.start()
    for copy in copies:
        copy.wait()
    g_out[...] = held[...]
    for i in range(2):
        at = slice(i * BLK, (i + 1) * BLK)
        both = []
        for k in range(NB):
            pair = blocks[i * NB + k]
            both.append(jnp.concatenate([pair[0], pair[1]], axis=1))
            both.append(jnp.concatenate([twist(pair[0]), twist(pair[1])], axis=1))
        y = front_rows(held[at, :], jnp.concatenate(both, axis=0))
        y_ref[0, at, :] = y[:, :BND]
        y_ref[1, at, :] = y[:, BND:]
    drive_ref[...] = packed(couple[...], wave[...]) - y_ref[0]


def drive_kernel(couple_ref, wave_ref, y_ref, drive_ref):
    drive_ref[...] = packed(couple_ref[...], wave_ref[...]) - y_ref[0]


def owner_slot(distance, c):
    return jnp.where(distance == 1, 1 + c, jnp.where(distance == 3, 2 - c, (distance // 2) * 3))


def slot_distance(slot, c):
    return (0, 1 + 2 * c, 3 - 2 * c, 2)[slot]


def lift_kernel(own_tree, far_tree, own_ref, far_ref, own_lift, far_lift, *refs):
    outs, acc = refs[:-1], refs[-1]
    x, c = lax.axis_index(X), lax.axis_index(C)
    acc[...] = jnp.zeros_like(acc)
    parts = []
    for drive_ref, mat in ((own_ref, own_lift), (far_ref, far_lift)):
        drive = drive_ref[...]
        pair = cols_split(jnp.concatenate([drive, twist(drive)], axis=0))
        parts.append(product(rows_split(mat[...]), pair))
    for tree, part in zip((own_tree, far_tree), parts):
        for p in range(P_SIZE):
            block = tree[p]

            @pl.when(block // 8 == c)
            def _():
                owner = (block % 8) // 2
                slot = owner_slot(jnp.bitwise_xor(owner, x), c) * 2 + block % 2
                acc[slot] += part[p * BND : (p + 1) * BND]

    for i, out in enumerate(outs):
        out[:BND] = acc[2 * i]
        out[BND:] = acc[2 * i + 1]


def sep_kernel(*refs):
    pieces, (own_ref, far_ref, own_out, far_out) = refs[:-4], refs[-4:]
    x, c = lax.axis_index(X), lax.axis_index(C)
    total = None
    for slot, piece in enumerate(pieces):
        owner = jnp.bitwise_xor(x, slot_distance(slot, c))
        col = c * HALF + owner * QUARTER
        real = pl.ds(pl.multiple_of(col, QUARTER), QUARTER)
        imag = pl.ds(pl.multiple_of(SEP + col, QUARTER), QUARTER)
        rows = jnp.concatenate(
            [own_ref[:, real], own_ref[:, imag], far_ref[:, real], far_ref[:, imag]], axis=0
        )
        part = product(rows_split(rows), cols_split(piece[...]))
        total = part if total is None else total + part
    own_out[...] = total[:BND] + twist(total[BND : 2 * BND])
    far_out[...] = total[2 * BND : 3 * BND] + twist(total[3 * BND :])


def spread_kernel(own_tree, far_tree, *refs):
    pieces, (own_mat, far_mat, own_out, far_out, sol) = refs[:-5], refs[-5:]
    x, z, c = lax.axis_index(X), lax.axis_index(Z), lax.axis_index(C)
    for i, piece in enumerate(pieces):
        sol[i] = piece[...]
    for tree, mat, out in ((own_tree, own_mat, own_out), (far_tree, far_mat, far_out)):
        both = []
        for p in range(P_SIZE):
            block = tree[p]
            side = lax.rem((block // 2) % 2 + z, 2)
            slot = owner_slot(jnp.bitwise_xor(block // 4, x), c) * 2 + side
            field = sol[slot] * (block % 2 == c).astype(F32)
            both += [field, twist(field)]
        out[...] = product(rows_split(mat[...]), cols_split(jnp.concatenate(both, axis=0)))


def out_kernel(patt_ref, near_ref, far_ref, y_ref, g_ref, z_ref, out_ref):
    z = near_ref[...] + far_ref[...]
    z_ref[...] = z
    tail = cols_split(tail_field(z))
    for i in range(2):
        at = slice(i * BLK, (i + 1) * BLK)
        cols = tail_columns(g_ref[at, :], patt_ref, BROWS - 2 + i)
        out_ref[at, :] = y_ref[0, at, :] - product(rows_split(cols), tail)


STEPS = 2
STEP_ROWS = LEAF // STEPS
GROUP = 2


def bulk_kernel(step, patt_ref, src_ref, g_ref, first_ref, second_ref, cols_ref):
    def take(block):
        at = pl.ds(pl.multiple_of(block * BLK, BLK), BLK)
        return src_ref[0, 0, at, :], src_ref[1, 0, at, :]

    def some(n, carry):
        for i in range(GROUP):
            local = n * GROUP + i
            at = pl.ds(pl.multiple_of(local * BLK, BLK), BLK)
            low = pl.ds(pl.multiple_of(STEP_ROWS + local * BLK, BLK), BLK)
            row = step * (STEP_ROWS // BLK) + local
            g = g_ref[at, :]
            y = front_rows(g, gathered(patt_ref, row, take))
            first_ref[at, :] = y[:, :BND]
            second_ref[at, :] = y[:, BND:]
            cols_ref[at, :], cols_ref[low, :] = split(tail_columns(g, patt_ref, row))
        return carry

    lax.fori_loop(0, STEP_ROWS // BLK // GROUP, some, 0)


def field_kernel(near_ref, far_ref, *refs):
    y_refs, col_refs, out_ref = refs[:STEPS], refs[STEPS : 2 * STEPS], refs[-1]
    tail = cols_split(tail_field(near_ref[...] + far_ref[...]))
    for i in range(STEPS):
        at = slice(i * STEP_ROWS, (i + 1) * STEP_ROWS)
        out_ref[0, at, :] = y_refs[i][...] - product(col_refs[i][...], tail)


VM = pl.BlockSpec(memory_space=pltpu.VMEM)
SM = pl.BlockSpec(memory_space=pltpu.SMEM)


def shape(*dims):
    return jax.ShapeDtypeStruct(dims, F32)


ROOM = pltpu.CompilerParams(vmem_limit_bytes=12 << 20)


def cost(flops, size):
    return pl.CostEstimate(flops=flops, bytes_accessed=size, transcendentals=0)


def shifted(value, axis, distance):
    size = lax.axis_size(axis)
    return lax.ppermute(value, axis, [(i, (i + distance) % size) for i in range(size)])


def swapped(value, axis):
    return shifted(value, axis, 1)


HB = pl.BlockSpec(memory_space=pl.ANY)
FULL = pltpu.CompilerParams(vmem_limit_bytes=66_000_000)
NEAR1 = (1, 0, 3, 2)
NEAR3 = (3, 2, 1, 0)


def beside(value, turn):
    route = []
    for x in range(NX):
        for c in range(2):
            route.append((2 * x + c, 2 * (NEAR1, NEAR3)[(turn + c) % 2][x] + c))
    return lax.ppermute(value, (X, C), route)


def sweep(sources, front_inv, pattern, tree, lift, spread, couple, sep_inv, inflow):
    gmat, own_tree, patt = front_inv[0], tree[0, 0], pattern[0].T
    own_lift, own_spread, kmat, own_sep = lift[0], spread[0], couple[0], sep_inv[0]
    whole = lambda *dims: pl.BlockSpec(dims, lambda *i: (0,) * len(dims))
    block, double = shape(BND, BND), shape(2 * BND, BND)

    far_tree = swapped(own_tree, C)
    far_lift = swapped(own_lift, C)
    far_sep = swapped(own_sep, C)
    far_spread = swapped(own_spread, C)

    ytail, drive, gtail = pl.pallas_call(
        start_kernel,
        in_specs=[SM, HB, HB, HB, HB],
        out_specs=[VM, VM, VM],
        out_shape=[shape(2, BND, BND), block, shape(BND, NB * 2 * BLK)],
        scratch_shapes=[
            pltpu.VMEM((2 * NB, 2, BLK, BND), F32),
            pltpu.VMEM((BND, NB * 2 * BLK), F32),
            pltpu.VMEM((BND, 2 * BND), F32),
            pltpu.VMEM((BND, BND), F32),
            pltpu.SemaphoreType.DMA((3 + 2 * NB,)),
        ],
        compiler_params=FULL,
        cost_estimate=cost(2 * 128 * 512 * 256 * 6, 1 << 21),
        name="start",
    )(patt, sources, front_inv, couple, inflow)

    ys, cols = [], []
    for step in range(STEPS):
        y0, y1, col = pl.pallas_call(
            functools.partial(bulk_kernel, step),
            grid=(1,),
            in_specs=[
                SM,
                whole(2, 1, LEAF, BND),
                pl.BlockSpec((STEP_ROWS, NB * 2 * BLK), lambda i, step=step: (step, 0)),
            ],
            out_specs=[
                whole(STEP_ROWS, BND),
                whole(STEP_ROWS, BND),
                whole(2 * STEP_ROWS, 2 * BND),
            ],
            out_shape=[
                shape(STEP_ROWS, BND),
                shape(STEP_ROWS, BND),
                jax.ShapeDtypeStruct((2 * STEP_ROWS, 2 * BND), BF16),
            ],
            compiler_params=ROOM,
            cost_estimate=cost(2 * 512 * 512 * 256 * 6, 3 << 20),
        )(patt, sources, gmat)
        ys.append((y0, y1))
        cols.append(col)

    def tail_of(beat):
        return pl.BlockSpec((1, BND, BND), lambda i, beat=beat: (beat, 0, 0))

    result = None
    for beat in range(BEATS):
        if beat:
            devices = lax.axis_size("slab")
            incoming = lax.ppermute(outgoing, "slab", [(i, i + 1) for i in range(devices - 1)])
            drive = pl.pallas_call(
                drive_kernel,
                grid=(1,),
                in_specs=[whole(BND, 2 * BND), whole(BND, BND), tail_of(beat)],
                out_specs=whole(BND, BND),
                out_shape=block,
                compiler_params=ROOM,
                cost_estimate=cost(2 * 128 * 256 * 128 * 4, 1 << 18),
            )(kmat, incoming, ytail)
        far_drive = swapped(drive, C)
        pieces = pl.pallas_call(
            lift_kernel,
            in_specs=[SM, SM, VM, VM, VM, VM],
            out_specs=[VM] * NX,
            out_shape=[double] * NX,
            scratch_shapes=[pltpu.VMEM((2 * NX, BND, BND), F32)],
            compiler_params=ROOM,
            cost_estimate=cost(2 * 512 * 256 * 128 * 4, 3 << 19),
        )(own_tree, far_tree, drive, far_drive, own_lift, far_lift)
        came3 = beside(pieces[3], 1)
        came2 = beside(pieces[2], 1)
        came1 = beside(pieces[1] + came3, 0)
        near = (pieces[0] + came2) + came1
        mine = near + swapped(near, Z)
        first = beside(mine, 0)
        second = beside(mine, 1)
        third = beside(first, 1)
        own_part, far_part = pl.pallas_call(
            sep_kernel,
            in_specs=[VM] * (NX + 2),
            out_specs=[VM] * 2,
            out_shape=[block] * 2,
            compiler_params=ROOM,
            cost_estimate=cost(2 * 256 * 2048 * 128 * 4, 5 << 20),
        )(mine, first, second, third, own_sep, far_sep)
        sol = own_part + swapped(far_part, C)
        other = swapped(sol, Z)
        held = [None] * (2 * NX)
        for j, part in enumerate((sol, other)):
            held[j] = part
            held[2 + j] = beside(part, 0)
            held[4 + j] = beside(part, 1)
            held[6 + j] = beside(held[2 + j], 1)
        own_z, far_z = pl.pallas_call(
            spread_kernel,
            in_specs=[SM, SM] + [VM] * (2 * NX + 2),
            out_specs=[VM] * 2,
            out_shape=[block] * 2,
            scratch_shapes=[pltpu.VMEM((2 * NX, BND, BND), F32)],
            compiler_params=ROOM,
            cost_estimate=cost(2 * 128 * 1024 * 128 * 4, 3 << 19),
        )(own_tree, far_tree, *held, own_spread, far_spread)
        came = swapped(far_z, C)
        if beat == 0:
            _, outgoing = pl.pallas_call(
                out_kernel,
                grid=(1,),
                in_specs=[
                    SM,
                    whole(BND, BND),
                    whole(BND, BND),
                    tail_of(0),
                    whole(BND, NB * 2 * BLK),
                ],
                out_specs=[whole(BND, BND)] * 2,
                out_shape=[block] * 2,
                compiler_params=ROOM,
                cost_estimate=cost(2 * 128 * 256 * 128 * 4, 1 << 19),
                name="outgoing",
            )(patt, own_z, came, ytail, gtail)
        earlier = () if result is None else (result,)
        result = pl.pallas_call(
            field_kernel,
            grid=(1,),
            in_specs=[whole(BND, BND), whole(BND, BND)]
            + [whole(STEP_ROWS, BND)] * STEPS
            + [whole(2 * STEP_ROWS, 2 * BND)] * STEPS
            + [pl.BlockSpec(memory_space=pl.ANY)] * len(earlier),
            out_specs=pl.BlockSpec((1, LEAF, BND), lambda i, beat=beat: (beat, 0, 0)),
            out_shape=shape(2, LEAF, BND),
            input_output_aliases={2 + 2 * STEPS: 0} if earlier else {},
            compiler_params=ROOM,
            cost_estimate=cost(2 * 1024 * 256 * 128 * 4, 3 << 20),
        )(own_z, came, *[y[beat] for y in ys], *cols, *earlier)
    return result[:, None]


def solution(mesh):
    torus = Mesh(
        mesh.devices.reshape(mesh.shape["slab"], 4, 2, 2), ("slab", "front_0", "front_1", "front_2")
    )
    in_specs = (
        P(None, "slab", FRONT, None),
        P("slab", FRONT, None),
        P("slab", FRONT, None),
        P("slab", FRONT, None),
        P("slab", FRONT, None),
        P("slab", FRONT, None),
        P("slab", FRONT, None),
        P("slab", FRONT, None),
        P("slab", FRONT, None),
    )
    out_specs = P(None, "slab", FRONT, None)
    return jax.shard_map(
        sweep, mesh=torus, in_specs=in_specs, out_specs=out_specs, check_vma=False
    )
```

profile of v0, /device:TPU:65, one launch (start us, length us, event | category | flops | bytes accessed | tf_op | source)
XLA Modules:
  0.0 144.4 jit_solution(15419009702030395993)
XLA Ops:
  0.8 3.1 %start.1 = (f32[2,128,128]{2,1,0:T(8,128)}, f32[128,128]{1,0:T(8,128)}, f32[128,512]{1,0:T(8,128)}) custom-call(s32[4,16]{1,0:T(4,128)} %bitcast.24, f32[2,1,1024,128]{3,2,1,0:T(8,128)} %src_ref.5, f32[1,1024,512]{2,1,0:T(8,128)} %g_ref.1, f32[1,128,256]{2,1,0:T(8,128)} %couple_ref.1, f32[1,128,128]{2,1,0:T(8,128)} %wave_ref.1), custom_call_target="tpu_custom_call" | custom-call | flops 201326592 | bytes 2097152 | tf_op jit(solution)/shard_map/start/pallas_call | solution.py:293
  6.5 1.7 %shard_map.91 = (f32[256,128]{1,0:T(8,128)S(1)}, f32[256,128]{1,0:T(8,128)S(1)}, f32[256,128]{1,0:T(8,128)S(1)}, f32[256,128]{1,0:T(8,128)S(1)}) custom-call(s32[4]{0:T(128)S(1)} %bitcast.29, s32[4]{0:T(128)S(1)} %collective-permute-done.far_tree, f32[128,128]{1,0:T(8,128)S(1)} %copy-done.8, f32[128,128]{1,0:T(8,128)S(1)} %collective-permute-done.1.far_ref, ...), custom_call_target="tpu_custom_call" | custom-call | flops 134217728 | bytes 1572864 | tf_op jit(solution)/shard_map/pallas_call | solution.py:354
  9.8 2.4 %collective-permute-done.4 = f32[256,128]{1,0:T(8,128)S(1)} collective-permute-done((f32[256,128]{1,0:T(8,128)S(1)}, f32[256,128]{1,0:T(8,128)S(1)}, u32[]{:S(2)}, u32[]{:S(2)}) %collective-permute-start.4) | collective-permute-done | bytes 131104 | tf_op jit(solution)/shard_map/ppermute | solution.py:279
  12.1 2.6 %collective-permute-start.5 = (f32[256,128]{1,0:T(8,128)S(1)}, f32[256,128]{1,0:T(8,128)S(1)}, u32[]{:S(2)}, u32[]{:S(2)}) collective-permute-start(f32[256,128]{1,0:T(8,128)S(1)} %add.31), channel_id=1, source_target_pairs={{0,4},{1,13},{4,0},{5,9},{8,12},{9,5},{12,8},{13,1},{2,6},{3,15},{... | collective-permute-start | bytes 393224 | tf_op jit(solution)/shard_map/ppermute | solution.py:279
  14.8 3.5 %collective-permute-done.5 = f32[256,128]{1,0:T(8,128)S(1)} collective-permute-done((f32[256,128]{1,0:T(8,128)S(1)}, f32[256,128]{1,0:T(8,128)S(1)}, u32[]{:S(2)}, u32[]{:S(2)}) %collective-permute-start.5) | collective-permute-done | bytes 131104 | tf_op jit(solution)/shard_map/ppermute | solution.py:279
  18.3 5.2 %collective-permute-start.6 = (f32[256,128]{1,0:T(8,128)S(1)}, f32[256,128]{1,0:T(8,128)S(1)}, u32[]{:S(2)}, u32[]{:S(2)}) collective-permute-start(f32[256,128]{1,0:T(8,128)S(1)} %add_add_fusion.1), channel_id=1, source_target_pairs={{0,2},{2,0},{1,3},{3,1},{4,6},{6,4},{5,7},{7,5},{8,10},{10,8},{9,1... | collective-permute-start | bytes 393224 | tf_op jit(solution)/shard_map/ppermute | solution.py:261
  23.5 6.4 %collective-permute-done.6 = f32[256,128]{1,0:T(8,128)S(1)} collective-permute-done((f32[256,128]{1,0:T(8,128)S(1)}, f32[256,128]{1,0:T(8,128)S(1)}, u32[]{:S(2)}, u32[]{:S(2)}) %collective-permute-start.6) | collective-permute-done | bytes 131104 | tf_op jit(solution)/shard_map/ppermute | solution.py:261
  33.2 1.9 %collective-permute-done.7.refs_1_ = f32[256,128]{1,0:T(8,128)S(1)} collective-permute-done((f32[256,128]{1,0:T(8,128)S(1)}, f32[256,128]{1,0:T(8,128)S(1)}, u32[]{:S(2)}, u32[]{:S(2)}) %collective-permute-start.7) | collective-permute-done | bytes 131104 | tf_op jit(solution)/shard_map/ppermute | solution.py:279
  35.1 2.1 %collective-permute-done.8.refs_2_ = f32[256,128]{1,0:T(8,128)S(1)} collective-permute-done((f32[256,128]{1,0:T(8,128)S(1)}, f32[256,128]{1,0:T(8,128)S(1)}, u32[]{:S(2)}, u32[]{:S(2)}) %collective-permute-start.8) | collective-permute-done | bytes 131104 | tf_op jit(solution)/shard_map/ppermute | solution.py:279
  38.9 2.4 %shard_map.92 = (f32[128,128]{1,0:T(8,128)S(1)}, f32[128,128]{1,0:T(8,128)S(1)}) custom-call(f32[256,128]{1,0:T(8,128)S(1)} %add.33.refs_0_, f32[256,128]{1,0:T(8,128)S(1)} %collective-permute-done.7.refs_1_, f32[256,128]{1,0:T(8,128)S(1)} %collective-permute-done.8.refs_2_, f32[256,128]{1,0:T(8,128)S(1)} %collective-permute-done.9.refs_3_, ...), custom_call_target="tpu_custom_call" | custom-call | flops 536870912 | bytes 5242880 | tf_op jit(solution)/shard_map/pallas_call | solution.py:371
  41.3 5.0 %collective-permute-start.11 = (f32[128,128]{1,0:T(8,128)S(1)}, f32[128,128]{1,0:T(8,128)S(1)}, u32[]{:S(2)}, u32[]{:S(2)}) collective-permute-start(f32[128,128]{1,0:T(8,128)S(1)} %get-tuple-element.37), channel_id=1, source_target_pairs={{0,1},{1,0},{2,3},{3,2},{4,5},{5,4},{6,7},{7,6},{8,9},{9,8},{10,11... | collective-permute-start | bytes 196616 | tf_op jit(solution)/shard_map/ppermute | solution.py:261
  47.2 5.0 %collective-permute-start.12 = (f32[128,128]{1,0:T(8,128)S(1)}, f32[128,128]{1,0:T(8,128)S(1)}, u32[]{:S(2)}, u32[]{:S(2)}) collective-permute-start(f32[128,128]{1,0:T(8,128)S(1)} %add.34.refs_0_), channel_id=1, source_target_pairs={{0,2},{2,0},{1,3},{3,1},{4,6},{6,4},{5,7},{7,5},{8,10},{10,8},{9,1... | collective-permute-start | bytes 196616 | tf_op jit(solution)/shard_map/ppermute | solution.py:261
  53.7 2.9 %collective-permute-done.12.refs_1_ = f32[128,128]{1,0:T(8,128)S(1)} collective-permute-done((f32[128,128]{1,0:T(8,128)S(1)}, f32[128,128]{1,0:T(8,128)S(1)}, u32[]{:S(2)}, u32[]{:S(2)}) %collective-permute-start.12) | collective-permute-done | bytes 65568 | tf_op jit(solution)/shard_map/ppermute | solution.py:261
  56.5 1.8 %collective-permute-start.14 = (f32[128,128]{1,0:T(8,128)S(1)}, f32[128,128]{1,0:T(8,128)S(1)}, u32[]{:S(2)}, u32[]{:S(2)}) collective-permute-start(f32[128,128]{1,0:T(8,128)S(1)} %collective-permute-done.12.refs_1_), channel_id=1, source_target_pairs={{0,4},{1,13},{4,0},{5,9},{8,12},{9,5},{12,8},{13,1},{2,6},{3,15},{... | collective-permute-start | bytes 196616 | tf_op jit(solution)/shard_map/ppermute | solution.py:279
  65.4 3.8 %collective-permute-start.20 = (f32[128,128]{1,0:T(8,128)S(1)}, f32[128,128]{1,0:T(8,128)S(1)}, u32[]{:S(2)}, u32[]{:S(2)}) collective-permute-start(f32[128,128]{1,0:T(8,128)S(1)} %get-tuple-element.39), channel_id=1, source_target_pairs={{0,1},{1,0},{2,3},{3,2},{4,5},{5,4},{6,7},{7,6},{8,9},{9,8},{10,11... | collective-permute-start | bytes 196616 | tf_op jit(solution)/shard_map/ppermute | solution.py:261
  71.4 3.2 %collective-permute-start.21 = (f32[128,128]{1,0:T(8,128)S(1)}, f32[128,128]{1,0:T(8,128)S(1)}, u32[]{:S(2)}, u32[]{:S(2)}) collective-permute-start(f32[128,128]{1,0:T(8,128)S(1)} %get-tuple-element.42), channel_id=1, source_target_pairs={{0,16},{16,32},{32,48},{48,64},{64,80},{80,96},{96,112},{112,128},... | collective-permute-start | bytes 196616 | tf_op jit(solution)/shard_map/ppermute | solution.py:343
  74.6 3.9 %collective-permute-done.21.wave_ref = f32[128,128]{1,0:T(8,128)S(1)} collective-permute-done((f32[128,128]{1,0:T(8,128)S(1)}, f32[128,128]{1,0:T(8,128)S(1)}, u32[]{:S(2)}, u32[]{:S(2)}) %collective-permute-start.21) | collective-permute-done | bytes 65568 | tf_op jit(solution)/shard_map/ppermute | solution.py:343
  81.2 1.7 %shard_map.95 = (f32[256,128]{1,0:T(8,128)S(1)}, f32[256,128]{1,0:T(8,128)S(1)}, f32[256,128]{1,0:T(8,128)S(1)}, f32[256,128]{1,0:T(8,128)S(1)}) custom-call(s32[4]{0:T(128)S(1)} %bitcast.31, s32[4]{0:T(128)S(1)} %collective-permute-done.far_tree, f32[128,128]{1,0:T(8,128)S(1)} %shard_map.94.own_ref, f32[128,128]{1,0:T(8,128)S(1)} %collective-permute-done.22.far_ref, ...), custom_call_target="tpu_custom_call" | custom-call | flops 134217728 | bytes 1572864 | tf_op jit(solution)/shard_map/pallas_call | solution.py:354
  84.5 2.4 %collective-permute-done.24 = f32[256,128]{1,0:T(8,128)S(1)} collective-permute-done((f32[256,128]{1,0:T(8,128)S(1)}, f32[256,128]{1,0:T(8,128)S(1)}, u32[]{:S(2)}, u32[]{:S(2)}) %collective-permute-start.24) | collective-permute-done | bytes 131104 | tf_op jit(solution)/shard_map/ppermute | solution.py:279
  88.6 3.5 %collective-permute-done.25 = f32[256,128]{1,0:T(8,128)S(1)} collective-permute-done((f32[256,128]{1,0:T(8,128)S(1)}, f32[256,128]{1,0:T(8,128)S(1)}, u32[]{:S(2)}, u32[]{:S(2)}) %collective-permute-start.25) | collective-permute-done | bytes 131104 | tf_op jit(solution)/shard_map/ppermute | solution.py:279
  92.1 4.6 %collective-permute-start.26 = (f32[256,128]{1,0:T(8,128)S(1)}, f32[256,128]{1,0:T(8,128)S(1)}, u32[]{:S(2)}, u32[]{:S(2)}) collective-permute-start(f32[256,128]{1,0:T(8,128)S(1)} %add_add_fusion), channel_id=1, source_target_pairs={{0,2},{2,0},{1,3},{3,1},{4,6},{6,4},{5,7},{7,5},{8,10},{10,8},{9,1... | collective-permute-start | bytes 393224 | tf_op jit(solution)/shard_map/ppermute | solution.py:261
  96.7 4.6 %collective-permute-done.26 = f32[256,128]{1,0:T(8,128)S(1)} collective-permute-done((f32[256,128]{1,0:T(8,128)S(1)}, f32[256,128]{1,0:T(8,128)S(1)}, u32[]{:S(2)}, u32[]{:S(2)}) %collective-permute-start.26) | collective-permute-done | bytes 131104 | tf_op jit(solution)/shard_map/ppermute | solution.py:261
  102.4 4.0 %collective-permute-done.27.refs_1_ = f32[256,128]{1,0:T(8,128)S(1)} collective-permute-done((f32[256,128]{1,0:T(8,128)S(1)}, f32[256,128]{1,0:T(8,128)S(1)}, u32[]{:S(2)}, u32[]{:S(2)}) %collective-permute-start.27) | collective-permute-done | bytes 131104 | tf_op jit(solution)/shard_map/ppermute | solution.py:279
  106.4 3.8 %collective-permute-done.29.refs_3_ = f32[256,128]{1,0:T(8,128)S(1)} collective-permute-done((f32[256,128]{1,0:T(8,128)S(1)}, f32[256,128]{1,0:T(8,128)S(1)}, u32[]{:S(2)}, u32[]{:S(2)}) %collective-permute-start.29) | collective-permute-done | bytes 131104 | tf_op jit(solution)/shard_map/ppermute | solution.py:279
  110.2 2.4 %shard_map.96 = (f32[128,128]{1,0:T(8,128)S(1)}, f32[128,128]{1,0:T(8,128)S(1)}) custom-call(f32[256,128]{1,0:T(8,128)S(1)} %add.38.refs_0_, f32[256,128]{1,0:T(8,128)S(1)} %collective-permute-done.27.refs_1_, f32[256,128]{1,0:T(8,128)S(1)} %collective-permute-done.28.refs_2_, f32[256,128]{1,0:T(8,128)S(1)} %collective-permute-done.29.refs_3_, ...), custom_call_target="tpu_custom_call" | custom-call | flops 536870912 | bytes 5242880 | tf_op jit(solution)/shard_map/pallas_call | solution.py:371
  112.6 4.9 %collective-permute-start.30 = (f32[128,128]{1,0:T(8,128)S(1)}, f32[128,128]{1,0:T(8,128)S(1)}, u32[]{:S(2)}, u32[]{:S(2)}) collective-permute-start(f32[128,128]{1,0:T(8,128)S(1)} %get-tuple-element.48), channel_id=1, source_target_pairs={{0,1},{1,0},{2,3},{3,2},{4,5},{5,4},{6,7},{7,6},{8,9},{9,8},{10,11... | collective-permute-start | bytes 196616 | tf_op jit(solution)/shard_map/ppermute | solution.py:261
  118.4 4.9 %collective-permute-start.31 = (f32[128,128]{1,0:T(8,128)S(1)}, f32[128,128]{1,0:T(8,128)S(1)}, u32[]{:S(2)}, u32[]{:S(2)}) collective-permute-start(f32[128,128]{1,0:T(8,128)S(1)} %add.39.refs_0_), channel_id=1, source_target_pairs={{0,2},{2,0},{1,3},{3,1},{4,6},{6,4},{5,7},{7,5},{8,10},{10,8},{9,1... | collective-permute-start | bytes 196616 | tf_op jit(solution)/shard_map/ppermute | solution.py:261
  124.5 2.5 %collective-permute-done.31.refs_1_ = f32[128,128]{1,0:T(8,128)S(1)} collective-permute-done((f32[128,128]{1,0:T(8,128)S(1)}, f32[128,128]{1,0:T(8,128)S(1)}, u32[]{:S(2)}, u32[]{:S(2)}) %collective-permute-start.31) | collective-permute-done | bytes 65568 | tf_op jit(solution)/shard_map/ppermute | solution.py:261
  129.4 1.9 %collective-permute-done.33.refs_3_ = f32[128,128]{1,0:T(8,128)S(1)} collective-permute-done((f32[128,128]{1,0:T(8,128)S(1)}, f32[128,128]{1,0:T(8,128)S(1)}, u32[]{:S(2)}, u32[]{:S(2)}) %collective-permute-start.33) | collective-permute-done | bytes 65568 | tf_op jit(solution)/shard_map/ppermute | solution.py:279
  131.3 2.4 %shard_map.98 = (f32[512,128]{1,0:T(8,128)S(1)}, f32[512,128]{1,0:T(8,128)S(1)}, bf16[1024,256]{1,0:T(8,128)(2,1)S(1)}) custom-call(s32[4,16]{1,0:T(4,128)S(1)} %bitcast.26, f32[2,1,1024,128]{3,2,1,0:T(8,128)S(1)} %copy-done.1, f32[1024,512]{1,0:T(8,128)S(1)} %bitcast.12), custom_call_target="tpu_custom_call" | custom-call | flops 805306368 | bytes 3145728 | tf_op jit(solution)/shard_map/pallas_call | solution.py:312
  135.5 3.8 %collective-permute-start.38 = (f32[128,128]{1,0:T(8,128)S(1)}, f32[128,128]{1,0:T(8,128)S(1)}, u32[]{:S(2)}, u32[]{:S(2)}) collective-permute-start(f32[128,128]{1,0:T(8,128)S(1)} %get-tuple-element.50), channel_id=1, source_target_pairs={{0,1},{1,0},{2,3},{3,2},{4,5},{5,4},{6,7},{7,6},{8,9},{9,8},{10,11... | collective-permute-start | bytes 196616 | tf_op jit(solution)/shard_map/ppermute | solution.py:261
  139.3 2.4 %shard_map.99 = (f32[512,128]{1,0:T(8,128)S(1)}, f32[512,128]{1,0:T(8,128)S(1)}, bf16[1024,256]{1,0:T(8,128)(2,1)S(1)}) custom-call(s32[4,16]{1,0:T(4,128)S(1)} %bitcast.27, f32[2,1,1024,128]{3,2,1,0:T(8,128)S(1)} %copy-done.1, f32[1024,512]{1,0:T(8,128)S(1)} %bitcast.13), custom_call_target="tpu_custom_call" | custom-call | flops 805306368 | bytes 3145728 | tf_op jit(solution)/shard_map/pallas_call | solution.py:312
  (89 shorter events, 37.4 us)
Async XLA Ops:
  0.0 38.9 %collective-permute-start.10 = (f32[128,4096]{1,0:T(8,128)}, f32[128,4096]{1,0:T(8,128)}, u32[]{:S(2)}, u32[]{:S(2)}) collective-permute-start(f32[128,4096]{1,0:T(8,128)} %bitcast.14), channel_id=1, source_target_pairs={{0,1},{1,0},{2,3},{3,2},{4,5},{5,4},{6,7},{7,6},{8,9},{9,8},{10,11... | collective-permute-start | bytes 6291464 | tf_op jit(solution)/shard_map/ppermute | solution.py:261
  0.7 4.9 %collective-permute-start.2 = (f32[512,256]{1,0:T(8,128)}, f32[512,256]{1,0:T(8,128)}, u32[]{:S(2)}, u32[]{:S(2)}) collective-permute-start(f32[512,256]{1,0:T(8,128)} %bitcast.17), channel_id=1, source_target_pairs={{0,1},{1,0},{2,3},{3,2},{4,5},{5,4},{6,7},{7,6},{8,9},{9,8},{10,11... | collective-permute-start | bytes 1572872 | tf_op jit(solution)/shard_map/ppermute | solution.py:261
  8.2 3.9 %collective-permute-start.4 = (f32[256,128]{1,0:T(8,128)S(1)}, f32[256,128]{1,0:T(8,128)S(1)}, u32[]{:S(2)}, u32[]{:S(2)}) collective-permute-start(f32[256,128]{1,0:T(8,128)S(1)} %get-tuple-element.35), channel_id=1, source_target_pairs={{0,12},{1,5},{4,8},{5,1},{8,4},{9,13},{12,0},{13,9},{2,14},{3,7},{... | collective-permute-start | bytes 393224 | tf_op jit(solution)/shard_map/ppermute | solution.py:279
  9.6 5.2 %collective-permute-start.3 = (f32[256,128]{1,0:T(8,128)S(1)}, f32[256,128]{1,0:T(8,128)S(1)}, u32[]{:S(2)}, u32[]{:S(2)}) collective-permute-start(f32[256,128]{1,0:T(8,128)S(1)} %get-tuple-element.33), channel_id=1, source_target_pairs={{0,12},{1,5},{4,8},{5,1},{8,4},{9,13},{12,0},{13,9},{2,14},{3,7},{... | collective-permute-start | bytes 393224 | tf_op jit(solution)/shard_map/ppermute | solution.py:279
  12.1 6.2 %collective-permute-start.5 = (f32[256,128]{1,0:T(8,128)S(1)}, f32[256,128]{1,0:T(8,128)S(1)}, u32[]{:S(2)}, u32[]{:S(2)}) collective-permute-start(f32[256,128]{1,0:T(8,128)S(1)} %add.31), channel_id=1, source_target_pairs={{0,4},{1,13},{4,0},{5,9},{8,12},{9,5},{12,8},{13,1},{2,6},{3,15},{... | collective-permute-start | bytes 393224 | tf_op jit(solution)/shard_map/ppermute | solution.py:279
  18.3 11.6 %collective-permute-start.6 = (f32[256,128]{1,0:T(8,128)S(1)}, f32[256,128]{1,0:T(8,128)S(1)}, u32[]{:S(2)}, u32[]{:S(2)}) collective-permute-start(f32[256,128]{1,0:T(8,128)S(1)} %add_add_fusion.1), channel_id=1, source_target_pairs={{0,2},{2,0},{1,3},{3,1},{4,6},{6,4},{5,7},{7,5},{8,10},{10,8},{9,1... | collective-permute-start | bytes 393224 | tf_op jit(solution)/shard_map/ppermute | solution.py:261
  29.9 5.1 %collective-permute-start.7 = (f32[256,128]{1,0:T(8,128)S(1)}, f32[256,128]{1,0:T(8,128)S(1)}, u32[]{:S(2)}, u32[]{:S(2)}) collective-permute-start(f32[256,128]{1,0:T(8,128)S(1)} %add.33.refs_0_), channel_id=1, source_target_pairs={{0,4},{1,13},{4,0},{5,9},{8,12},{9,5},{12,8},{13,1},{2,6},{3,15},{... | collective-permute-start | bytes 393224 | tf_op jit(solution)/shard_map/ppermute | solution.py:279
  30.1 31.2 %collective-permute-start.19 = (f32[128,1024]{1,0:T(8,128)}, f32[128,1024]{1,0:T(8,128)S(1)}, u32[]{:S(2)}, u32[]{:S(2)}) collective-permute-start(f32[128,1024]{1,0:T(8,128)} %bitcast.20), channel_id=1, source_target_pairs={{0,1},{1,0},{2,3},{3,2},{4,5},{5,4},{6,7},{7,6},{8,9},{9,8},{10,11... | collective-permute-start | bytes 1572872 | tf_op jit(solution)/shard_map/ppermute | solution.py:261
  31.5 5.7 %collective-permute-start.8 = (f32[256,128]{1,0:T(8,128)S(1)}, f32[256,128]{1,0:T(8,128)S(1)}, u32[]{:S(2)}, u32[]{:S(2)}) collective-permute-start(f32[256,128]{1,0:T(8,128)S(1)} %add.33.refs_0_), channel_id=1, source_target_pairs={{0,12},{1,5},{4,8},{5,1},{8,4},{9,13},{12,0},{13,9},{2,14},{3,7},{... | collective-permute-start | bytes 393224 | tf_op jit(solution)/shard_map/ppermute | solution.py:279
  35.1 3.8 %collective-permute-start.9 = (f32[256,128]{1,0:T(8,128)S(1)}, f32[256,128]{1,0:T(8,128)S(1)}, u32[]{:S(2)}, u32[]{:S(2)}) collective-permute-start(f32[256,128]{1,0:T(8,128)S(1)} %collective-permute-done.7.refs_1_), channel_id=1, source_target_pairs={{0,12},{1,5},{4,8},{5,1},{8,4},{9,13},{12,0},{13,9},{2,14},{3,7},{... | collective-permute-start | bytes 393224 | tf_op jit(solution)/shard_map/ppermute | solution.py:279
  41.3 5.9 %collective-permute-start.11 = (f32[128,128]{1,0:T(8,128)S(1)}, f32[128,128]{1,0:T(8,128)S(1)}, u32[]{:S(2)}, u32[]{:S(2)}) collective-permute-start(f32[128,128]{1,0:T(8,128)S(1)} %get-tuple-element.37), channel_id=1, source_target_pairs={{0,1},{1,0},{2,3},{3,2},{4,5},{5,4},{6,7},{7,6},{8,9},{9,8},{10,11... | collective-permute-start | bytes 196616 | tf_op jit(solution)/shard_map/ppermute | solution.py:261
  47.2 9.3 %collective-permute-start.12 = (f32[128,128]{1,0:T(8,128)S(1)}, f32[128,128]{1,0:T(8,128)S(1)}, u32[]{:S(2)}, u32[]{:S(2)}) collective-permute-start(f32[128,128]{1,0:T(8,128)S(1)} %add.34.refs_0_), channel_id=1, source_target_pairs={{0,2},{2,0},{1,3},{3,1},{4,6},{6,4},{5,7},{7,5},{8,10},{10,8},{9,1... | collective-permute-start | bytes 196616 | tf_op jit(solution)/shard_map/ppermute | solution.py:261
  52.2 7.5 %collective-permute-start.13 = (f32[128,128]{1,0:T(8,128)S(1)}, f32[128,128]{1,0:T(8,128)S(1)}, u32[]{:S(2)}, u32[]{:S(2)}) collective-permute-start(f32[128,128]{1,0:T(8,128)S(1)} %add.34.refs_0_), channel_id=1, source_target_pairs={{0,4},{1,13},{4,0},{5,9},{8,12},{9,5},{12,8},{13,1},{2,6},{3,15},{... | collective-permute-start | bytes 196616 | tf_op jit(solution)/shard_map/ppermute | solution.py:279
  56.5 4.3 %collective-permute-start.14 = (f32[128,128]{1,0:T(8,128)S(1)}, f32[128,128]{1,0:T(8,128)S(1)}, u32[]{:S(2)}, u32[]{:S(2)}) collective-permute-start(f32[128,128]{1,0:T(8,128)S(1)} %collective-permute-done.12.refs_1_), channel_id=1, source_target_pairs={{0,4},{1,13},{4,0},{5,9},{8,12},{9,5},{12,8},{13,1},{2,6},{3,15},{... | collective-permute-start | bytes 196616 | tf_op jit(solution)/shard_map/ppermute | solution.py:279
  58.3 3.9 %collective-permute-start.16 = (f32[128,128]{1,0:T(8,128)S(1)}, f32[128,128]{1,0:T(8,128)S(1)}, u32[]{:S(2)}, u32[]{:S(2)}) collective-permute-start(f32[128,128]{1,0:T(8,128)S(1)} %collective-permute-done.12.refs_1_), channel_id=1, source_target_pairs={{0,12},{1,5},{4,8},{5,1},{8,4},{9,13},{12,0},{13,9},{2,14},{3,7},{... | collective-permute-start | bytes 196616 | tf_op jit(solution)/shard_map/ppermute | solution.py:279
  65.4 4.7 %collective-permute-start.20 = (f32[128,128]{1,0:T(8,128)S(1)}, f32[128,128]{1,0:T(8,128)S(1)}, u32[]{:S(2)}, u32[]{:S(2)}) collective-permute-start(f32[128,128]{1,0:T(8,128)S(1)} %get-tuple-element.39), channel_id=1, source_target_pairs={{0,1},{1,0},{2,3},{3,2},{4,5},{5,4},{6,7},{7,6},{8,9},{9,8},{10,11... | collective-permute-start | bytes 196616 | tf_op jit(solution)/shard_map/ppermute | solution.py:261
  71.4 7.1 %collective-permute-start.21 = (f32[128,128]{1,0:T(8,128)S(1)}, f32[128,128]{1,0:T(8,128)S(1)}, u32[]{:S(2)}, u32[]{:S(2)}) collective-permute-start(f32[128,128]{1,0:T(8,128)S(1)} %get-tuple-element.42), channel_id=1, source_target_pairs={{0,16},{16,32},{32,48},{48,64},{64,80},{80,96},{96,112},{112,128},... | collective-permute-start | bytes 196616 | tf_op jit(solution)/shard_map/ppermute | solution.py:343
  83.0 3.9 %collective-permute-start.24 = (f32[256,128]{1,0:T(8,128)S(1)}, f32[256,128]{1,0:T(8,128)S(1)}, u32[]{:S(2)}, u32[]{:S(2)}) collective-permute-start(f32[256,128]{1,0:T(8,128)S(1)} %get-tuple-element.46), channel_id=1, source_target_pairs={{0,12},{1,5},{4,8},{5,1},{8,4},{9,13},{12,0},{13,9},{2,14},{3,7},{... | collective-permute-start | bytes 393224 | tf_op jit(solution)/shard_map/ppermute | solution.py:279
  83.1 5.5 %collective-permute-start.23 = (f32[256,128]{1,0:T(8,128)S(1)}, f32[256,128]{1,0:T(8,128)S(1)}, u32[]{:S(2)}, u32[]{:S(2)}) collective-permute-start(f32[256,128]{1,0:T(8,128)S(1)} %get-tuple-element.44), channel_id=1, source_target_pairs={{0,12},{1,5},{4,8},{5,1},{8,4},{9,13},{12,0},{13,9},{2,14},{3,7},{... | collective-permute-start | bytes 393224 | tf_op jit(solution)/shard_map/ppermute | solution.py:279
  86.9 5.1 %collective-permute-start.25 = (f32[256,128]{1,0:T(8,128)S(1)}, f32[256,128]{1,0:T(8,128)S(1)}, u32[]{:S(2)}, u32[]{:S(2)}) collective-permute-start(f32[256,128]{1,0:T(8,128)S(1)} %add.36), channel_id=1, source_target_pairs={{0,4},{1,13},{4,0},{5,9},{8,12},{9,5},{12,8},{13,1},{2,6},{3,15},{... | collective-permute-start | bytes 393224 | tf_op jit(solution)/shard_map/ppermute | solution.py:279
  92.1 9.1 %collective-permute-start.26 = (f32[256,128]{1,0:T(8,128)S(1)}, f32[256,128]{1,0:T(8,128)S(1)}, u32[]{:S(2)}, u32[]{:S(2)}) collective-permute-start(f32[256,128]{1,0:T(8,128)S(1)} %add_add_fusion), channel_id=1, source_target_pairs={{0,2},{2,0},{1,3},{3,1},{4,6},{6,4},{5,7},{7,5},{8,10},{10,8},{9,1... | collective-permute-start | bytes 393224 | tf_op jit(solution)/shard_map/ppermute | solution.py:261
  101.3 5.1 %collective-permute-start.27 = (f32[256,128]{1,0:T(8,128)S(1)}, f32[256,128]{1,0:T(8,128)S(1)}, u32[]{:S(2)}, u32[]{:S(2)}) collective-permute-start(f32[256,128]{1,0:T(8,128)S(1)} %add.38.refs_0_), channel_id=1, source_target_pairs={{0,4},{1,13},{4,0},{5,9},{8,12},{9,5},{12,8},{13,1},{2,6},{3,15},{... | collective-permute-start | bytes 393224 | tf_op jit(solution)/shard_map/ppermute | solution.py:279
  102.4 4.0 %collective-permute-start.28 = (f32[256,128]{1,0:T(8,128)S(1)}, f32[256,128]{1,0:T(8,128)S(1)}, u32[]{:S(2)}, u32[]{:S(2)}) collective-permute-start(f32[256,128]{1,0:T(8,128)S(1)} %add.38.refs_0_), channel_id=1, source_target_pairs={{0,12},{1,5},{4,8},{5,1},{8,4},{9,13},{12,0},{13,9},{2,14},{3,7},{... | collective-permute-start | bytes 393224 | tf_op jit(solution)/shard_map/ppermute | solution.py:279
  106.4 3.8 %collective-permute-start.29 = (f32[256,128]{1,0:T(8,128)S(1)}, f32[256,128]{1,0:T(8,128)S(1)}, u32[]{:S(2)}, u32[]{:S(2)}) collective-permute-start(f32[256,128]{1,0:T(8,128)S(1)} %collective-permute-done.27.refs_1_), channel_id=1, source_target_pairs={{0,12},{1,5},{4,8},{5,1},{8,4},{9,13},{12,0},{13,9},{2,14},{3,7},{... | collective-permute-start | bytes 393224 | tf_op jit(solution)/shard_map/ppermute | solution.py:279
  112.6 5.8 %collective-permute-start.30 = (f32[128,128]{1,0:T(8,128)S(1)}, f32[128,128]{1,0:T(8,128)S(1)}, u32[]{:S(2)}, u32[]{:S(2)}) collective-permute-start(f32[128,128]{1,0:T(8,128)S(1)} %get-tuple-element.48), channel_id=1, source_target_pairs={{0,1},{1,0},{2,3},{3,2},{4,5},{5,4},{6,7},{7,6},{8,9},{9,8},{10,11... | collective-permute-start | bytes 196616 | tf_op jit(solution)/shard_map/ppermute | solution.py:261
  118.4 8.5 %collective-permute-start.31 = (f32[128,128]{1,0:T(8,128)S(1)}, f32[128,128]{1,0:T(8,128)S(1)}, u32[]{:S(2)}, u32[]{:S(2)}) collective-permute-start(f32[128,128]{1,0:T(8,128)S(1)} %add.39.refs_0_), channel_id=1, source_target_pairs={{0,2},{2,0},{1,3},{3,1},{4,6},{6,4},{5,7},{7,5},{8,10},{10,8},{9,1... | collective-permute-start | bytes 196616 | tf_op jit(solution)/shard_map/ppermute | solution.py:261
  123.4 6.0 %collective-permute-start.32 = (f32[128,128]{1,0:T(8,128)S(1)}, f32[128,128]{1,0:T(8,128)S(1)}, u32[]{:S(2)}, u32[]{:S(2)}) collective-permute-start(f32[128,128]{1,0:T(8,128)S(1)} %add.39.refs_0_), channel_id=1, source_target_pairs={{0,4},{1,13},{4,0},{5,9},{8,12},{9,5},{12,8},{13,1},{2,6},{3,15},{... | collective-permute-start | bytes 196616 | tf_op jit(solution)/shard_map/ppermute | solution.py:279
  126.9 4.3 %collective-permute-start.33 = (f32[128,128]{1,0:T(8,128)S(1)}, f32[128,128]{1,0:T(8,128)S(1)}, u32[]{:S(2)}, u32[]{:S(2)}) collective-permute-start(f32[128,128]{1,0:T(8,128)S(1)} %collective-permute-done.31.refs_1_), channel_id=1, source_target_pairs={{0,4},{1,13},{4,0},{5,9},{8,12},{9,5},{12,8},{13,1},{2,6},{3,15},{... | collective-permute-start | bytes 196616 | tf_op jit(solution)/shard_map/ppermute | solution.py:279
  127.9 5.8 %collective-permute-start.34 = (f32[128,128]{1,0:T(8,128)S(1)}, f32[128,128]{1,0:T(8,128)S(1)}, u32[]{:S(2)}, u32[]{:S(2)}) collective-permute-start(f32[128,128]{1,0:T(8,128)S(1)} %add.39.refs_0_), channel_id=1, source_target_pairs={{0,12},{1,5},{4,8},{5,1},{8,4},{9,13},{12,0},{13,9},{2,14},{3,7},{... | collective-permute-start | bytes 196616 | tf_op jit(solution)/shard_map/ppermute | solution.py:279
  127.9 5.8 %collective-permute-start.35 = (f32[128,128]{1,0:T(8,128)S(1)}, f32[128,128]{1,0:T(8,128)S(1)}, u32[]{:S(2)}, u32[]{:S(2)}) collective-permute-start(f32[128,128]{1,0:T(8,128)S(1)} %collective-permute-done.31.refs_1_), channel_id=1, source_target_pairs={{0,12},{1,5},{4,8},{5,1},{8,4},{9,13},{12,0},{13,9},{2,14},{3,7},{... | collective-permute-start | bytes 196616 | tf_op jit(solution)/shard_map/ppermute | solution.py:279
  129.3 4.4 %collective-permute-start.36 = (f32[128,128]{1,0:T(8,128)S(1)}, f32[128,128]{1,0:T(8,128)S(1)}, u32[]{:S(2)}, u32[]{:S(2)}) collective-permute-start(f32[128,128]{1,0:T(8,128)S(1)} %collective-permute-done.32.refs_2_), channel_id=1, source_target_pairs={{0,12},{1,5},{4,8},{5,1},{8,4},{9,13},{12,0},{13,9},{2,14},{3,7},{... | collective-permute-start | bytes 196616 | tf_op jit(solution)/shard_map/ppermute | solution.py:279
  135.5 7.5 %collective-permute-start.38 = (f32[128,128]{1,0:T(8,128)S(1)}, f32[128,128]{1,0:T(8,128)S(1)}, u32[]{:S(2)}, u32[]{:S(2)}) collective-permute-start(f32[128,128]{1,0:T(8,128)S(1)} %get-tuple-element.50), channel_id=1, source_target_pairs={{0,1},{1,0},{2,3},{3,2},{4,5},{5,4},{6,7},{7,6},{8,9},{9,8},{10,11... | collective-permute-start | bytes 196616 | tf_op jit(solution)/shard_map/ppermute | solution.py:261
  (18 other events, 315.9 us)
where the time goes:
time: 146 us; the launch traced here: 144 us
  starting transfers between devices  63.7 us (44%)
  waiting for transfers between devices  56.7 us (39%)
  Pallas kernels  22.7 us (16%)
    ppermute x14, starting transfers between devices, shifted(): lax.ppermute(value, axis, [(i, (i + distance) % size) for i in range(size)])  41.6 us
    ppermute x24, waiting for transfers between devices, beside(): return lax.ppermute(value, (X, C), route)  31.9 us
    ppermute x14, waiting for transfers between devices, shifted(): lax.ppermute(value, axis, [(i, (i + distance) % size) for i in range(size)])  20.9 us
    ppermute x24, starting transfers between devices, beside(): return lax.ppermute(value, (X, C), route)  18.9 us
    pallas_call x2, Pallas kernels, sweep(): pl.pallas_call(functools.partial(bulk_kernel, step), grid=(1,), in_specs=...  4.88 us
    pallas_call x2, Pallas kernels, sweep(): pl.pallas_call(sep_kernel, in_specs=[VM] * (NX + 2), out_specs=[VM] * 2,...  4.79 us
    ppermute x1, waiting for transfers between devices, sweep(): lax.ppermute(outgoing, 'slab', [(i, i + 1) for i in range(devices - 1)])  3.91 us
    pallas_call x2, Pallas kernels, sweep(): pl.pallas_call(lift_kernel, in_specs=[SM, SM, VM, VM, VM, VM], out_specs=...  3.49 us
  transfers between devices with their start and end apart: 39, of which 27 were waited for; matrix products, arithmetic and copies ran while one was open for 0% of the time, Pallas kernels for 9%

commit v1 on v0

v1 whole, which is shorter than its diff:
```python
import functools

import jax
import jax.numpy as jnp
from jax import lax
from jax.experimental import pallas as pl
from jax.experimental.pallas import tpu as pltpu
from jax.sharding import Mesh
from jax.sharding import PartitionSpec as P

BEATS = 2
LEAF = 1024
SEP = 2048
BLK = 64
NB = 4
BND = 128
P_SIZE = 4
BROWS = LEAF // BLK
FRONT = ("front_0", "front_1", "front_2")
X, Z, C = FRONT
NX = 4
HALF = SEP // 2
QUARTER = HALF // NX
F32 = jnp.float32
BF16 = jnp.bfloat16


def twist(field):
    half = field.shape[-1] // 2
    lane = lax.broadcasted_iota(jnp.int32, field.shape, len(field.shape) - 1)
    turned = pltpu.roll(field, half, len(field.shape) - 1)
    return jnp.where(lane < half, -turned, turned)


def split(a):
    high = a.astype(BF16)
    low = (a - high.astype(F32)).astype(BF16)
    return high, low


def mm(a, b):
    return jnp.dot(a, b, preferred_element_type=F32)


def rows_split(a):
    return jnp.concatenate(split(a), axis=0)


def cols_split(b):
    return jnp.concatenate(split(b), axis=1)


def product(stacked, paired):
    rows, cols = stacked.shape[0] // 2, paired.shape[1] // 2
    full = mm(stacked, paired)
    return full[:rows, :cols] + (full[:rows, cols:] + full[rows:, :cols])


def packed(matrix, field):
    both = jnp.concatenate([field, twist(field)], axis=0)
    return product(rows_split(matrix), cols_split(both))


QUAD = 32


def is_first(field):
    lane = lax.broadcasted_iota(jnp.int32, field.shape, 1)
    return (lane // QUAD) % 2 == 0


def to_second(field):
    return pltpu.roll(field, QUAD, 1)


def to_first(field):
    return pltpu.roll(field, field.shape[1] - QUAD, 1)


def pair_of(first, second):
    return jnp.where(is_first(first), first, to_second(second))


def half_of(field, c):
    return jnp.where(c == 0, field, to_first(field))


def wide(field):
    high = field.astype(BF16).astype(F32)
    return pair_of(high, field - high).astype(BF16)


def narrow(full):
    rows = full.shape[0] // 2
    total = full[:rows] + full[rows:]
    return total + jnp.where(is_first(total), to_first(total), to_second(total))


def applied(matrix, field):
    both = jnp.concatenate([field, twist(field)], axis=0)
    return narrow(mm(rows_split(matrix), wide(both)))


def front_rows(g, field):
    gh, gl = split(g)
    fh, fl = split(field)
    rows = g.shape[0]
    first = mm(jnp.concatenate([gh, gl], axis=0), fh)
    return first[:rows] + (first[rows:] + mm(gh, fl))


def gathered(patt_ref, row, take):
    both = []
    for k in range(NB):
        a, b = take(patt_ref[k, row])
        both.append(jnp.concatenate([a, b], axis=1))
        both.append(jnp.concatenate([twist(a), twist(b)], axis=1))
    return jnp.concatenate(both, axis=0)


def tail_columns(g, patt_ref, row):
    parts = []
    for block in (BROWS - 2, BROWS - 1):
        total = jnp.zeros((BLK, 2 * BLK), F32)
        for k in range(NB):
            held = (patt_ref[k, row] == block).astype(F32)
            total = total + held * g[:, k * 2 * BLK : (k + 1) * 2 * BLK]
        parts.append(total)
    return jnp.concatenate(parts, axis=1)


def tail_field(z):
    tz = twist(z)
    return jnp.concatenate([z[:BLK], tz[:BLK], z[BLK:], tz[BLK:]], axis=0)


def start_kernel(
    patt_ref, src_ref, g_ref, couple_ref, wave_ref, keep_ref, send_ref, cols_ref, blocks, held, couple, wave, sems
):
    copies = [
        pltpu.make_async_copy(g_ref.at[0, pl.ds(LEAF - BND, BND), :], held, sems.at[0]),
        pltpu.make_async_copy(couple_ref.at[0], couple, sems.at[1]),
        pltpu.make_async_copy(wave_ref.at[0], wave, sems.at[2]),
    ]
    for i in range(2):
        for k in range(NB):
            at = pl.ds(pl.multiple_of(patt_ref[k, BROWS - 2 + i] * BLK, BLK), BLK)
            n = i * NB + k
            copies.append(
                pltpu.make_async_copy(src_ref.at[:, 0, at, :], blocks.at[n], sems.at[3 + n])
            )
    for copy in copies:
        copy.start()
    for copy in copies[1:3]:
        copy.wait()
    drive = packed(couple[...], wave[...])
    for copy in copies[:1] + copies[3:]:
        copy.wait()
    ys = []
    for i in range(2):
        at = slice(i * BLK, (i + 1) * BLK)
        both = []
        for k in range(NB):
            pair = blocks[i * NB + k]
            both.append(jnp.concatenate([pair[0], pair[1]], axis=1))
            both.append(jnp.concatenate([twist(pair[0]), twist(pair[1])], axis=1))
        ys.append(front_rows(held[at, :], jnp.concatenate(both, axis=0)))
        cols_ref[at, :] = tail_columns(held[at, :], patt_ref, BROWS - 2 + i)
    y = jnp.concatenate(ys, axis=0)
    y0, y1 = y[:, :BND], y[:, BND:]
    drive = drive - y0
    c = lax.axis_index(C)
    for out, which in ((keep_ref, c), (send_ref, 1 - c)):
        out[:BND] = pair_of(half_of(drive, which), half_of(y0, which))
        later = half_of(y1, which)
        out[BND:] = pair_of(later, later)


def owner_slot(distance, c):
    return jnp.where(distance == 1, 1 + c, jnp.where(distance == 3, 2 - c, (distance // 2) * 3))


def slot_distance(slot, c):
    return (0, 1 + 2 * c, 3 - 2 * c, 2)[slot]


def lift_kernel(beat, own_tree, far_tree, keep_ref, came_ref, own_lift, far_lift, *refs):
    acc = refs[-1]
    outs = refs[-4:-1]
    x, c = lax.axis_index(X), lax.axis_index(C)
    acc[...] = jnp.zeros_like(acc)
    if beat == 0:
        drives = keep_ref[:BND], came_ref[:BND]
    else:
        own_couple, far_couple, wave_ref = refs[:3]
        wave = wave_ref[...]
        drives = (
            applied(own_couple[...], wave) - keep_ref[BND:],
            applied(far_couple[...], to_first(wave)) - came_ref[BND:],
        )
    parts = [applied(mat[...], drive) for mat, drive in zip((own_lift, far_lift), drives)]
    first = is_first(parts[0][:BND]).astype(jnp.int32)
    for tree, part in zip((own_tree, far_tree), parts):
        for p in range(P_SIZE):
            block = tree[p]
            owner = (block % 8) // 2
            slot = owner_slot(jnp.bitwise_xor(owner, x), c) * 2 + block % 2
            term = part[p * BND : (p + 1) * BND]
            acc[slot] += jnp.where(first == 1 - block // 8, term, 0.0)

    at = 0
    for out in outs:
        for i in range(out.shape[0] // BND):
            out[i * BND : (i + 1) * BND] = acc[at]
            at += 1


def sep_kernel(*refs):
    pieces, (own_ref, far_ref, out_ref) = refs[:-3], refs[-3:]
    x, c = lax.axis_index(X), lax.axis_index(C)
    total = None
    for slot in range(NX):
        owner = jnp.bitwise_xor(x, slot_distance(slot, c))
        piece = pieces[slot // 2][slot % 2 * 2 * BND : (slot % 2 + 1) * 2 * BND]

        def columns(ref, base):
            return jnp.concatenate(
                [
                    ref[:, pl.ds(pl.multiple_of(base + at + owner * QUARTER, QUARTER), QUARTER)]
                    for at in (0, HALF)
                ],
                axis=1,
            )

        rows = jnp.concatenate(
            [columns(ref, base) for ref in (own_ref, far_ref) for base in (0, SEP)], axis=0
        )
        field = jnp.concatenate([piece, to_first(piece)], axis=0)
        part = mm(rows_split(rows), wide(field))
        total = part if total is None else total + part
    total = narrow(total)
    own = total[:BND] + twist(total[BND : 2 * BND])
    far = total[2 * BND : 3 * BND] + twist(total[3 * BND :])
    out_ref[...] = jnp.where(is_first(own), own, far)


def spread_kernel(beat, own_tree, far_tree, own_mat, far_mat, *refs):
    pieces, sol = refs[:NX], refs[-1]
    x, z, c = lax.axis_index(X), lax.axis_index(Z), lax.axis_index(C)
    for i, piece in enumerate(pieces):
        for k in range(2):
            sol[2 * (2 * (i // 2) + k) + i % 2] = piece[k * BND : (k + 1) * BND]
    zs = []
    for tree, mat in ((own_tree, own_mat), (far_tree, far_mat)):
        both = []
        for p in range(P_SIZE):
            block = tree[p]
            side = lax.rem((block // 2) % 2 + z, 2)
            slot = owner_slot(jnp.bitwise_xor(block // 4, x), c) * 2 + side
            field = sol[slot]
            field = jnp.where(block % 2 == c, field, to_first(field))
            both += [field, twist(field)]
        zs.append(narrow(mm(rows_split(mat[...]), wide(jnp.concatenate(both, axis=0)))))
    first = is_first(zs[0])
    if beat:
        refs[-2][:BND] = refs[NX][...]
        refs[-2][BND:] = jnp.where(first, zs[0], zs[1])
        return
    keep_ref, came_ref, own_cols, far_cols, z_ref, out_ref = refs[NX:-1]
    z_ref[...] = jnp.where(first, zs[0], zs[1])
    outs = []
    for held, cols, value in zip((keep_ref, came_ref), (own_cols, far_cols), zs):
        moved = narrow(mm(rows_split(cols[...]), wide(tail_field(value))))
        outs.append(held[:BND] - moved)
    out_ref[...] = jnp.where(first, to_first(outs[0]), outs[1])


STEPS = 2
STEP_ROWS = LEAF // STEPS
GROUP = 2


def bulk_kernel(step, patt_ref, src_ref, g_ref, first_ref, second_ref, cols_ref):
    def take(block):
        at = pl.ds(pl.multiple_of(block * BLK, BLK), BLK)
        return src_ref[0, 0, at, :], src_ref[1, 0, at, :]

    def some(n, carry):
        for i in range(GROUP):
            local = n * GROUP + i
            at = pl.ds(pl.multiple_of(local * BLK, BLK), BLK)
            low = pl.ds(pl.multiple_of(STEP_ROWS + local * BLK, BLK), BLK)
            row = step * (STEP_ROWS // BLK) + local
            g = g_ref[at, :]
            y = front_rows(g, gathered(patt_ref, row, take))
            first_ref[at, :] = y[:, :BND]
            second_ref[at, :] = y[:, BND:]
            cols_ref[at, :], cols_ref[low, :] = split(tail_columns(g, patt_ref, row))
        return carry

    lax.fori_loop(0, STEP_ROWS // BLK // GROUP, some, 0)


def field_kernel(own_ref, came_ref, *refs):
    y_refs, col_refs = refs[: 2 * STEPS], refs[2 * STEPS : 3 * STEPS]
    out_ref, buffer, sems = refs[3 * STEPS :]
    copies = []
    for beat in range(BEATS):
        own = own_ref[beat * BND : (beat + 1) * BND]
        came = came_ref[beat * BND : (beat + 1) * BND]
        first = is_first(own)
        z = jnp.where(
            lax.axis_index(C) == 0,
            jnp.where(first, own, came),
            jnp.where(first, to_first(came), to_second(own)),
        )
        tail = cols_split(tail_field(z))
        for i in range(STEPS):
            buffer[beat, i] = y_refs[2 * i + beat][...] - product(col_refs[i][...], tail)
            copy = pltpu.make_async_copy(
                buffer.at[beat, i],
                out_ref.at[beat, pl.ds(i * STEP_ROWS, STEP_ROWS), :],
                sems.at[beat, i],
            )
            copy.start()
            copies.append(copy)
    for copy in copies:
        copy.wait()


VM = pl.BlockSpec(memory_space=pltpu.VMEM)
SM = pl.BlockSpec(memory_space=pltpu.SMEM)


def shape(*dims):
    return jax.ShapeDtypeStruct(dims, F32)


ROOM = pltpu.CompilerParams(vmem_limit_bytes=12 << 20)


def cost(flops, size):
    return pl.CostEstimate(flops=flops, bytes_accessed=size, transcendentals=0)


def shifted(value, axis, distance):
    size = lax.axis_size(axis)
    return lax.ppermute(value, axis, [(i, (i + distance) % size) for i in range(size)])


def swapped(value, axis):
    return shifted(value, axis, 1)


HB = pl.BlockSpec(memory_space=pl.ANY)
FULL = pltpu.CompilerParams(vmem_limit_bytes=66_000_000)
NEAR1 = (1, 0, 3, 2)
NEAR3 = (3, 2, 1, 0)


def beside(value, turn):
    route = []
    for x in range(NX):
        for c in range(2):
            route.append((2 * x + c, 2 * (NEAR1, NEAR3)[(turn + c) % 2][x] + c))
    return lax.ppermute(value, (X, C), route)


def sweep(sources, front_inv, pattern, tree, lift, spread, couple, sep_inv, inflow):
    gmat, own_tree, patt = front_inv[0], tree[0, 0], pattern[0].T
    own_lift, own_spread, kmat, own_sep = lift[0], spread[0], couple[0], sep_inv[0]
    whole = lambda *dims: pl.BlockSpec(dims, lambda *i: (0,) * len(dims))
    block, double = shape(BND, BND), shape(2 * BND, BND)

    far_tree = swapped(own_tree, C)
    far_lift = swapped(own_lift, C)
    far_sep = swapped(own_sep, C)
    far_spread = swapped(own_spread, C)
    far_couple = swapped(kmat, C)

    keep, send, own_cols = pl.pallas_call(
        start_kernel,
        in_specs=[SM, HB, HB, HB, HB],
        out_specs=[VM, VM, VM],
        out_shape=[double, double, shape(BND, 2 * BND)],
        scratch_shapes=[
            pltpu.VMEM((2 * NB, 2, BLK, BND), F32),
            pltpu.VMEM((BND, NB * 2 * BLK), F32),
            pltpu.VMEM((BND, 2 * BND), F32),
            pltpu.VMEM((BND, BND), F32),
            pltpu.SemaphoreType.DMA((3 + 2 * NB,)),
        ],
        compiler_params=FULL,
        cost_estimate=cost(2 * 128 * 512 * 256 * 6, 1 << 21),
        name="start",
    )(patt, sources, front_inv, couple, inflow)
    came = swapped(send, C)
    far_cols = swapped(own_cols, C)

    ys, cols = [], []
    for step in range(STEPS):
        y0, y1, col = pl.pallas_call(
            functools.partial(bulk_kernel, step),
            grid=(1,),
            in_specs=[
                SM,
                whole(2, 1, LEAF, BND),
                pl.BlockSpec((STEP_ROWS, NB * 2 * BLK), lambda i, step=step: (step, 0)),
            ],
            out_specs=[
                whole(STEP_ROWS, BND),
                whole(STEP_ROWS, BND),
                whole(2 * STEP_ROWS, 2 * BND),
            ],
            out_shape=[
                shape(STEP_ROWS, BND),
                shape(STEP_ROWS, BND),
                jax.ShapeDtypeStruct((2 * STEP_ROWS, 2 * BND), BF16),
            ],
            compiler_params=ROOM,
            cost_estimate=cost(2 * 512 * 512 * 256 * 6, 3 << 20),
        )(patt, sources, gmat)
        ys.append((y0, y1))
        cols.append(col)

    for beat in range(BEATS):
        extra = ()
        if beat:
            devices = lax.axis_size("slab")
            incoming = lax.ppermute(outgoing, "slab", [(i, i + 1) for i in range(devices - 1)])
            extra = (kmat, far_couple, incoming)
        pieces = pl.pallas_call(
            functools.partial(lift_kernel, beat),
            in_specs=[SM, SM] + [VM] * (4 + len(extra)),
            out_specs=[VM] * 3,
            out_shape=[double, double, shape(4 * BND, BND)],
            scratch_shapes=[pltpu.VMEM((2 * NX, BND, BND), F32)],
            compiler_params=ROOM,
            cost_estimate=cost(2 * 512 * 256 * 128 * 4, 3 << 19),
        )(own_tree, far_tree, keep, came, own_lift, far_lift, *extra)
        outer = beside(pieces[2], 1)
        inner = beside(pieces[1] + outer[2 * BND :], 0)
        near = (pieces[0] + outer[: 2 * BND]) + inner
        mine = near + swapped(near, Z)
        inner = jnp.concatenate([mine, beside(mine, 0)], axis=0)
        outer = beside(inner, 1)
        sol = pl.pallas_call(
            sep_kernel,
            in_specs=[VM] * 4,
            out_specs=VM,
            out_shape=block,
            compiler_params=ROOM,
            cost_estimate=cost(2 * 256 * 2048 * 128 * 4, 5 << 20),
        )(inner, outer, own_sep, far_sep)
        other = swapped(sol, Z)
        held = [None] * NX
        for j, part in enumerate((sol, other)):
            held[j] = jnp.concatenate([part, beside(part, 0)], axis=0)
            held[2 + j] = beside(held[j], 1)
        extra = (zvals,) if beat else (keep, came, own_cols, far_cols)
        answer = pl.pallas_call(
            functools.partial(spread_kernel, beat),
            in_specs=[SM, SM] + [VM] * (NX + 2 + len(extra)),
            out_specs=[VM] * (2 - beat),
            out_shape=[double] if beat else [block] * 2,
            scratch_shapes=[pltpu.VMEM((2 * NX, BND, BND), F32)],
            compiler_params=ROOM,
            cost_estimate=cost(2 * 128 * 1024 * 128 * 4, 3 << 19),
        )(own_tree, far_tree, own_spread, far_spread, *held, *extra)
        zvals, outgoing = answer[0], answer[-1]
    zcame = swapped(zvals, C)
    result = pl.pallas_call(
        field_kernel,
        in_specs=[VM] * (2 + 3 * STEPS),
        out_specs=pl.BlockSpec(memory_space=pl.ANY),
        out_shape=shape(BEATS, LEAF, BND),
        scratch_shapes=[
            pltpu.VMEM((BEATS, STEPS, STEP_ROWS, BND), F32),
            pltpu.SemaphoreType.DMA((BEATS, STEPS)),
        ],
        compiler_params=ROOM,
        cost_estimate=cost(2 * 1024 * 256 * 256 * 4, 3 << 20),
        name="field",
    )(zvals, zcame, *ys[0], *ys[1], *cols)
    return result[:, None]


def solution(mesh):
    torus = Mesh(
        mesh.devices.reshape(mesh.shape["slab"], 4, 2, 2), ("slab", "front_0", "front_1", "front_2")
    )
    in_specs = (
        P(None, "slab", FRONT, None),
        P("slab", FRONT, None),
        P("slab", FRONT, None),
        P("slab", FRONT, None),
        P("slab", FRONT, None),
        P("slab", FRONT, None),
        P("slab", FRONT, None),
        P("slab", FRONT, None),
        P("slab", FRONT, None),
    )
    out_specs = P(None, "slab", FRONT, None)
    return jax.shard_map(sweep, mesh=torus, in_specs=in_specs, out_specs=out_specs, check_vma=False)
```

time: 146 us -> 151 us (1.034)
  waiting for transfers between devices: 56.7 us -> 59.9 us
  Pallas kernels: 22.7 us -> 24.4 us
    ppermute x24 -> x16, waiting for transfers between devices: 31.9 us -> 42.8 us  [beside(): return lax.ppermute(value, (X, C), route)]
    ppermute x14 -> x12, starting transfers between devices: 41.6 us -> 32.5 us  [shifted(): lax.ppermute(value, axis, [(i, (i + distance) % size) for i in range(size)])]
    ppermute x24 -> x16, starting transfers between devices: 18.9 us -> 27.4 us  [beside(): return lax.ppermute(value, (X, C), route)]
    ppermute x14 -> x12, waiting for transfers between devices: 20.9 us -> 13.5 us  [shifted(): lax.ppermute(value, axis, [(i, (i + distance) % size) for i in range(size)])]
    pallas_call x10 -> x7, Pallas kernels: 14.7 us -> 15.9 us  [the longest x2 6.37 us: sweep(): pl.pallas_call(sep_kernel, in_specs=[VM] * 4, out_specs=VM, out_shape=blo...]
  transfers between devices with their start and end apart: 39 -> 29, of which waited for: 27 -> 19; matrix products, arithmetic and copies ran while one was open for 0% -> 0% of each run, Pallas kernels for 9% -> 8%
where the time goes in v1:
time: 151 us; the launch traced here: 149 us
  starting transfers between devices  63.3 us (42%)
  waiting for transfers between devices  59.9 us (40%)
  Pallas kernels  24.4 us (16%)
    ppermute x16, waiting for transfers between devices, beside(): return lax.ppermute(value, (X, C), route)  42.8 us
    ppermute x12, starting transfers between devices, shifted(): lax.ppermute(value, axis, [(i, (i + distance) % size) for i in range(size)])  32.5 us
    ppermute x16, starting transfers between devices, beside(): return lax.ppermute(value, (X, C), route)  27.4 us
    ppermute x12, waiting for transfers between devices, shifted(): lax.ppermute(value, axis, [(i, (i + distance) % size) for i in range(size)])  13.5 us
    pallas_call x2, Pallas kernels, sweep(): pl.pallas_call(sep_kernel, in_specs=[VM] * 4, out_specs=VM, out_shape=blo...  6.37 us
    pallas_call x2, Pallas kernels, sweep(): pl.pallas_call(functools.partial(bulk_kernel, step), grid=(1,), in_specs=...  5.08 us
    pallas_call x2, Pallas kernels, sweep(): pl.pallas_call(functools.partial(lift_kernel, beat), in_specs=[SM, SM] +...  4.2 us
    ppermute x1, waiting for transfers between devices, sweep(): lax.ppermute(outgoing, 'slab', [(i, i + 1) for i in range(devices - 1)])  3.69 us
  transfers between devices with their start and end apart: 29, of which 19 were waited for; matrix products, arithmetic and copies ran while one was open for 0% of the time, Pallas kernels for 8%

profile of v1, /device:TPU:65, one launch (start us, length us, event | category | flops | bytes accessed | tf_op | source)
XLA Modules:
  0.0 149.2 jit_solution(15727053876509214515)
XLA Ops:
  0.8 3.4 %start.1 = (f32[256,128]{1,0:T(8,128)}, f32[256,128]{1,0:T(8,128)}, f32[128,256]{1,0:T(8,128)}) custom-call(s32[4,16]{1,0:T(4,128)} %bitcast.25, f32[2,1,1024,128]{3,2,1,0:T(8,128)} %src_ref.5, f32[1,1024,512]{2,1,0:T(8,128)} %g_ref.1, f32[1,128,256]{2,1,0:T(8,128)} %couple_ref.1, f32[1,128,128]{2,1,0:T(8,128)} %wave_ref.1), custom_call_target="tpu_custom_call" | custom-call | flops 201326592 | bytes 2097152 | tf_op jit(solution)/shard_map/start/pallas_call | solution.py:381
  10.0 4.3 %collective-permute-done.5 = f32[512,128]{1,0:T(8,128)S(1)} collective-permute-done((f32[512,128]{1,0:T(8,128)S(1)}, f32[512,128]{1,0:T(8,128)S(1)}, u32[]{:S(2)}, u32[]{:S(2)}) %collective-permute-start.5) | collective-permute-done | bytes 262176 | tf_op jit(solution)/shard_map/ppermute | solution.py:366
  14.4 2.6 %collective-permute-start.6 = (f32[256,128]{1,0:T(8,128)S(1)}, f32[256,128]{1,0:T(8,128)S(1)}, u32[]{:S(2)}, u32[]{:S(2)}) collective-permute-start(f32[256,128]{1,0:T(8,128)S(1)} %slice_add_fusion.2), channel_id=1, source_target_pairs={{0,4},{1,13},{4,0},{5,9},{8,12},{9,5},{12,8},{13,1},{2,6},{3,15},{... | collective-permute-start | bytes 393224 | tf_op jit(solution)/shard_map/ppermute | solution.py:366
  16.9 2.6 %collective-permute-done.6 = f32[256,128]{1,0:T(8,128)S(1)} collective-permute-done((f32[256,128]{1,0:T(8,128)S(1)}, f32[256,128]{1,0:T(8,128)S(1)}, u32[]{:S(2)}, u32[]{:S(2)}) %collective-permute-start.6) | collective-permute-done | bytes 131104 | tf_op jit(solution)/shard_map/ppermute | solution.py:366
  19.5 5.2 %collective-permute-start.7 = (f32[256,128]{1,0:T(8,128)S(1)}, f32[256,128]{1,0:T(8,128)S(1)}, u32[]{:S(2)}, u32[]{:S(2)}) collective-permute-start(f32[256,128]{1,0:T(8,128)S(1)} %fusion.1), channel_id=1, source_target_pairs={{0,2},{2,0},{1,3},{3,1},{4,6},{6,4},{5,7},{7,5},{8,10},{10,8},{9,1... | collective-permute-start | bytes 393224 | tf_op jit(solution)/shard_map/ppermute | solution.py:348
  24.7 4.1 %collective-permute-done.7 = f32[256,128]{1,0:T(8,128)S(1)} collective-permute-done((f32[256,128]{1,0:T(8,128)S(1)}, f32[256,128]{1,0:T(8,128)S(1)}, u32[]{:S(2)}, u32[]{:S(2)}) %collective-permute-start.7) | collective-permute-done | bytes 131104 | tf_op jit(solution)/shard_map/ppermute | solution.py:348
  28.8 2.7 %collective-permute-start.8 = (f32[256,128]{1,0:T(8,128)S(1)}, f32[256,128]{1,0:T(8,128)S(1)}, u32[]{:S(2)}, u32[]{:S(2)}) collective-permute-start(f32[256,128]{1,0:T(8,128)S(1)} %add.27), channel_id=1, source_target_pairs={{0,4},{1,13},{4,0},{5,9},{8,12},{9,5},{12,8},{13,1},{2,6},{3,15},{... | collective-permute-start | bytes 393224 | tf_op jit(solution)/shard_map/ppermute | solution.py:366
  31.5 2.5 %collective-permute-done.8 = f32[256,128]{1,0:T(8,128)S(1)} collective-permute-done((f32[256,128]{1,0:T(8,128)S(1)}, f32[256,128]{1,0:T(8,128)S(1)}, u32[]{:S(2)}, u32[]{:S(2)}) %collective-permute-start.8) | collective-permute-done | bytes 131104 | tf_op jit(solution)/shard_map/ppermute | solution.py:366
  34.1 5.4 %collective-permute-done.9.refs_1_ = f32[512,128]{1,0:T(8,128)S(1)} collective-permute-done((f32[512,128]{1,0:T(8,128)S(1)}, f32[512,128]{1,0:T(8,128)S(1)}, u32[]{:S(2)}, u32[]{:S(2)}) %collective-permute-start.9) | collective-permute-done | bytes 262176 | tf_op jit(solution)/shard_map/ppermute | solution.py:366
  39.5 3.1 %shard_map.92 = f32[128,128]{1,0:T(8,128)S(1)} custom-call(f32[512,128]{1,0:T(8,128)S(1)} %pad_maximum_fusion.refs_0_, f32[512,128]{1,0:T(8,128)S(1)} %collective-permute-done.9.refs_1_, f32[128,4096]{1,0:T(8,128)S(1)} %bitcast.15, f32[128,4096]{1,0:T(8,128)} %collective-permute-done.10.refs_3_), custom_call_target="tpu_custom_call" | custom-call | flops 536870912 | bytes 5242880 | tf_op jit(solution)/shard_map/pallas_call | solution.py:447
  42.7 2.6 %collective-permute-start.11 = (f32[128,128]{1,0:T(8,128)S(1)}, f32[128,128]{1,0:T(8,128)S(1)}, u32[]{:S(2)}, u32[]{:S(2)}) collective-permute-start(f32[128,128]{1,0:T(8,128)S(1)} %shard_map.92), channel_id=1, source_target_pairs={{0,4},{1,13},{4,0},{5,9},{8,12},{9,5},{12,8},{13,1},{2,6},{3,15},{... | collective-permute-start | bytes 196616 | tf_op jit(solution)/shard_map/ppermute | solution.py:366
  45.3 3.4 %collective-permute-start.1 = (f32[128,1024]{1,0:T(8,128)S(1)}, f32[128,1024]{1,0:T(8,128)S(1)}, u32[]{:S(2)}, u32[]{:S(2)}) collective-permute-start(f32[128,1024]{1,0:T(8,128)S(1)} %bitcast.17), channel_id=1, source_target_pairs={{0,1},{1,0},{2,3},{3,2},{4,5},{5,4},{6,7},{7,6},{8,9},{9,8},{10,11... | collective-permute-start | bytes 1572872 | tf_op jit(solution)/shard_map/ppermute | solution.py:348
  48.8 5.0 %collective-permute-start.12 = (f32[128,128]{1,0:T(8,128)S(1)}, f32[128,128]{1,0:T(8,128)S(1)}, u32[]{:S(2)}, u32[]{:S(2)}) collective-permute-start(f32[128,128]{1,0:T(8,128)S(1)} %shard_map.92), channel_id=1, source_target_pairs={{0,2},{2,0},{1,3},{3,1},{4,6},{6,4},{5,7},{7,5},{8,10},{10,8},{9,1... | collective-permute-start | bytes 196616 | tf_op jit(solution)/shard_map/ppermute | solution.py:348
  55.9 4.6 %collective-permute-start.13 = (f32[128,128]{1,0:T(8,128)S(1)}, f32[128,128]{1,0:T(8,128)S(1)}, u32[]{:S(2)}, u32[]{:S(2)}) collective-permute-start(f32[128,128]{1,0:T(8,128)S(1)} %collective-permute-done.12), channel_id=1, source_target_pairs={{0,4},{1,13},{4,0},{5,9},{8,12},{9,5},{12,8},{13,1},{2,6},{3,15},{... | collective-permute-start | bytes 196616 | tf_op jit(solution)/shard_map/ppermute | solution.py:366
  63.2 2.5 %collective-permute-start.4 = (f32[128,256]{1,0:T(8,128)S(1)}, f32[128,256]{1,0:T(8,128)S(1)}, u32[]{:S(2)}, u32[]{:S(2)}) collective-permute-start(f32[128,256]{1,0:T(8,128)S(1)} %bitcast.23), channel_id=1, source_target_pairs={{0,1},{1,0},{2,3},{3,2},{4,5},{5,4},{6,7},{7,6},{8,9},{9,8},{10,11... | collective-permute-start | bytes 393224 | tf_op jit(solution)/shard_map/ppermute | solution.py:348
  68.0 3.4 %collective-permute-start.17 = (f32[128,128]{1,0:T(8,128)S(1)}, f32[128,128]{1,0:T(8,128)S(1)}, u32[]{:S(2)}, u32[]{:S(2)}) collective-permute-start(f32[128,128]{1,0:T(8,128)S(1)} %get-tuple-element.28), channel_id=1, source_target_pairs={{0,16},{16,32},{32,48},{48,64},{64,80},{80,96},{96,112},{112,128},... | collective-permute-start | bytes 196616 | tf_op jit(solution)/shard_map/ppermute | solution.py:430
  71.4 3.7 %collective-permute-done.17.refs_2_ = f32[128,128]{1,0:T(8,128)S(1)} collective-permute-done((f32[128,128]{1,0:T(8,128)S(1)}, f32[128,128]{1,0:T(8,128)S(1)}, u32[]{:S(2)}, u32[]{:S(2)}) %collective-permute-start.17) | collective-permute-done | bytes 65568 | tf_op jit(solution)/shard_map/ppermute | solution.py:430
  78.5 4.2 %collective-permute-done.18 = f32[512,128]{1,0:T(8,128)S(1)} collective-permute-done((f32[512,128]{1,0:T(8,128)S(1)}, f32[512,128]{1,0:T(8,128)S(1)}, u32[]{:S(2)}, u32[]{:S(2)}) %collective-permute-start.18) | collective-permute-done | bytes 262176 | tf_op jit(solution)/shard_map/ppermute | solution.py:366
  82.8 2.8 %collective-permute-start.19 = (f32[256,128]{1,0:T(8,128)S(1)}, f32[256,128]{1,0:T(8,128)S(1)}, u32[]{:S(2)}, u32[]{:S(2)}) collective-permute-start(f32[256,128]{1,0:T(8,128)S(1)} %slice_add_fusion), channel_id=1, source_target_pairs={{0,4},{1,13},{4,0},{5,9},{8,12},{9,5},{12,8},{13,1},{2,6},{3,15},{... | collective-permute-start | bytes 393224 | tf_op jit(solution)/shard_map/ppermute | solution.py:366
  85.5 4.1 %collective-permute-done.19 = f32[256,128]{1,0:T(8,128)S(1)} collective-permute-done((f32[256,128]{1,0:T(8,128)S(1)}, f32[256,128]{1,0:T(8,128)S(1)}, u32[]{:S(2)}, u32[]{:S(2)}) %collective-permute-start.19) | collective-permute-done | bytes 131104 | tf_op jit(solution)/shard_map/ppermute | solution.py:366
  89.6 4.2 %collective-permute-start.20 = (f32[256,128]{1,0:T(8,128)S(1)}, f32[256,128]{1,0:T(8,128)S(1)}, u32[]{:S(2)}, u32[]{:S(2)}) collective-permute-start(f32[256,128]{1,0:T(8,128)S(1)} %fusion), channel_id=1, source_target_pairs={{0,2},{2,0},{1,3},{3,1},{4,6},{6,4},{5,7},{7,5},{8,10},{10,8},{9,1... | collective-permute-start | bytes 393224 | tf_op jit(solution)/shard_map/ppermute | solution.py:348
  93.8 3.6 %collective-permute-done.20 = f32[256,128]{1,0:T(8,128)S(1)} collective-permute-done((f32[256,128]{1,0:T(8,128)S(1)}, f32[256,128]{1,0:T(8,128)S(1)}, u32[]{:S(2)}, u32[]{:S(2)}) %collective-permute-start.20) | collective-permute-done | bytes 131104 | tf_op jit(solution)/shard_map/ppermute | solution.py:348
  97.4 2.8 %collective-permute-start.21 = (f32[256,128]{1,0:T(8,128)S(1)}, f32[256,128]{1,0:T(8,128)S(1)}, u32[]{:S(2)}, u32[]{:S(2)}) collective-permute-start(f32[256,128]{1,0:T(8,128)S(1)} %add.31), channel_id=1, source_target_pairs={{0,4},{1,13},{4,0},{5,9},{8,12},{9,5},{12,8},{13,1},{2,6},{3,15},{... | collective-permute-start | bytes 393224 | tf_op jit(solution)/shard_map/ppermute | solution.py:366
  102.7 5.2 %collective-permute-done.22.refs_1_ = f32[512,128]{1,0:T(8,128)S(1)} collective-permute-done((f32[512,128]{1,0:T(8,128)S(1)}, f32[512,128]{1,0:T(8,128)S(1)}, u32[]{:S(2)}, u32[]{:S(2)}) %collective-permute-start.22) | collective-permute-done | bytes 262176 | tf_op jit(solution)/shard_map/ppermute | solution.py:366
  107.9 3.2 %shard_map.95 = f32[128,128]{1,0:T(8,128)S(1)} custom-call(f32[512,128]{1,0:T(8,128)S(1)} %pad_maximum_fusion.1.refs_0_, f32[512,128]{1,0:T(8,128)S(1)} %collective-permute-done.22.refs_1_, f32[128,4096]{1,0:T(8,128)S(1)} %bitcast.16, f32[128,4096]{1,0:T(8,128)} %collective-permute-done.10.refs_3_), custom_call_target="tpu_custom_call" | custom-call | flops 536870912 | bytes 5242880 | tf_op jit(solution)/shard_map/pallas_call | solution.py:447
  111.1 3.9 %collective-permute-start.23 = (f32[128,128]{1,0:T(8,128)S(1)}, f32[128,128]{1,0:T(8,128)S(1)}, u32[]{:S(2)}, u32[]{:S(2)}) collective-permute-start(f32[128,128]{1,0:T(8,128)S(1)} %shard_map.95), channel_id=1, source_target_pairs={{0,4},{1,13},{4,0},{5,9},{8,12},{9,5},{12,8},{13,1},{2,6},{3,15},{... | collective-permute-start | bytes 196616 | tf_op jit(solution)/shard_map/ppermute | solution.py:366
  117.8 4.3 %collective-permute-done.24 = f32[128,128]{1,0:T(8,128)S(1)} collective-permute-done((f32[128,128]{1,0:T(8,128)S(1)}, f32[128,128]{1,0:T(8,128)S(1)}, u32[]{:S(2)}, u32[]{:S(2)}) %collective-permute-start.24) | collective-permute-done | bytes 65568 | tf_op jit(solution)/shard_map/ppermute | solution.py:348
  122.2 4.2 %collective-permute-done.25 = f32[128,128]{1,0:T(8,128)S(1)} collective-permute-done((f32[128,128]{1,0:T(8,128)S(1)}, f32[128,128]{1,0:T(8,128)S(1)}, u32[]{:S(2)}, u32[]{:S(2)}) %collective-permute-start.25) | collective-permute-done | bytes 65568 | tf_op jit(solution)/shard_map/ppermute | solution.py:366
  126.5 3.8 %collective-permute-done.27.refs_3_ = f32[256,128]{1,0:T(8,128)S(1)} collective-permute-done((f32[256,128]{1,0:T(8,128)S(1)}, f32[256,128]{1,0:T(8,128)S(1)}, u32[]{:S(2)}, u32[]{:S(2)}) %collective-permute-start.27) | collective-permute-done | bytes 131104 | tf_op jit(solution)/shard_map/ppermute | solution.py:366
  131.8 10.3 %collective-permute-start.28 = (f32[256,128]{1,0:T(8,128)S(1)}, f32[256,128]{1,0:T(8,128)S(1)}, u32[]{:S(2)}, u32[]{:S(2)}) collective-permute-start(f32[256,128]{1,0:T(8,128)S(1)} %shard_map.96.own_ref), channel_id=1, source_target_pairs={{0,1},{1,0},{2,3},{3,2},{4,5},{5,4},{6,7},{7,6},{8,9},{9,8},{10,11... | collective-permute-start | bytes 393224 | tf_op jit(solution)/shard_map/ppermute | solution.py:348
  142.2 2.5 %shard_map.97 = (f32[512,128]{1,0:T(8,128)S(1)}, f32[512,128]{1,0:T(8,128)S(1)}, bf16[1024,256]{1,0:T(8,128)(2,1)S(1)}) custom-call(s32[4,16]{1,0:T(4,128)S(1)} %bitcast.26, f32[2,1,1024,128]{3,2,1,0:T(8,128)S(1)} %copy-done.1, f32[1024,512]{1,0:T(8,128)S(1)} %bitcast.12), custom_call_target="tpu_custom_call" | custom-call | flops 805306368 | bytes 3145728 | tf_op jit(solution)/shard_map/pallas_call | solution.py:402
  144.7 2.6 %shard_map.98 = (f32[512,128]{1,0:T(8,128)S(1)}, f32[512,128]{1,0:T(8,128)S(1)}, bf16[1024,256]{1,0:T(8,128)(2,1)S(1)}) custom-call(s32[4,16]{1,0:T(4,128)S(1)} %bitcast.27, f32[2,1,1024,128]{3,2,1,0:T(8,128)S(1)} %copy-done.1, f32[1024,512]{1,0:T(8,128)S(1)} %bitcast.13), custom_call_target="tpu_custom_call" | custom-call | flops 805306368 | bytes 3145728 | tf_op jit(solution)/shard_map/pallas_call | solution.py:402
  (72 shorter events, 26.2 us)
Async XLA Ops:
  0.0 39.5 %collective-permute-start.10 = (f32[128,4096]{1,0:T(8,128)}, f32[128,4096]{1,0:T(8,128)}, u32[]{:S(2)}, u32[]{:S(2)}) collective-permute-start(f32[128,4096]{1,0:T(8,128)} %bitcast.14), channel_id=1, source_target_pairs={{0,1},{1,0},{2,3},{3,2},{4,5},{5,4},{6,7},{7,6},{8,9},{9,8},{10,11... | collective-permute-start | bytes 6291464 | tf_op jit(solution)/shard_map/ppermute | solution.py:348
  0.7 5.2 %collective-permute-start.3 = (f32[512,256]{1,0:T(8,128)}, f32[512,256]{1,0:T(8,128)}, u32[]{:S(2)}, u32[]{:S(2)}) collective-permute-start(f32[512,256]{1,0:T(8,128)} %bitcast.20), channel_id=1, source_target_pairs={{0,1},{1,0},{2,3},{3,2},{4,5},{5,4},{6,7},{7,6},{8,9},{9,8},{10,11... | collective-permute-start | bytes 1572872 | tf_op jit(solution)/shard_map/ppermute | solution.py:348
  4.2 35.3 %copy-start.2 = (f32[1,128,4096]{2,1,0:T(8,128)S(1)}, f32[1,128,4096]{2,1,0:T(8,128)}, u32[]{:S(2)}) copy-start(f32[1,128,4096]{2,1,0:T(8,128)} %param.16) | copy-start | bytes 6291460
  4.2 1.7 %collective-permute-start.2 = (f32[256,128]{1,0:T(8,128)}, f32[256,128]{1,0:T(8,128)S(1)}, u32[]{:S(2)}, u32[]{:S(2)}) collective-permute-start(f32[256,128]{1,0:T(8,128)} %get-tuple-element.23), channel_id=1, source_target_pairs={{0,1},{1,0},{2,3},{3,2},{4,5},{5,4},{6,7},{7,6},{8,9},{9,8},{10,11... | collective-permute-start | bytes 393224 | tf_op jit(solution)/shard_map/ppermute | solution.py:348
  4.7 1.2 collective-permute-start
  8.8 5.6 %collective-permute-start.5 = (f32[512,128]{1,0:T(8,128)S(1)}, f32[512,128]{1,0:T(8,128)S(1)}, u32[]{:S(2)}, u32[]{:S(2)}) collective-permute-start(f32[512,128]{1,0:T(8,128)S(1)} %get-tuple-element.25), channel_id=1, source_target_pairs={{0,12},{1,5},{4,8},{5,1},{8,4},{9,13},{12,0},{13,9},{2,14},{3,7},{... | collective-permute-start | bytes 786440 | tf_op jit(solution)/shard_map/ppermute | solution.py:366
  14.4 5.1 %collective-permute-start.6 = (f32[256,128]{1,0:T(8,128)S(1)}, f32[256,128]{1,0:T(8,128)S(1)}, u32[]{:S(2)}, u32[]{:S(2)}) collective-permute-start(f32[256,128]{1,0:T(8,128)S(1)} %slice_add_fusion.2), channel_id=1, source_target_pairs={{0,4},{1,13},{4,0},{5,9},{8,12},{9,5},{12,8},{13,1},{2,6},{3,15},{... | collective-permute-start | bytes 393224 | tf_op jit(solution)/shard_map/ppermute | solution.py:366
  19.5 9.3 %collective-permute-start.7 = (f32[256,128]{1,0:T(8,128)S(1)}, f32[256,128]{1,0:T(8,128)S(1)}, u32[]{:S(2)}, u32[]{:S(2)}) collective-permute-start(f32[256,128]{1,0:T(8,128)S(1)} %fusion.1), channel_id=1, source_target_pairs={{0,2},{2,0},{1,3},{3,1},{4,6},{6,4},{5,7},{7,5},{8,10},{10,8},{9,1... | collective-permute-start | bytes 393224 | tf_op jit(solution)/shard_map/ppermute | solution.py:348
  28.8 5.1 %collective-permute-start.8 = (f32[256,128]{1,0:T(8,128)S(1)}, f32[256,128]{1,0:T(8,128)S(1)}, u32[]{:S(2)}, u32[]{:S(2)}) collective-permute-start(f32[256,128]{1,0:T(8,128)S(1)} %add.27), channel_id=1, source_target_pairs={{0,4},{1,13},{4,0},{5,9},{8,12},{9,5},{12,8},{13,1},{2,6},{3,15},{... | collective-permute-start | bytes 393224 | tf_op jit(solution)/shard_map/ppermute | solution.py:366
  34.0 32.0 %copy-start.6 = (f32[256,128]{1,0:T(8,128)S(1)}, f32[256,128]{1,0:T(8,128)}, u32[]{:S(2)}) copy-start(f32[256,128]{1,0:T(8,128)} %get-tuple-element.22.keep_ref.refs_4_) | copy-start | bytes 393220
  34.0 5.5 %collective-permute-start.9 = (f32[512,128]{1,0:T(8,128)S(1)}, f32[512,128]{1,0:T(8,128)S(1)}, u32[]{:S(2)}, u32[]{:S(2)}) collective-permute-start(f32[512,128]{1,0:T(8,128)S(1)} %pad_maximum_fusion.refs_0_), channel_id=1, source_target_pairs={{0,12},{1,5},{4,8},{5,1},{8,4},{9,13},{12,0},{13,9},{2,14},{3,7},{... | collective-permute-start | bytes 786440 | tf_op jit(solution)/shard_map/ppermute | solution.py:366
  42.7 11.1 %collective-permute-start.11 = (f32[128,128]{1,0:T(8,128)S(1)}, f32[128,128]{1,0:T(8,128)S(1)}, u32[]{:S(2)}, u32[]{:S(2)}) collective-permute-start(f32[128,128]{1,0:T(8,128)S(1)} %shard_map.92), channel_id=1, source_target_pairs={{0,4},{1,13},{4,0},{5,9},{8,12},{9,5},{12,8},{13,1},{2,6},{3,15},{... | collective-permute-start | bytes 196616 | tf_op jit(solution)/shard_map/ppermute | solution.py:366
  45.3 20.4 %collective-permute-start.1 = (f32[128,1024]{1,0:T(8,128)S(1)}, f32[128,1024]{1,0:T(8,128)S(1)}, u32[]{:S(2)}, u32[]{:S(2)}) collective-permute-start(f32[128,1024]{1,0:T(8,128)S(1)} %bitcast.17), channel_id=1, source_target_pairs={{0,1},{1,0},{2,3},{3,2},{4,5},{5,4},{6,7},{7,6},{8,9},{9,8},{10,11... | collective-permute-start | bytes 1572872 | tf_op jit(solution)/shard_map/ppermute | solution.py:348
  48.7 17.0 %collective-permute-start.16 = (f32[128,256]{1,0:T(8,128)S(1)}, f32[128,256]{1,0:T(8,128)S(1)}, u32[]{:S(2)}, u32[]{:S(2)}) collective-permute-start(f32[128,256]{1,0:T(8,128)S(1)} %copy-done.8), channel_id=1, source_target_pairs={{0,1},{1,0},{2,3},{3,2},{4,5},{5,4},{6,7},{7,6},{8,9},{9,8},{10,11... | collective-permute-start | bytes 393224 | tf_op jit(solution)/shard_map/ppermute | solution.py:348
  48.8 7.1 %collective-permute-start.12 = (f32[128,128]{1,0:T(8,128)S(1)}, f32[128,128]{1,0:T(8,128)S(1)}, u32[]{:S(2)}, u32[]{:S(2)}) collective-permute-start(f32[128,128]{1,0:T(8,128)S(1)} %shard_map.92), channel_id=1, source_target_pairs={{0,2},{2,0},{1,3},{3,1},{4,6},{6,4},{5,7},{7,5},{8,10},{10,8},{9,1... | collective-permute-start | bytes 196616 | tf_op jit(solution)/shard_map/ppermute | solution.py:348
  53.8 11.8 %collective-permute-start.14 = (f32[256,128]{1,0:T(8,128)S(1)}, f32[256,128]{1,0:T(8,128)S(1)}, u32[]{:S(2)}, u32[]{:S(2)}) collective-permute-start(f32[256,128]{1,0:T(8,128)S(1)} %pad_maximum_fusion.2.refs_0_), channel_id=1, source_target_pairs={{0,12},{1,5},{4,8},{5,1},{8,4},{9,13},{12,0},{13,9},{2,14},{3,7},{... | collective-permute-start | bytes 393224 | tf_op jit(solution)/shard_map/ppermute | solution.py:366
  55.9 6.2 %collective-permute-start.13 = (f32[128,128]{1,0:T(8,128)S(1)}, f32[128,128]{1,0:T(8,128)S(1)}, u32[]{:S(2)}, u32[]{:S(2)}) collective-permute-start(f32[128,128]{1,0:T(8,128)S(1)} %collective-permute-done.12), channel_id=1, source_target_pairs={{0,4},{1,13},{4,0},{5,9},{8,12},{9,5},{12,8},{13,1},{2,6},{3,15},{... | collective-permute-start | bytes 196616 | tf_op jit(solution)/shard_map/ppermute | solution.py:366
  62.2 3.8 %collective-permute-start.15 = (f32[256,128]{1,0:T(8,128)S(1)}, f32[256,128]{1,0:T(8,128)S(1)}, u32[]{:S(2)}, u32[]{:S(2)}) collective-permute-start(f32[256,128]{1,0:T(8,128)S(1)} %constant_dynamic-update-slice_fusion.refs_1_), channel_id=1, source_target_pairs={{0,12},{1,5},{4,8},{5,1},{8,4},{9,13},{12,0},{13,9},{2,14},{3,7},{... | collective-permute-start | bytes 393224 | tf_op jit(solution)/shard_map/ppermute | solution.py:366
  63.2 8.2 %collective-permute-start.4 = (f32[128,256]{1,0:T(8,128)S(1)}, f32[128,256]{1,0:T(8,128)S(1)}, u32[]{:S(2)}, u32[]{:S(2)}) collective-permute-start(f32[128,256]{1,0:T(8,128)S(1)} %bitcast.23), channel_id=1, source_target_pairs={{0,1},{1,0},{2,3},{3,2},{4,5},{5,4},{6,7},{7,6},{8,9},{9,8},{10,11... | collective-permute-start | bytes 393224 | tf_op jit(solution)/shard_map/ppermute | solution.py:348
  68.0 7.1 %collective-permute-start.17 = (f32[128,128]{1,0:T(8,128)S(1)}, f32[128,128]{1,0:T(8,128)S(1)}, u32[]{:S(2)}, u32[]{:S(2)}) collective-permute-start(f32[128,128]{1,0:T(8,128)S(1)} %get-tuple-element.28), channel_id=1, source_target_pairs={{0,16},{16,32},{32,48},{48,64},{64,80},{80,96},{96,112},{112,128},... | collective-permute-start | bytes 196616 | tf_op jit(solution)/shard_map/ppermute | solution.py:430
  77.4 5.3 %collective-permute-start.18 = (f32[512,128]{1,0:T(8,128)S(1)}, f32[512,128]{1,0:T(8,128)S(1)}, u32[]{:S(2)}, u32[]{:S(2)}) collective-permute-start(f32[512,128]{1,0:T(8,128)S(1)} %get-tuple-element.30), channel_id=1, source_target_pairs={{0,12},{1,5},{4,8},{5,1},{8,4},{9,13},{12,0},{13,9},{2,14},{3,7},{... | collective-permute-start | bytes 786440 | tf_op jit(solution)/shard_map/ppermute | solution.py:366
  82.8 6.8 %collective-permute-start.19 = (f32[256,128]{1,0:T(8,128)S(1)}, f32[256,128]{1,0:T(8,128)S(1)}, u32[]{:S(2)}, u32[]{:S(2)}) collective-permute-start(f32[256,128]{1,0:T(8,128)S(1)} %slice_add_fusion), channel_id=1, source_target_pairs={{0,4},{1,13},{4,0},{5,9},{8,12},{9,5},{12,8},{13,1},{2,6},{3,15},{... | collective-permute-start | bytes 393224 | tf_op jit(solution)/shard_map/ppermute | solution.py:366
  89.6 7.8 %collective-permute-start.20 = (f32[256,128]{1,0:T(8,128)S(1)}, f32[256,128]{1,0:T(8,128)S(1)}, u32[]{:S(2)}, u32[]{:S(2)}) collective-permute-start(f32[256,128]{1,0:T(8,128)S(1)} %fusion), channel_id=1, source_target_pairs={{0,2},{2,0},{1,3},{3,1},{4,6},{6,4},{5,7},{7,5},{8,10},{10,8},{9,1... | collective-permute-start | bytes 393224 | tf_op jit(solution)/shard_map/ppermute | solution.py:348
  97.4 5.1 %collective-permute-start.21 = (f32[256,128]{1,0:T(8,128)S(1)}, f32[256,128]{1,0:T(8,128)S(1)}, u32[]{:S(2)}, u32[]{:S(2)}) collective-permute-start(f32[256,128]{1,0:T(8,128)S(1)} %add.31), channel_id=1, source_target_pairs={{0,4},{1,13},{4,0},{5,9},{8,12},{9,5},{12,8},{13,1},{2,6},{3,15},{... | collective-permute-start | bytes 393224 | tf_op jit(solution)/shard_map/ppermute | solution.py:366
  102.6 5.3 %collective-permute-start.22 = (f32[512,128]{1,0:T(8,128)S(1)}, f32[512,128]{1,0:T(8,128)S(1)}, u32[]{:S(2)}, u32[]{:S(2)}) collective-permute-start(f32[512,128]{1,0:T(8,128)S(1)} %pad_maximum_fusion.1.refs_0_), channel_id=1, source_target_pairs={{0,12},{1,5},{4,8},{5,1},{8,4},{9,13},{12,0},{13,9},{2,14},{3,7},{... | collective-permute-start | bytes 786440 | tf_op jit(solution)/shard_map/ppermute | solution.py:366
  107.9 34.3 %copy-start.1 = (f32[2,1,1024,128]{3,2,1,0:T(8,128)S(1)}, f32[2,1,1024,128]{3,2,1,0:T(8,128)}, u32[]{:S(2)}) copy-start(f32[2,1,1024,128]{3,2,1,0:T(8,128)} %src_ref.5) | copy-start | bytes 3145732
  111.1 6.6 %collective-permute-start.23 = (f32[128,128]{1,0:T(8,128)S(1)}, f32[128,128]{1,0:T(8,128)S(1)}, u32[]{:S(2)}, u32[]{:S(2)}) collective-permute-start(f32[128,128]{1,0:T(8,128)S(1)} %shard_map.95), channel_id=1, source_target_pairs={{0,4},{1,13},{4,0},{5,9},{8,12},{9,5},{12,8},{13,1},{2,6},{3,15},{... | collective-permute-start | bytes 196616 | tf_op jit(solution)/shard_map/ppermute | solution.py:366
  115.1 7.0 %collective-permute-start.24 = (f32[128,128]{1,0:T(8,128)S(1)}, f32[128,128]{1,0:T(8,128)S(1)}, u32[]{:S(2)}, u32[]{:S(2)}) collective-permute-start(f32[128,128]{1,0:T(8,128)S(1)} %shard_map.95), channel_id=1, source_target_pairs={{0,2},{2,0},{1,3},{3,1},{4,6},{6,4},{5,7},{7,5},{8,10},{10,8},{9,1... | collective-permute-start | bytes 196616 | tf_op jit(solution)/shard_map/ppermute | solution.py:348
  117.7 8.7 %collective-permute-start.26 = (f32[256,128]{1,0:T(8,128)S(1)}, f32[256,128]{1,0:T(8,128)S(1)}, u32[]{:S(2)}, u32[]{:S(2)}) collective-permute-start(f32[256,128]{1,0:T(8,128)S(1)} %pad_maximum_fusion.3.refs_0_), channel_id=1, source_target_pairs={{0,12},{1,5},{4,8},{5,1},{8,4},{9,13},{12,0},{13,9},{2,14},{3,7},{... | collective-permute-start | bytes 393224 | tf_op jit(solution)/shard_map/ppermute | solution.py:366
  122.1 4.3 %collective-permute-start.25 = (f32[128,128]{1,0:T(8,128)S(1)}, f32[128,128]{1,0:T(8,128)S(1)}, u32[]{:S(2)}, u32[]{:S(2)}) collective-permute-start(f32[128,128]{1,0:T(8,128)S(1)} %collective-permute-done.24), channel_id=1, source_target_pairs={{0,4},{1,13},{4,0},{5,9},{8,12},{9,5},{12,8},{13,1},{2,6},{3,15},{... | collective-permute-start | bytes 196616 | tf_op jit(solution)/shard_map/ppermute | solution.py:366
  126.4 3.8 %collective-permute-start.27 = (f32[256,128]{1,0:T(8,128)S(1)}, f32[256,128]{1,0:T(8,128)S(1)}, u32[]{:S(2)}, u32[]{:S(2)}) collective-permute-start(f32[256,128]{1,0:T(8,128)S(1)} %constant_dynamic-update-slice_fusion.2.refs_1_), channel_id=1, source_target_pairs={{0,12},{1,5},{4,8},{5,1},{8,4},{9,13},{12,0},{13,9},{2,14},{3,7},{... | collective-permute-start | bytes 393224 | tf_op jit(solution)/shard_map/ppermute | solution.py:366
  131.8 15.4 %collective-permute-start.28 = (f32[256,128]{1,0:T(8,128)S(1)}, f32[256,128]{1,0:T(8,128)S(1)}, u32[]{:S(2)}, u32[]{:S(2)}) collective-permute-start(f32[256,128]{1,0:T(8,128)S(1)} %shard_map.96.own_ref), channel_id=1, source_target_pairs={{0,1},{1,0},{2,3},{3,2},{4,5},{5,4},{6,7},{7,6},{8,9},{9,8},{10,11... | collective-permute-start | bytes 393224 | tf_op jit(solution)/shard_map/ppermute | solution.py:348
  (8 other events, 128.9 us)

commit v2 on v1

--- a/solution.py
+++ b/solution.py
@@ -176,18 +176,20 @@
         out[BND:] = pair_of(later, later)
 
 
-def owner_slot(distance, c):
-    return jnp.where(distance == 1, 1 + c, jnp.where(distance == 3, 2 - c, (distance // 2) * 3))
-
-
-def slot_distance(slot, c):
-    return (0, 1 + 2 * c, 3 - 2 * c, 2)[slot]
-
-
 def lift_kernel(beat, own_tree, far_tree, keep_ref, came_ref, own_lift, far_lift, *refs):
+    copies = ()
+    if beat == 0:
+        *refs, lift_here, tree_here, sems = refs
+        copies = (
+            pltpu.make_async_copy(own_lift, lift_here, sems.at[0]),
+            pltpu.make_async_copy(own_tree, tree_here, sems.at[1]),
+        )
+        for copy in copies:
+            copy.start()
+        own_lift, own_tree = lift_here, tree_here
     acc = refs[-1]
-    outs = refs[-4:-1]
-    x, c = lax.axis_index(X), lax.axis_index(C)
+    outs = refs[-1 - NX : -1]
+    x = lax.axis_index(X)
     acc[...] = jnp.zeros_like(acc)
     if beat == 0:
         drives = keep_ref[:BND], came_ref[:BND]
@@ -198,13 +200,16 @@
             applied(own_couple[...], wave) - keep_ref[BND:],
             applied(far_couple[...], to_first(wave)) - came_ref[BND:],
         )
-    parts = [applied(mat[...], drive) for mat, drive in zip((own_lift, far_lift), drives)]
+    far_part = applied(far_lift[...], drives[1])
+    for copy in copies:
+        copy.wait()
+    parts = [applied(own_lift[...], drives[0]), far_part]
     first = is_first(parts[0][:BND]).astype(jnp.int32)
     for tree, part in zip((own_tree, far_tree), parts):
         for p in range(P_SIZE):
             block = tree[p]
             owner = (block % 8) // 2
-            slot = owner_slot(jnp.bitwise_xor(owner, x), c) * 2 + block % 2
+            slot = lax.rem(owner - x + NX, NX) * 2 + block % 2
             term = part[p * BND : (p + 1) * BND]
             acc[slot] += jnp.where(first == 1 - block // 8, term, 0.0)
 
@@ -217,11 +222,11 @@
 
 def sep_kernel(*refs):
     pieces, (own_ref, far_ref, out_ref) = refs[:-3], refs[-3:]
-    x, c = lax.axis_index(X), lax.axis_index(C)
+    x = lax.axis_index(X)
     total = None
     for slot in range(NX):
-        owner = jnp.bitwise_xor(x, slot_distance(slot, c))
-        piece = pieces[slot // 2][slot % 2 * 2 * BND : (slot % 2 + 1) * 2 * BND]
+        owner = lax.rem(x - slot + NX, NX)
+        piece = pieces[slot][...]
 
         def columns(ref, base):
             return jnp.concatenate(
@@ -245,28 +250,27 @@
 
 
 def spread_kernel(beat, own_tree, far_tree, own_mat, far_mat, *refs):
-    pieces, sol = refs[:NX], refs[-1]
+    pieces, sol = refs[: 2 * NX], refs[-1]
     x, z, c = lax.axis_index(X), lax.axis_index(Z), lax.axis_index(C)
     for i, piece in enumerate(pieces):
-        for k in range(2):
-            sol[2 * (2 * (i // 2) + k) + i % 2] = piece[k * BND : (k + 1) * BND]
+        sol[i] = piece[...]
     zs = []
     for tree, mat in ((own_tree, own_mat), (far_tree, far_mat)):
         both = []
         for p in range(P_SIZE):
             block = tree[p]
             side = lax.rem((block // 2) % 2 + z, 2)
-            slot = owner_slot(jnp.bitwise_xor(block // 4, x), c) * 2 + side
-            field = sol[slot]
+            slot = lax.rem(x - block // 4 + NX, NX)
+            field = sol[side * NX + slot]
             field = jnp.where(block % 2 == c, field, to_first(field))
             both += [field, twist(field)]
         zs.append(narrow(mm(rows_split(mat[...]), wide(jnp.concatenate(both, axis=0)))))
     first = is_first(zs[0])
     if beat:
-        refs[-2][:BND] = refs[NX][...]
+        refs[-2][:BND] = refs[2 * NX][...]
         refs[-2][BND:] = jnp.where(first, zs[0], zs[1])
         return
-    keep_ref, came_ref, own_cols, far_cols, z_ref, out_ref = refs[NX:-1]
+    keep_ref, came_ref, own_cols, far_cols, z_ref, out_ref = refs[2 * NX : -1]
     z_ref[...] = jnp.where(first, zs[0], zs[1])
     outs = []
     for held, cols, value in zip((keep_ref, came_ref), (own_cols, far_cols), zs):
@@ -352,18 +356,18 @@
     return shifted(value, axis, 1)
 
 
-HB = pl.BlockSpec(memory_space=pl.ANY)
-FULL = pltpu.CompilerParams(vmem_limit_bytes=66_000_000)
-NEAR1 = (1, 0, 3, 2)
-NEAR3 = (3, 2, 1, 0)
-
-
-def beside(value, turn):
-    route = []
-    for x in range(NX):
-        for c in range(2):
-            route.append((2 * x + c, 2 * (NEAR1, NEAR3)[(turn + c) % 2][x] + c))
-    return lax.ppermute(value, (X, C), route)
+HB = pl.BlockSpec(memory_space=pltpu.HBM)
+
+
+def in_hbm(value):
+    return pltpu.with_memory_space_constraint(value, pltpu.HBM)
+
+
+def around(pieces):
+    got = [pieces[0]] + [None] * (NX - 1)
+    for d in (2, 1, 3):
+        got[d] = shifted(pieces[d], X, d)
+    return got
 
 
 def sweep(sources, front_inv, pattern, tree, lift, spread, couple, sep_inv, inflow):
@@ -390,10 +394,10 @@
             pltpu.VMEM((BND, BND), F32),
             pltpu.SemaphoreType.DMA((3 + 2 * NB,)),
         ],
-        compiler_params=FULL,
+        compiler_params=ROOM,
         cost_estimate=cost(2 * 128 * 512 * 256 * 6, 1 << 21),
         name="start",
-    )(patt, sources, front_inv, couple, inflow)
+    )(patt, *[in_hbm(a) for a in (sources, front_inv, couple, inflow)])
     came = swapped(send, C)
     far_cols = swapped(own_cols, C)
 
@@ -429,38 +433,47 @@
             devices = lax.axis_size("slab")
             incoming = lax.ppermute(outgoing, "slab", [(i, i + 1) for i in range(devices - 1)])
             extra = (kmat, far_couple, incoming)
+        fetched = [
+            pltpu.VMEM((P_SIZE * BND, 2 * BND), F32),
+            pltpu.SMEM((P_SIZE,), jnp.int32),
+            pltpu.SemaphoreType.DMA((2,)),
+        ]
+        fetched = [] if beat else fetched
         pieces = pl.pallas_call(
             functools.partial(lift_kernel, beat),
-            in_specs=[SM, SM] + [VM] * (4 + len(extra)),
-            out_specs=[VM] * 3,
-            out_shape=[double, double, shape(4 * BND, BND)],
-            scratch_shapes=[pltpu.VMEM((2 * NX, BND, BND), F32)],
+            in_specs=[SM if beat else HB, SM, VM, VM, VM if beat else HB] + [VM] * (1 + len(extra)),
+            out_specs=[VM] * NX,
+            out_shape=[double] * NX,
+            scratch_shapes=[pltpu.VMEM((2 * NX, BND, BND), F32)] + fetched,
             compiler_params=ROOM,
             cost_estimate=cost(2 * 512 * 256 * 128 * 4, 3 << 19),
-        )(own_tree, far_tree, keep, came, own_lift, far_lift, *extra)
-        outer = beside(pieces[2], 1)
-        inner = beside(pieces[1] + outer[2 * BND :], 0)
-        near = (pieces[0] + outer[: 2 * BND]) + inner
+        )(
+            own_tree if beat else in_hbm(own_tree),
+            far_tree,
+            keep,
+            came,
+            own_lift if beat else in_hbm(own_lift),
+            far_lift,
+            *extra,
+        )
+        got = around(pieces)
+        near = (pieces[0] + got[1]) + (got[2] + got[3])
         mine = near + swapped(near, Z)
-        inner = jnp.concatenate([mine, beside(mine, 0)], axis=0)
-        outer = beside(inner, 1)
+        held = around([mine] * NX)
         sol = pl.pallas_call(
             sep_kernel,
-            in_specs=[VM] * 4,
+            in_specs=[VM] * (NX + 2),
             out_specs=VM,
             out_shape=block,
             compiler_params=ROOM,
             cost_estimate=cost(2 * 256 * 2048 * 128 * 4, 5 << 20),
-        )(inner, outer, own_sep, far_sep)
+        )(*held, own_sep, far_sep)
         other = swapped(sol, Z)
-        held = [None] * NX
-        for j, part in enumerate((sol, other)):
-            held[j] = jnp.concatenate([part, beside(part, 0)], axis=0)
-            held[2 + j] = beside(held[j], 1)
+        held = around([sol] * NX) + around([other] * NX)
         extra = (zvals,) if beat else (keep, came, own_cols, far_cols)
         answer = pl.pallas_call(
             functools.partial(spread_kernel, beat),
-            in_specs=[SM, SM] + [VM] * (NX + 2 + len(extra)),
+            in_specs=[SM, SM] + [VM] * (2 * NX + 2 + len(extra)),
             out_specs=[VM] * (2 - beat),
             out_shape=[double] if beat else [block] * 2,
             scratch_shapes=[pltpu.VMEM((2 * NX, BND, BND), F32)],

time: 151 us -> 128 us (0.85)
  the two profiles are of different devices: /device:TPU:65 before, /device:TPU:33 now
where the time goes in v2:
time: 128 us
  starting transfers between devices  75.2 us (59%)
  waiting for transfers between devices  31 us (24%)
  Pallas kernels  20.1 us (16%)
    ppermute x36, starting transfers between devices, shifted(): lax.ppermute(value, axis, [(i, (i + distance) % size) for i in range(size)])  72 us
    ppermute x36, waiting for transfers between devices, shifted(): lax.ppermute(value, axis, [(i, (i + distance) % size) for i in range(size)])  27.1 us
    pallas_call x2, Pallas kernels, sweep(): pl.pallas_call(functools.partial(bulk_kernel, step), grid=(1,), in_specs=...  4.89 us
    pallas_call x2, Pallas kernels, sweep(): pl.pallas_call(functools.partial(lift_kernel, beat), in_specs=[SM if beat...  4.12 us
    ppermute x1, waiting for transfers between devices, sweep(): lax.ppermute(outgoing, 'slab', [(i, i + 1) for i in range(devices - 1)])  3.9 us
    pallas_call x2, Pallas kernels, sweep(): pl.pallas_call(functools.partial(spread_kernel, beat), in_specs=[SM, SM]...  3.56 us
    ppermute x1, starting transfers between devices, sweep(): lax.ppermute(outgoing, 'slab', [(i, i + 1) for i in range(devices - 1)])  3.21 us
    pallas_call x2, Pallas kernels, sweep(): pl.pallas_call(sep_kernel, in_specs=[VM] * (NX + 2), out_specs=VM, out_sh...  3.03 us
  transfers between devices with their start and end apart: 37, of which 15 were waited for; matrix products, arithmetic and copies ran while one was open for 0% of the time, Pallas kernels for 11%

profile of v2, /device:TPU:33, one launch (start us, length us, event | category | flops | bytes accessed | tf_op | source)
XLA Modules:
  0.0 127.5 jit_solution(5408070551346013327)
XLA Ops:
  1.4 2.8 %start.1 = (f32[256,128]{1,0:T(8,128)S(1)}, f32[256,128]{1,0:T(8,128)S(1)}, f32[128,256]{1,0:T(8,128)S(1)}) custom-call(s32[4,16]{1,0:T(4,128)S(1)} %bitcast.25, f32[2,1,1024,128]{3,2,1,0:T(8,128)} %src_ref.5, f32[1,1024,512]{2,1,0:T(8,128)} %g_ref.1, f32[1,128,256]{2,1,0:T(8,128)} %couple_ref.1, f32[1,128,128]{2,1,0:T(8,128)} %wave_ref.1), custom_call_target="tpu_custom_call" | custom-call | flops 201326592 | bytes 2097152 | tf_op jit(solution)/shard_map/start/pallas_call | solution.py:385
  5.9 2.3 %shard_map.91 = (f32[256,128]{1,0:T(8,128)S(1)}, f32[256,128]{1,0:T(8,128)S(1)}, f32[256,128]{1,0:T(8,128)S(1)}, f32[256,128]{1,0:T(8,128)S(1)}) custom-call(s32[4]{0:T(128)} %bitcast.28, s32[4]{0:T(128)S(1)} %collective-permute-done.far_tree, f32[256,128]{1,0:T(8,128)S(1)} %get-tuple-element.24.keep_ref.refs_8_, ...), custom_call_target="tpu_custom_call" | custom-call | flops 134217728 | bytes 1572864 | tf_op jit(solution)/shard_map/pallas_call | solution.py:442
  9.5 2.5 %collective-permute-start.6 = (f32[256,128]{1,0:T(8,128)S(1)}, f32[256,128]{1,0:T(8,128)S(1)}, u32[]{:S(2)}, u32[]{:S(2)}) collective-permute-start(f32[256,128]{1,0:T(8,128)S(1)} %get-tuple-element.28), channel_id=1, source_target_pairs={{0,8},{4,12},{8,0},{12,4},{1,9},{5,13},{9,1},{13,5},{2,10},{6,14},... | collective-permute-start | bytes 393224 | tf_op jit(solution)/shard_map/ppermute | solution.py:352
  14.4 3.8 %collective-permute-done.6 = f32[256,128]{1,0:T(8,128)S(1)} collective-permute-done((f32[256,128]{1,0:T(8,128)S(1)}, f32[256,128]{1,0:T(8,128)S(1)}, u32[]{:S(2)}, u32[]{:S(2)}) %collective-permute-start.6) | collective-permute-done | bytes 131104 | tf_op jit(solution)/shard_map/ppermute | solution.py:352
  18.2 6.1 %collective-permute-start.8 = (f32[256,128]{1,0:T(8,128)S(1)}, f32[256,128]{1,0:T(8,128)S(1)}, u32[]{:S(2)}, u32[]{:S(2)}) collective-permute-start(f32[256,128]{1,0:T(8,128)S(1)} %add_add_fusion.1), channel_id=1, source_target_pairs={{0,2},{2,0},{1,3},{3,1},{4,6},{6,4},{5,7},{7,5},{8,10},{10,8},{9,1... | collective-permute-start | bytes 393224 | tf_op jit(solution)/shard_map/ppermute | solution.py:352
  24.3 2.8 %collective-permute-done.8 = f32[256,128]{1,0:T(8,128)S(1)} collective-permute-done((f32[256,128]{1,0:T(8,128)S(1)}, f32[256,128]{1,0:T(8,128)S(1)}, u32[]{:S(2)}, u32[]{:S(2)}) %collective-permute-start.8) | collective-permute-done | bytes 131104 | tf_op jit(solution)/shard_map/ppermute | solution.py:352
  27.2 1.7 %collective-permute-start.10 = (f32[256,128]{1,0:T(8,128)S(1)}, f32[256,128]{1,0:T(8,128)S(1)}, u32[]{:S(2)}, u32[]{:S(2)}) collective-permute-start(f32[256,128]{1,0:T(8,128)S(1)} %add.27.refs_0_), channel_id=1, source_target_pairs={{0,8},{4,12},{8,0},{12,4},{1,9},{5,13},{9,1},{13,5},{2,10},{6,14},... | collective-permute-start | bytes 393224 | tf_op jit(solution)/shard_map/ppermute | solution.py:352
  28.9 1.6 %collective-permute-start.11 = (f32[256,128]{1,0:T(8,128)S(1)}, f32[256,128]{1,0:T(8,128)S(1)}, u32[]{:S(2)}, u32[]{:S(2)}) collective-permute-start(f32[256,128]{1,0:T(8,128)S(1)} %add.27.refs_0_), channel_id=1, source_target_pairs={{0,12},{4,0},{8,4},{12,8},{1,13},{5,1},{9,5},{13,9},{2,14},{6,2},{... | collective-permute-start | bytes 393224 | tf_op jit(solution)/shard_map/ppermute | solution.py:352
  30.4 2.1 %collective-permute-done.10.refs_2_ = f32[256,128]{1,0:T(8,128)S(1)} collective-permute-done((f32[256,128]{1,0:T(8,128)S(1)}, f32[256,128]{1,0:T(8,128)S(1)}, u32[]{:S(2)}, u32[]{:S(2)}) %collective-permute-start.10) | collective-permute-done | bytes 131104 | tf_op jit(solution)/shard_map/ppermute | solution.py:352
  32.6 5.6 %collective-permute-start.20 = (f32[128,256]{1,0:T(8,128)S(1)}, f32[128,256]{1,0:T(8,128)S(1)}, u32[]{:S(2)}, u32[]{:S(2)}) collective-permute-start(f32[128,256]{1,0:T(8,128)S(1)} %get-tuple-element.30.refs_10_), channel_id=1, source_target_pairs={{0,1},{1,0},{2,3},{3,2},{4,5},{5,4},{6,7},{7,6},{8,9},{9,8},{10,11... | collective-permute-start | bytes 393224 | tf_op jit(solution)/shard_map/ppermute | solution.py:352
  39.8 5.5 %collective-permute-start.16 = (f32[128,128]{1,0:T(8,128)S(1)}, f32[128,128]{1,0:T(8,128)S(1)}, u32[]{:S(2)}, u32[]{:S(2)}) collective-permute-start(f32[128,128]{1,0:T(8,128)S(1)} %shard_map.92.refs_0_), channel_id=1, source_target_pairs={{0,2},{2,0},{1,3},{3,1},{4,6},{6,4},{5,7},{7,5},{8,10},{10,8},{9,1... | collective-permute-start | bytes 196616 | tf_op jit(solution)/shard_map/ppermute | solution.py:352
  46.3 2.0 %collective-permute-start.14 = (f32[128,128]{1,0:T(8,128)S(1)}, f32[128,128]{1,0:T(8,128)S(1)}, u32[]{:S(2)}, u32[]{:S(2)}) collective-permute-start(f32[128,128]{1,0:T(8,128)S(1)} %shard_map.92.refs_0_), channel_id=1, source_target_pairs={{0,8},{4,12},{8,0},{12,4},{1,9},{5,13},{9,1},{13,5},{2,10},{6,14},... | collective-permute-start | bytes 196616 | tf_op jit(solution)/shard_map/ppermute | solution.py:352
  52.4 5.6 %collective-permute-start.4 = (f32[128,256]{1,0:T(8,128)S(1)}, f32[128,256]{1,0:T(8,128)S(1)}, u32[]{:S(2)}, u32[]{:S(2)}) collective-permute-start(f32[128,256]{1,0:T(8,128)S(1)} %bitcast.23), channel_id=1, source_target_pairs={{0,1},{1,0},{2,3},{3,2},{4,5},{5,4},{6,7},{7,6},{8,9},{9,8},{10,11... | collective-permute-start | bytes 393224 | tf_op jit(solution)/shard_map/ppermute | solution.py:352
  58.0 2.0 %shard_map.93 = (f32[128,128]{1,0:T(8,128)S(1)}, f32[128,128]{1,0:T(8,128)S(1)}) custom-call(s32[4]{0:T(128)S(1)} %bitcast.30, s32[4]{0:T(128)S(1)} %collective-permute-done.far_tree, f32[128,1024]{1,0:T(8,128)S(1)} %bitcast.18, f32[128,1024]{1,0:T(8,128)S(1)} %collective-permute-done.1.far_mat, f32[128,128]{1,0:T(8,128)S(1)} %shard_map.92.refs_0_, ...), custom_call_target="tpu_custom_call" | custom-call | flops 134217728 | bytes 1572864 | tf_op jit(solution)/shard_map/pallas_call | solution.py:474
  60.0 3.2 %collective-permute-start.21 = (f32[128,128]{1,0:T(8,128)S(1)}, f32[128,128]{1,0:T(8,128)S(1)}, u32[]{:S(2)}, u32[]{:S(2)}) collective-permute-start(f32[128,128]{1,0:T(8,128)S(1)} %get-tuple-element.31), channel_id=1, source_target_pairs={{0,16},{16,32},{32,48},{48,64},{64,80},{80,96},{96,112},{112,128},... | collective-permute-start | bytes 196616 | tf_op jit(solution)/shard_map/ppermute | solution.py:434
  63.2 3.9 %collective-permute-done.21.refs_2_ = f32[128,128]{1,0:T(8,128)S(1)} collective-permute-done((f32[128,128]{1,0:T(8,128)S(1)}, f32[128,128]{1,0:T(8,128)S(1)}, u32[]{:S(2)}, u32[]{:S(2)}) %collective-permute-start.21) | collective-permute-done | bytes 65568 | tf_op jit(solution)/shard_map/ppermute | solution.py:434
  67.1 1.8 %shard_map.94 = (f32[256,128]{1,0:T(8,128)S(1)}, f32[256,128]{1,0:T(8,128)S(1)}, f32[256,128]{1,0:T(8,128)S(1)}, f32[256,128]{1,0:T(8,128)S(1)}) custom-call(s32[4]{0:T(128)S(1)} %bitcast.31, s32[4]{0:T(128)S(1)} %collective-permute-done.far_tree, f32[256,128]{1,0:T(8,128)S(1)} %get-tuple-element.24.keep_ref.refs_8_, ...), custom_call_target="tpu_custom_call" | custom-call | flops 134217728 | bytes 1572864 | tf_op jit(solution)/shard_map/pallas_call | solution.py:442
  69.5 1.6 %collective-permute-start.23 = (f32[256,128]{1,0:T(8,128)S(1)}, f32[256,128]{1,0:T(8,128)S(1)}, u32[]{:S(2)}, u32[]{:S(2)}) collective-permute-start(f32[256,128]{1,0:T(8,128)S(1)} %get-tuple-element.34), channel_id=1, source_target_pairs={{0,8},{4,12},{8,0},{12,4},{1,9},{5,13},{9,1},{13,5},{2,10},{6,14},... | collective-permute-start | bytes 393224 | tf_op jit(solution)/shard_map/ppermute | solution.py:352
  72.0 3.4 %collective-permute-done.22 = f32[256,128]{1,0:T(8,128)S(1)} collective-permute-done((f32[256,128]{1,0:T(8,128)S(1)}, f32[256,128]{1,0:T(8,128)S(1)}, u32[]{:S(2)}, u32[]{:S(2)}) %collective-permute-start.22) | collective-permute-done | bytes 131104 | tf_op jit(solution)/shard_map/ppermute | solution.py:352
  76.1 2.8 %collective-permute-start.25 = (f32[256,128]{1,0:T(8,128)S(1)}, f32[256,128]{1,0:T(8,128)S(1)}, u32[]{:S(2)}, u32[]{:S(2)}) collective-permute-start(f32[256,128]{1,0:T(8,128)S(1)} %add_add_fusion), channel_id=1, source_target_pairs={{0,2},{2,0},{1,3},{3,1},{4,6},{6,4},{5,7},{7,5},{8,10},{10,8},{9,1... | collective-permute-start | bytes 393224 | tf_op jit(solution)/shard_map/ppermute | solution.py:352
  78.9 6.4 %collective-permute-done.25 = f32[256,128]{1,0:T(8,128)S(1)} collective-permute-done((f32[256,128]{1,0:T(8,128)S(1)}, f32[256,128]{1,0:T(8,128)S(1)}, u32[]{:S(2)}, u32[]{:S(2)}) %collective-permute-start.25) | collective-permute-done | bytes 131104 | tf_op jit(solution)/shard_map/ppermute | solution.py:352
  85.7 3.3 %collective-permute-start.27 = (f32[256,128]{1,0:T(8,128)S(1)}, f32[256,128]{1,0:T(8,128)S(1)}, u32[]{:S(2)}, u32[]{:S(2)}) collective-permute-start(f32[256,128]{1,0:T(8,128)S(1)} %add.31.refs_0_), channel_id=1, source_target_pairs={{0,8},{4,12},{8,0},{12,4},{1,9},{5,13},{9,1},{13,5},{2,10},{6,14},... | collective-permute-start | bytes 393224 | tf_op jit(solution)/shard_map/ppermute | solution.py:352
  89.0 1.8 %collective-permute-done.26.refs_1_ = f32[256,128]{1,0:T(8,128)S(1)} collective-permute-done((f32[256,128]{1,0:T(8,128)S(1)}, f32[256,128]{1,0:T(8,128)S(1)}, u32[]{:S(2)}, u32[]{:S(2)}) %collective-permute-start.26) | collective-permute-done | bytes 131104 | tf_op jit(solution)/shard_map/ppermute | solution.py:352
  90.8 2.0 %collective-permute-done.27.refs_2_ = f32[256,128]{1,0:T(8,128)S(1)} collective-permute-done((f32[256,128]{1,0:T(8,128)S(1)}, f32[256,128]{1,0:T(8,128)S(1)}, u32[]{:S(2)}, u32[]{:S(2)}) %collective-permute-start.27) | collective-permute-done | bytes 131104 | tf_op jit(solution)/shard_map/ppermute | solution.py:352
  94.3 2.9 %collective-permute-start.32 = (f32[128,128]{1,0:T(8,128)S(1)}, f32[128,128]{1,0:T(8,128)S(1)}, u32[]{:S(2)}, u32[]{:S(2)}) collective-permute-start(f32[128,128]{1,0:T(8,128)S(1)} %shard_map.95.refs_0_), channel_id=1, source_target_pairs={{0,2},{2,0},{1,3},{3,1},{4,6},{6,4},{5,7},{7,5},{8,10},{10,8},{9,1... | collective-permute-start | bytes 196616 | tf_op jit(solution)/shard_map/ppermute | solution.py:352
  98.3 2.4 %collective-permute-start.30 = (f32[128,128]{1,0:T(8,128)S(1)}, f32[128,128]{1,0:T(8,128)S(1)}, u32[]{:S(2)}, u32[]{:S(2)}) collective-permute-start(f32[128,128]{1,0:T(8,128)S(1)} %shard_map.95.refs_0_), channel_id=1, source_target_pairs={{0,8},{4,12},{8,0},{12,4},{1,9},{5,13},{9,1},{13,5},{2,10},{6,14},... | collective-permute-start | bytes 196616 | tf_op jit(solution)/shard_map/ppermute | solution.py:352
  102.2 2.5 %collective-permute-start.34 = (f32[128,128]{1,0:T(8,128)S(1)}, f32[128,128]{1,0:T(8,128)S(1)}, u32[]{:S(2)}, u32[]{:S(2)}) collective-permute-start(f32[128,128]{1,0:T(8,128)S(1)} %collective-permute-done.32.refs_4_), channel_id=1, source_target_pairs={{0,8},{4,12},{8,0},{12,4},{1,9},{5,13},{9,1},{13,5},{2,10},{6,14},... | collective-permute-start | bytes 196616 | tf_op jit(solution)/shard_map/ppermute | solution.py:352
  107.8 1.6 %shard_map.96.own_ref = f32[256,128]{1,0:T(8,128)S(1)} custom-call(s32[4]{0:T(128)S(1)} %bitcast.32, s32[4]{0:T(128)S(1)} %collective-permute-done.far_tree, f32[128,1024]{1,0:T(8,128)S(1)} %bitcast.19, f32[128,1024]{1,0:T(8,128)S(1)} %collective-permute-done.1.far_mat, f32[128,128]{1,0:T(8,128)S(1)} %shard_map.95.refs_0_, ...), custom_call_target="tpu_custom_call" | custom-call | flops 134217728 | bytes 1572864 | tf_op jit(solution)/shard_map/pallas_call | solution.py:474
  109.4 11.3 %collective-permute-start.36 = (f32[256,128]{1,0:T(8,128)S(1)}, f32[256,128]{1,0:T(8,128)S(1)}, u32[]{:S(2)}, u32[]{:S(2)}) collective-permute-start(f32[256,128]{1,0:T(8,128)S(1)} %shard_map.96.own_ref), channel_id=1, source_target_pairs={{0,1},{1,0},{2,3},{3,2},{4,5},{5,4},{6,7},{7,6},{8,9},{9,8},{10,11... | collective-permute-start | bytes 393224 | tf_op jit(solution)/shard_map/ppermute | solution.py:352
  120.7 2.5 %shard_map.97 = (f32[512,128]{1,0:T(8,128)S(1)}, f32[512,128]{1,0:T(8,128)S(1)}, bf16[1024,256]{1,0:T(8,128)(2,1)S(1)}) custom-call(s32[4,16]{1,0:T(4,128)S(1)} %bitcast.26, f32[2,1,1024,128]{3,2,1,0:T(8,128)S(1)} %copy-done.1, f32[1024,512]{1,0:T(8,128)S(1)} %bitcast.12), custom_call_target="tpu_custom_call" | custom-call | flops 805306368 | bytes 3145728 | tf_op jit(solution)/shard_map/pallas_call | solution.py:406
  123.1 2.4 %shard_map.98 = (f32[512,128]{1,0:T(8,128)S(1)}, f32[512,128]{1,0:T(8,128)S(1)}, bf16[1024,256]{1,0:T(8,128)(2,1)S(1)}) custom-call(s32[4,16]{1,0:T(4,128)S(1)} %bitcast.27, f32[2,1,1024,128]{3,2,1,0:T(8,128)S(1)} %copy-done.1, f32[1024,512]{1,0:T(8,128)S(1)} %bitcast.13), custom_call_target="tpu_custom_call" | custom-call | flops 805306368 | bytes 3145728 | tf_op jit(solution)/shard_map/pallas_call | solution.py:406
  125.6 1.7 %field.1 = f32[2,1024,128]{2,1,0:T(8,128)} custom-call(f32[256,128]{1,0:T(8,128)S(1)} %shard_map.96.own_ref, f32[256,128]{1,0:T(8,128)S(1)} %collective-permute-done.36.came_ref, f32[512,128]{1,0:T(8,128)S(1)} %get-tuple-element.37.refs_0_, f32[512,128]{1,0:T(8,128)S(1)} %get-tuple-element.38.refs_1_, f32[512,128]{1,0:T(8,128)S(1)} %get-tuple-element.39.refs_2_, ...), custom_call_target="tpu_custom_call" | custom-call | flops 536870912 | bytes 3145728 | tf_op jit(solution)/shard_map/field/pallas_call | solution.py:485
  (76 shorter events, 23.3 us)
Async XLA Ops:
  0.0 38.2 %collective-permute-start.12 = (f32[128,4096]{1,0:T(8,128)}, f32[128,4096]{1,0:T(8,128)S(1)}, u32[]{:S(2)}, u32[]{:S(2)}) collective-permute-start(f32[128,4096]{1,0:T(8,128)} %bitcast.14), channel_id=1, source_target_pairs={{0,1},{1,0},{2,3},{3,2},{4,5},{5,4},{6,7},{7,6},{8,9},{9,8},{10,11... | collective-permute-start | bytes 6291464 | tf_op jit(solution)/shard_map/ppermute | solution.py:352
  0.7 5.2 %collective-permute-start.3 = (f32[512,256]{1,0:T(8,128)}, f32[512,256]{1,0:T(8,128)S(1)}, u32[]{:S(2)}, u32[]{:S(2)}) collective-permute-start(f32[512,256]{1,0:T(8,128)} %bitcast.20), channel_id=1, source_target_pairs={{0,1},{1,0},{2,3},{3,2},{4,5},{5,4},{6,7},{7,6},{8,9},{9,8},{10,11... | collective-permute-start | bytes 1572872 | tf_op jit(solution)/shard_map/ppermute | solution.py:352
  8.2 6.2 %collective-permute-start.5 = (f32[256,128]{1,0:T(8,128)S(1)}, f32[256,128]{1,0:T(8,128)S(1)}, u32[]{:S(2)}, u32[]{:S(2)}) collective-permute-start(f32[256,128]{1,0:T(8,128)S(1)} %get-tuple-element.27), channel_id=1, source_target_pairs={{0,4},{4,8},{8,12},{12,0},{1,5},{5,9},{9,13},{13,1},{2,6},{6,10},{... | collective-permute-start | bytes 393224 | tf_op jit(solution)/shard_map/ppermute | solution.py:352
  9.5 8.7 %collective-permute-start.6 = (f32[256,128]{1,0:T(8,128)S(1)}, f32[256,128]{1,0:T(8,128)S(1)}, u32[]{:S(2)}, u32[]{:S(2)}) collective-permute-start(f32[256,128]{1,0:T(8,128)S(1)} %get-tuple-element.28), channel_id=1, source_target_pairs={{0,8},{4,12},{8,0},{12,4},{1,9},{5,13},{9,1},{13,5},{2,10},{6,14},... | collective-permute-start | bytes 393224 | tf_op jit(solution)/shard_map/ppermute | solution.py:352
  12.0 6.2 %collective-permute-start.7 = (f32[256,128]{1,0:T(8,128)S(1)}, f32[256,128]{1,0:T(8,128)S(1)}, u32[]{:S(2)}, u32[]{:S(2)}) collective-permute-start(f32[256,128]{1,0:T(8,128)S(1)} %get-tuple-element.29), channel_id=1, source_target_pairs={{0,12},{4,0},{8,4},{12,8},{1,13},{5,1},{9,5},{13,9},{2,14},{6,2},{... | collective-permute-start | bytes 393224 | tf_op jit(solution)/shard_map/ppermute | solution.py:352
  13.1 36.8 %collective-permute-start.1 = (f32[128,1024]{1,0:T(8,128)S(1)}, f32[128,1024]{1,0:T(8,128)S(1)}, u32[]{:S(2)}, u32[]{:S(2)}) collective-permute-start(f32[128,1024]{1,0:T(8,128)S(1)} %bitcast.17), channel_id=1, source_target_pairs={{0,1},{1,0},{2,3},{3,2},{4,5},{5,4},{6,7},{7,6},{8,9},{9,8},{10,11... | collective-permute-start | bytes 1572872 | tf_op jit(solution)/shard_map/ppermute | solution.py:352
  18.2 8.9 %collective-permute-start.8 = (f32[256,128]{1,0:T(8,128)S(1)}, f32[256,128]{1,0:T(8,128)S(1)}, u32[]{:S(2)}, u32[]{:S(2)}) collective-permute-start(f32[256,128]{1,0:T(8,128)S(1)} %add_add_fusion.1), channel_id=1, source_target_pairs={{0,2},{2,0},{1,3},{3,1},{4,6},{6,4},{5,7},{7,5},{8,10},{10,8},{9,1... | collective-permute-start | bytes 393224 | tf_op jit(solution)/shard_map/ppermute | solution.py:352
  27.2 5.4 %collective-permute-start.10 = (f32[256,128]{1,0:T(8,128)S(1)}, f32[256,128]{1,0:T(8,128)S(1)}, u32[]{:S(2)}, u32[]{:S(2)}) collective-permute-start(f32[256,128]{1,0:T(8,128)S(1)} %add.27.refs_0_), channel_id=1, source_target_pairs={{0,8},{4,12},{8,0},{12,4},{1,9},{5,13},{9,1},{13,5},{2,10},{6,14},... | collective-permute-start | bytes 393224 | tf_op jit(solution)/shard_map/ppermute | solution.py:352
  28.9 9.3 %collective-permute-start.11 = (f32[256,128]{1,0:T(8,128)S(1)}, f32[256,128]{1,0:T(8,128)S(1)}, u32[]{:S(2)}, u32[]{:S(2)}) collective-permute-start(f32[256,128]{1,0:T(8,128)S(1)} %add.27.refs_0_), channel_id=1, source_target_pairs={{0,12},{4,0},{8,4},{12,8},{1,13},{5,1},{9,5},{13,9},{2,14},{6,2},{... | collective-permute-start | bytes 393224 | tf_op jit(solution)/shard_map/ppermute | solution.py:352
  30.4 7.8 %collective-permute-start.9 = (f32[256,128]{1,0:T(8,128)S(1)}, f32[256,128]{1,0:T(8,128)S(1)}, u32[]{:S(2)}, u32[]{:S(2)}) collective-permute-start(f32[256,128]{1,0:T(8,128)S(1)} %add.27.refs_0_), channel_id=1, source_target_pairs={{0,4},{4,8},{8,12},{12,0},{1,5},{5,9},{9,13},{13,1},{2,6},{6,10},{... | collective-permute-start | bytes 393224 | tf_op jit(solution)/shard_map/ppermute | solution.py:352
  32.6 15.8 %collective-permute-start.20 = (f32[128,256]{1,0:T(8,128)S(1)}, f32[128,256]{1,0:T(8,128)S(1)}, u32[]{:S(2)}, u32[]{:S(2)}) collective-permute-start(f32[128,256]{1,0:T(8,128)S(1)} %get-tuple-element.30.refs_10_), channel_id=1, source_target_pairs={{0,1},{1,0},{2,3},{3,2},{4,5},{5,4},{6,7},{7,6},{8,9},{9,8},{10,11... | collective-permute-start | bytes 393224 | tf_op jit(solution)/shard_map/ppermute | solution.py:352
  39.8 9.9 %collective-permute-start.16 = (f32[128,128]{1,0:T(8,128)S(1)}, f32[128,128]{1,0:T(8,128)S(1)}, u32[]{:S(2)}, u32[]{:S(2)}) collective-permute-start(f32[128,128]{1,0:T(8,128)S(1)} %shard_map.92.refs_0_), channel_id=1, source_target_pairs={{0,2},{2,0},{1,3},{3,1},{4,6},{6,4},{5,7},{7,5},{8,10},{10,8},{9,1... | collective-permute-start | bytes 196616 | tf_op jit(solution)/shard_map/ppermute | solution.py:352
  45.2 5.7 %collective-permute-start.13 = (f32[128,128]{1,0:T(8,128)S(1)}, f32[128,128]{1,0:T(8,128)S(1)}, u32[]{:S(2)}, u32[]{:S(2)}) collective-permute-start(f32[128,128]{1,0:T(8,128)S(1)} %shard_map.92.refs_0_), channel_id=1, source_target_pairs={{0,4},{4,8},{8,12},{12,0},{1,5},{5,9},{9,13},{13,1},{2,6},{6,10},{... | collective-permute-start | bytes 196616 | tf_op jit(solution)/shard_map/ppermute | solution.py:352
  46.3 6.1 %collective-permute-start.14 = (f32[128,128]{1,0:T(8,128)S(1)}, f32[128,128]{1,0:T(8,128)S(1)}, u32[]{:S(2)}, u32[]{:S(2)}) collective-permute-start(f32[128,128]{1,0:T(8,128)S(1)} %shard_map.92.refs_0_), channel_id=1, source_target_pairs={{0,8},{4,12},{8,0},{12,4},{1,9},{5,13},{9,1},{13,5},{2,10},{6,14},... | collective-permute-start | bytes 196616 | tf_op jit(solution)/shard_map/ppermute | solution.py:352
  48.4 9.6 %collective-permute-start.15 = (f32[128,128]{1,0:T(8,128)S(1)}, f32[128,128]{1,0:T(8,128)S(1)}, u32[]{:S(2)}, u32[]{:S(2)}) collective-permute-start(f32[128,128]{1,0:T(8,128)S(1)} %shard_map.92.refs_0_), channel_id=1, source_target_pairs={{0,12},{4,0},{8,4},{12,8},{1,13},{5,1},{9,5},{13,9},{2,14},{6,2},{... | collective-permute-start | bytes 196616 | tf_op jit(solution)/shard_map/ppermute | solution.py:352
  49.6 8.3 %collective-permute-start.17 = (f32[128,128]{1,0:T(8,128)S(1)}, f32[128,128]{1,0:T(8,128)S(1)}, u32[]{:S(2)}, u32[]{:S(2)}) collective-permute-start(f32[128,128]{1,0:T(8,128)S(1)} %collective-permute-done.16.refs_4_), channel_id=1, source_target_pairs={{0,4},{4,8},{8,12},{12,0},{1,5},{5,9},{9,13},{13,1},{2,6},{6,10},{... | collective-permute-start | bytes 196616 | tf_op jit(solution)/shard_map/ppermute | solution.py:352
  49.9 8.1 %collective-permute-start.18 = (f32[128,128]{1,0:T(8,128)S(1)}, f32[128,128]{1,0:T(8,128)S(1)}, u32[]{:S(2)}, u32[]{:S(2)}) collective-permute-start(f32[128,128]{1,0:T(8,128)S(1)} %collective-permute-done.16.refs_4_), channel_id=1, source_target_pairs={{0,8},{4,12},{8,0},{12,4},{1,9},{5,13},{9,1},{13,5},{2,10},{6,14},... | collective-permute-start | bytes 196616 | tf_op jit(solution)/shard_map/ppermute | solution.py:352
  50.9 7.1 %collective-permute-start.19 = (f32[128,128]{1,0:T(8,128)S(1)}, f32[128,128]{1,0:T(8,128)S(1)}, u32[]{:S(2)}, u32[]{:S(2)}) collective-permute-start(f32[128,128]{1,0:T(8,128)S(1)} %collective-permute-done.16.refs_4_), channel_id=1, source_target_pairs={{0,12},{4,0},{8,4},{12,8},{1,13},{5,1},{9,5},{13,9},{2,14},{6,2},{... | collective-permute-start | bytes 196616 | tf_op jit(solution)/shard_map/ppermute | solution.py:352
  52.4 10.8 %collective-permute-start.4 = (f32[128,256]{1,0:T(8,128)S(1)}, f32[128,256]{1,0:T(8,128)S(1)}, u32[]{:S(2)}, u32[]{:S(2)}) collective-permute-start(f32[128,256]{1,0:T(8,128)S(1)} %bitcast.23), channel_id=1, source_target_pairs={{0,1},{1,0},{2,3},{3,2},{4,5},{5,4},{6,7},{7,6},{8,9},{9,8},{10,11... | collective-permute-start | bytes 393224 | tf_op jit(solution)/shard_map/ppermute | solution.py:352
  60.0 7.1 %collective-permute-start.21 = (f32[128,128]{1,0:T(8,128)S(1)}, f32[128,128]{1,0:T(8,128)S(1)}, u32[]{:S(2)}, u32[]{:S(2)}) collective-permute-start(f32[128,128]{1,0:T(8,128)S(1)} %get-tuple-element.31), channel_id=1, source_target_pairs={{0,16},{16,32},{32,48},{48,64},{64,80},{80,96},{96,112},{112,128},... | collective-permute-start | bytes 196616 | tf_op jit(solution)/shard_map/ppermute | solution.py:434
  69.0 6.5 %collective-permute-start.22 = (f32[256,128]{1,0:T(8,128)S(1)}, f32[256,128]{1,0:T(8,128)S(1)}, u32[]{:S(2)}, u32[]{:S(2)}) collective-permute-start(f32[256,128]{1,0:T(8,128)S(1)} %get-tuple-element.33), channel_id=1, source_target_pairs={{0,4},{4,8},{8,12},{12,0},{1,5},{5,9},{9,13},{13,1},{2,6},{6,10},{... | collective-permute-start | bytes 393224 | tf_op jit(solution)/shard_map/ppermute | solution.py:352
  69.5 5.9 %collective-permute-start.23 = (f32[256,128]{1,0:T(8,128)S(1)}, f32[256,128]{1,0:T(8,128)S(1)}, u32[]{:S(2)}, u32[]{:S(2)}) collective-permute-start(f32[256,128]{1,0:T(8,128)S(1)} %get-tuple-element.34), channel_id=1, source_target_pairs={{0,8},{4,12},{8,0},{12,4},{1,9},{5,13},{9,1},{13,5},{2,10},{6,14},... | collective-permute-start | bytes 393224 | tf_op jit(solution)/shard_map/ppermute | solution.py:352
  71.2 4.9 %collective-permute-start.24 = (f32[256,128]{1,0:T(8,128)S(1)}, f32[256,128]{1,0:T(8,128)S(1)}, u32[]{:S(2)}, u32[]{:S(2)}) collective-permute-start(f32[256,128]{1,0:T(8,128)S(1)} %get-tuple-element.35), channel_id=1, source_target_pairs={{0,12},{4,0},{8,4},{12,8},{1,13},{5,1},{9,5},{13,9},{2,14},{6,2},{... | collective-permute-start | bytes 393224 | tf_op jit(solution)/shard_map/ppermute | solution.py:352
  76.1 9.2 %collective-permute-start.25 = (f32[256,128]{1,0:T(8,128)S(1)}, f32[256,128]{1,0:T(8,128)S(1)}, u32[]{:S(2)}, u32[]{:S(2)}) collective-permute-start(f32[256,128]{1,0:T(8,128)S(1)} %add_add_fusion), channel_id=1, source_target_pairs={{0,2},{2,0},{1,3},{3,1},{4,6},{6,4},{5,7},{7,5},{8,10},{10,8},{9,1... | collective-permute-start | bytes 393224 | tf_op jit(solution)/shard_map/ppermute | solution.py:352
  85.4 5.4 %collective-permute-start.26 = (f32[256,128]{1,0:T(8,128)S(1)}, f32[256,128]{1,0:T(8,128)S(1)}, u32[]{:S(2)}, u32[]{:S(2)}) collective-permute-start(f32[256,128]{1,0:T(8,128)S(1)} %add.31.refs_0_), channel_id=1, source_target_pairs={{0,4},{4,8},{8,12},{12,0},{1,5},{5,9},{9,13},{13,1},{2,6},{6,10},{... | collective-permute-start | bytes 393224 | tf_op jit(solution)/shard_map/ppermute | solution.py:352
  85.7 7.0 %collective-permute-start.27 = (f32[256,128]{1,0:T(8,128)S(1)}, f32[256,128]{1,0:T(8,128)S(1)}, u32[]{:S(2)}, u32[]{:S(2)}) collective-permute-start(f32[256,128]{1,0:T(8,128)S(1)} %add.31.refs_0_), channel_id=1, source_target_pairs={{0,8},{4,12},{8,0},{12,4},{1,9},{5,13},{9,1},{13,5},{2,10},{6,14},... | collective-permute-start | bytes 393224 | tf_op jit(solution)/shard_map/ppermute | solution.py:352
  94.3 7.2 %collective-permute-start.32 = (f32[128,128]{1,0:T(8,128)S(1)}, f32[128,128]{1,0:T(8,128)S(1)}, u32[]{:S(2)}, u32[]{:S(2)}) collective-permute-start(f32[128,128]{1,0:T(8,128)S(1)} %shard_map.95.refs_0_), channel_id=1, source_target_pairs={{0,2},{2,0},{1,3},{3,1},{4,6},{6,4},{5,7},{7,5},{8,10},{10,8},{9,1... | collective-permute-start | bytes 196616 | tf_op jit(solution)/shard_map/ppermute | solution.py:352
  97.2 7.5 %collective-permute-start.29 = (f32[128,128]{1,0:T(8,128)S(1)}, f32[128,128]{1,0:T(8,128)S(1)}, u32[]{:S(2)}, u32[]{:S(2)}) collective-permute-start(f32[128,128]{1,0:T(8,128)S(1)} %shard_map.95.refs_0_), channel_id=1, source_target_pairs={{0,4},{4,8},{8,12},{12,0},{1,5},{5,9},{9,13},{13,1},{2,6},{6,10},{... | collective-permute-start | bytes 196616 | tf_op jit(solution)/shard_map/ppermute | solution.py:352
  98.3 6.8 %collective-permute-start.30 = (f32[128,128]{1,0:T(8,128)S(1)}, f32[128,128]{1,0:T(8,128)S(1)}, u32[]{:S(2)}, u32[]{:S(2)}) collective-permute-start(f32[128,128]{1,0:T(8,128)S(1)} %shard_map.95.refs_0_), channel_id=1, source_target_pairs={{0,8},{4,12},{8,0},{12,4},{1,9},{5,13},{9,1},{13,5},{2,10},{6,14},... | collective-permute-start | bytes 196616 | tf_op jit(solution)/shard_map/ppermute | solution.py:352
  100.7 4.3 %collective-permute-start.31 = (f32[128,128]{1,0:T(8,128)S(1)}, f32[128,128]{1,0:T(8,128)S(1)}, u32[]{:S(2)}, u32[]{:S(2)}) collective-permute-start(f32[128,128]{1,0:T(8,128)S(1)} %shard_map.95.refs_0_), channel_id=1, source_target_pairs={{0,12},{4,0},{8,4},{12,8},{1,13},{5,1},{9,5},{13,9},{2,14},{6,2},{... | collective-permute-start | bytes 196616 | tf_op jit(solution)/shard_map/ppermute | solution.py:352
  102.2 4.9 %collective-permute-start.34 = (f32[128,128]{1,0:T(8,128)S(1)}, f32[128,128]{1,0:T(8,128)S(1)}, u32[]{:S(2)}, u32[]{:S(2)}) collective-permute-start(f32[128,128]{1,0:T(8,128)S(1)} %collective-permute-done.32.refs_4_), channel_id=1, source_target_pairs={{0,8},{4,12},{8,0},{12,4},{1,9},{5,13},{9,1},{13,5},{2,10},{6,14},... | collective-permute-start | bytes 196616 | tf_op jit(solution)/shard_map/ppermute | solution.py:352
  109.4 16.2 %collective-permute-start.36 = (f32[256,128]{1,0:T(8,128)S(1)}, f32[256,128]{1,0:T(8,128)S(1)}, u32[]{:S(2)}, u32[]{:S(2)}) collective-permute-start(f32[256,128]{1,0:T(8,128)S(1)} %shard_map.96.own_ref), channel_id=1, source_target_pairs={{0,1},{1,0},{2,3},{3,2},{4,5},{5,4},{6,7},{7,6},{8,9},{9,8},{10,11... | collective-permute-start | bytes 393224 | tf_op jit(solution)/shard_map/ppermute | solution.py:352
  (15 other events, 246.7 us)

commit v3 on v2

--- a/solution.py
+++ b/solution.py
@@ -135,7 +135,7 @@
 
 
 def start_kernel(
-    patt_ref, src_ref, g_ref, couple_ref, wave_ref, keep_ref, send_ref, cols_ref, blocks, held, couple, wave, sems
+    patt_ref, src_ref, g_ref, couple_ref, wave_ref, lift_ref, keep_ref, send_ref, cols_ref, lift_out, blocks, held, couple, wave, sems
 ):
     copies = [
         pltpu.make_async_copy(g_ref.at[0, pl.ds(LEAF - BND, BND), :], held, sems.at[0]),
@@ -149,7 +149,8 @@
             copies.append(
                 pltpu.make_async_copy(src_ref.at[:, 0, at, :], blocks.at[n], sems.at[3 + n])
             )
-    for copy in copies:
+    late = pltpu.make_async_copy(lift_ref, lift_out, sems.at[3 + 2 * NB])
+    for copy in copies + [late]:
         copy.start()
     for copy in copies[1:3]:
         copy.wait()
@@ -172,21 +173,19 @@
     c = lax.axis_index(C)
     for out, which in ((keep_ref, c), (send_ref, 1 - c)):
         out[:BND] = pair_of(half_of(drive, which), half_of(y0, which))
-        later = half_of(y1, which)
+        later = half_of(y1, 1 - which)
         out[BND:] = pair_of(later, later)
+    late.wait()
 
 
 def lift_kernel(beat, own_tree, far_tree, keep_ref, came_ref, own_lift, far_lift, *refs):
     copies = ()
     if beat == 0:
-        *refs, lift_here, tree_here, sems = refs
-        copies = (
-            pltpu.make_async_copy(own_lift, lift_here, sems.at[0]),
-            pltpu.make_async_copy(own_tree, tree_here, sems.at[1]),
-        )
+        *refs, tree_here, sem = refs
+        copies = (pltpu.make_async_copy(own_tree, tree_here, sem),)
         for copy in copies:
             copy.start()
-        own_lift, own_tree = lift_here, tree_here
+        own_tree = tree_here
     acc = refs[-1]
     outs = refs[-1 - NX : -1]
     x = lax.axis_index(X)
@@ -197,13 +196,12 @@
         own_couple, far_couple, wave_ref = refs[:3]
         wave = wave_ref[...]
         drives = (
-            applied(own_couple[...], wave) - keep_ref[BND:],
-            applied(far_couple[...], to_first(wave)) - came_ref[BND:],
+            applied(own_couple[...], to_first(wave)) - keep_ref[BND:],
+            applied(far_couple[...], wave) - came_ref[BND:],
         )
-    far_part = applied(far_lift[...], drives[1])
+    parts = [applied(own_lift[...], drives[0]), applied(far_lift[...], drives[1])]
     for copy in copies:
         copy.wait()
-    parts = [applied(own_lift[...], drives[0]), far_part]
     first = is_first(parts[0][:BND]).astype(jnp.int32)
     for tree, part in zip((own_tree, far_tree), parts):
         for p in range(P_SIZE):
@@ -314,7 +312,7 @@
         came = came_ref[beat * BND : (beat + 1) * BND]
         first = is_first(own)
         z = jnp.where(
-            lax.axis_index(C) == 0,
+            lax.axis_index(C) == beat,
             jnp.where(first, own, came),
             jnp.where(first, to_first(came), to_second(own)),
         )
@@ -372,32 +370,32 @@
 
 def sweep(sources, front_inv, pattern, tree, lift, spread, couple, sep_inv, inflow):
     gmat, own_tree, patt = front_inv[0], tree[0, 0], pattern[0].T
-    own_lift, own_spread, kmat, own_sep = lift[0], spread[0], couple[0], sep_inv[0]
+    own_spread, kmat, own_sep = spread[0], couple[0], sep_inv[0]
     whole = lambda *dims: pl.BlockSpec(dims, lambda *i: (0,) * len(dims))
     block, double = shape(BND, BND), shape(2 * BND, BND)
 
     far_tree = swapped(own_tree, C)
-    far_lift = swapped(own_lift, C)
+    far_lift = swapped(lift[0], C)
     far_sep = swapped(own_sep, C)
     far_spread = swapped(own_spread, C)
     far_couple = swapped(kmat, C)
 
-    keep, send, own_cols = pl.pallas_call(
+    keep, send, own_cols, own_lift = pl.pallas_call(
         start_kernel,
-        in_specs=[SM, HB, HB, HB, HB],
-        out_specs=[VM, VM, VM],
-        out_shape=[double, double, shape(BND, 2 * BND)],
+        in_specs=[SM, HB, HB, HB, HB, HB],
+        out_specs=[VM, VM, VM, VM],
+        out_shape=[double, double, shape(BND, 2 * BND), shape(P_SIZE * BND, 2 * BND)],
         scratch_shapes=[
             pltpu.VMEM((2 * NB, 2, BLK, BND), F32),
             pltpu.VMEM((BND, NB * 2 * BLK), F32),
             pltpu.VMEM((BND, 2 * BND), F32),
             pltpu.VMEM((BND, BND), F32),
-            pltpu.SemaphoreType.DMA((3 + 2 * NB,)),
+            pltpu.SemaphoreType.DMA((4 + 2 * NB,)),
         ],
         compiler_params=ROOM,
         cost_estimate=cost(2 * 128 * 512 * 256 * 6, 1 << 21),
         name="start",
-    )(patt, *[in_hbm(a) for a in (sources, front_inv, couple, inflow)])
+    )(patt, *[in_hbm(a) for a in (sources, front_inv, couple, inflow, lift[0])])
     came = swapped(send, C)
     far_cols = swapped(own_cols, C)
 
@@ -431,17 +429,17 @@
         extra = ()
         if beat:
             devices = lax.axis_size("slab")
-            incoming = lax.ppermute(outgoing, "slab", [(i, i + 1) for i in range(devices - 1)])
+            route = [(2 * i + c, 2 * i + 3 - c) for i in range(devices - 1) for c in range(2)]
+            incoming = lax.ppermute(outgoing, ("slab", C), route)
             extra = (kmat, far_couple, incoming)
         fetched = [
-            pltpu.VMEM((P_SIZE * BND, 2 * BND), F32),
             pltpu.SMEM((P_SIZE,), jnp.int32),
-            pltpu.SemaphoreType.DMA((2,)),
+            pltpu.SemaphoreType.DMA,
         ]
         fetched = [] if beat else fetched
         pieces = pl.pallas_call(
             functools.partial(lift_kernel, beat),
-            in_specs=[SM if beat else HB, SM, VM, VM, VM if beat else HB] + [VM] * (1 + len(extra)),
+            in_specs=[SM if beat else HB, SM] + [VM] * (4 + len(extra)),
             out_specs=[VM] * NX,
             out_shape=[double] * NX,
             scratch_shapes=[pltpu.VMEM((2 * NX, BND, BND), F32)] + fetched,
@@ -452,7 +450,7 @@
             far_tree,
             keep,
             came,
-            own_lift if beat else in_hbm(own_lift),
+            own_lift,
             far_lift,
             *extra,
         )

time: 128 us -> 130 us (1.016)
  the two profiles are of different devices: /device:TPU:33 before, /device:TPU:39 now
where the time goes in v3:
time: 130 us
  starting transfers between devices  70 us (54%)
  waiting for transfers between devices  38.9 us (30%)
  Pallas kernels  19.5 us (15%)
    ppermute x36, starting transfers between devices, shifted(): lax.ppermute(value, axis, [(i, (i + distance) % size) for i in range(size)])  62.6 us
    ppermute x36, waiting for transfers between devices, shifted(): lax.ppermute(value, axis, [(i, (i + distance) % size) for i in range(size)])  35.7 us
    ppermute x1, starting transfers between devices, sweep(): incoming = lax.ppermute(outgoing, ('slab', C), route)  7.42 us
    pallas_call x2, Pallas kernels, sweep(): pl.pallas_call(functools.partial(bulk_kernel, step), grid=(1,), in_specs=...  4.89 us
    pallas_call x2, Pallas kernels, sweep(): pl.pallas_call(functools.partial(lift_kernel, beat), in_specs=[SM if beat...  3.76 us
    pallas_call x2, Pallas kernels, sweep(): pl.pallas_call(functools.partial(spread_kernel, beat), in_specs=[SM, SM]...  3.55 us
    ppermute x1, waiting for transfers between devices, sweep(): incoming = lax.ppermute(outgoing, ('slab', C), route)  3.14 us
    pallas_call x2, Pallas kernels, sweep(): pl.pallas_call(sep_kernel, in_specs=[VM] * (NX + 2), out_specs=VM, out_sh...  3.03 us
  transfers between devices with their start and end apart: 37, of which 19 were waited for; matrix products, arithmetic and copies ran while one was open for 0% of the time, Pallas kernels for 10%

profile of v3, /device:TPU:39, one launch (start us, length us, event | category | flops | bytes accessed | tf_op | source)
XLA Modules:
  0.0 129.6 jit_solution(6767243942292786447)
XLA Ops:
  1.4 2.6 %start.1 = (f32[256,128]{1,0:T(8,128)S(1)}, f32[256,128]{1,0:T(8,128)S(1)}, f32[128,256]{1,0:T(8,128)S(1)}, f32[512,256]{1,0:T(8,128)S(1)}) custom-call(s32[4,16]{1,0:T(4,128)S(1)} %bitcast.22, f32[2,1,1024,128]{3,2,1,0:T(8,128)} %src_ref.5, f32[1,1024,512]{2,1,0:T(8,128)} %g_ref.1, f32[1,128,256]{2,1,0:T(8,128)} %couple_ref.1, f32[1,128,128]{2,1,0:T(8,128)} %wave_ref.1, ...), custom_call_target="tpu_custom_call" | custom-call | flops 201326592 | bytes 2097152 | tf_op jit(solution)/shard_map/start/pallas_call | solution.py:383
  5.7 1.9 %shard_map.91 = (f32[256,128]{1,0:T(8,128)S(1)}, f32[256,128]{1,0:T(8,128)S(1)}, f32[256,128]{1,0:T(8,128)S(1)}, f32[256,128]{1,0:T(8,128)S(1)}) custom-call(s32[4]{0:T(128)} %bitcast.25, s32[4]{0:T(128)S(1)} %collective-permute-done.far_tree, f32[256,128]{1,0:T(8,128)S(1)} %get-tuple-element.25.keep_ref.refs_8_, ...), custom_call_target="tpu_custom_call" | custom-call | flops 134217728 | bytes 1572864 | tf_op jit(solution)/shard_map/pallas_call | solution.py:440
  7.9 2.1 %collective-permute-start.6 = (f32[256,128]{1,0:T(8,128)S(1)}, f32[256,128]{1,0:T(8,128)S(1)}, u32[]{:S(2)}, u32[]{:S(2)}) collective-permute-start(f32[256,128]{1,0:T(8,128)S(1)} %get-tuple-element.30), channel_id=1, source_target_pairs={{0,8},{4,12},{8,0},{12,4},{1,9},{5,13},{9,1},{13,5},{2,10},{6,14},... | collective-permute-start | bytes 393224 | tf_op jit(solution)/shard_map/ppermute | solution.py:350
  10.8 1.6 %collective-permute-done.5 = f32[256,128]{1,0:T(8,128)S(1)} collective-permute-done((f32[256,128]{1,0:T(8,128)S(1)}, f32[256,128]{1,0:T(8,128)S(1)}, u32[]{:S(2)}, u32[]{:S(2)}) %collective-permute-start.5) | collective-permute-done | bytes 131104 | tf_op jit(solution)/shard_map/ppermute | solution.py:350
  13.9 3.2 %collective-permute-done.7 = f32[256,128]{1,0:T(8,128)S(1)} collective-permute-done((f32[256,128]{1,0:T(8,128)S(1)}, f32[256,128]{1,0:T(8,128)S(1)}, u32[]{:S(2)}, u32[]{:S(2)}) %collective-permute-start.7) | collective-permute-done | bytes 131104 | tf_op jit(solution)/shard_map/ppermute | solution.py:350
  17.1 6.1 %collective-permute-start.8 = (f32[256,128]{1,0:T(8,128)S(1)}, f32[256,128]{1,0:T(8,128)S(1)}, u32[]{:S(2)}, u32[]{:S(2)}) collective-permute-start(f32[256,128]{1,0:T(8,128)S(1)} %add_add_fusion.1), channel_id=1, source_target_pairs={{0,2},{2,0},{1,3},{3,1},{4,6},{6,4},{5,7},{7,5},{8,10},{10,8},{9,1... | collective-permute-start | bytes 393224 | tf_op jit(solution)/shard_map/ppermute | solution.py:350
  23.2 2.8 %collective-permute-done.8 = f32[256,128]{1,0:T(8,128)S(1)} collective-permute-done((f32[256,128]{1,0:T(8,128)S(1)}, f32[256,128]{1,0:T(8,128)S(1)}, u32[]{:S(2)}, u32[]{:S(2)}) %collective-permute-start.8) | collective-permute-done | bytes 131104 | tf_op jit(solution)/shard_map/ppermute | solution.py:350
  27.3 2.7 %collective-permute-start.9 = (f32[256,128]{1,0:T(8,128)S(1)}, f32[256,128]{1,0:T(8,128)S(1)}, u32[]{:S(2)}, u32[]{:S(2)}) collective-permute-start(f32[256,128]{1,0:T(8,128)S(1)} %add.27.refs_0_), channel_id=1, source_target_pairs={{0,4},{4,8},{8,12},{12,0},{1,5},{5,9},{9,13},{13,1},{2,6},{6,10},{... | collective-permute-start | bytes 393224 | tf_op jit(solution)/shard_map/ppermute | solution.py:350
  31.5 5.6 %collective-permute-start.20 = (f32[128,256]{1,0:T(8,128)S(1)}, f32[128,256]{1,0:T(8,128)S(1)}, u32[]{:S(2)}, u32[]{:S(2)}) collective-permute-start(f32[128,256]{1,0:T(8,128)S(1)} %get-tuple-element.32.refs_10_), channel_id=1, source_target_pairs={{0,1},{1,0},{2,3},{3,2},{4,5},{5,4},{6,7},{7,6},{8,9},{9,8},{10,11... | collective-permute-start | bytes 393224 | tf_op jit(solution)/shard_map/ppermute | solution.py:350
  38.6 5.4 %collective-permute-start.16 = (f32[128,128]{1,0:T(8,128)S(1)}, f32[128,128]{1,0:T(8,128)S(1)}, u32[]{:S(2)}, u32[]{:S(2)}) collective-permute-start(f32[128,128]{1,0:T(8,128)S(1)} %shard_map.92.refs_0_), channel_id=1, source_target_pairs={{0,2},{2,0},{1,3},{3,1},{4,6},{6,4},{5,7},{7,5},{8,10},{10,8},{9,1... | collective-permute-start | bytes 196616 | tf_op jit(solution)/shard_map/ppermute | solution.py:350
  44.7 1.7 %collective-permute-start.14 = (f32[128,128]{1,0:T(8,128)S(1)}, f32[128,128]{1,0:T(8,128)S(1)}, u32[]{:S(2)}, u32[]{:S(2)}) collective-permute-start(f32[128,128]{1,0:T(8,128)S(1)} %shard_map.92.refs_0_), channel_id=1, source_target_pairs={{0,8},{4,12},{8,0},{12,4},{1,9},{5,13},{9,1},{13,5},{2,10},{6,14},... | collective-permute-start | bytes 196616 | tf_op jit(solution)/shard_map/ppermute | solution.py:350
  46.5 2.6 %collective-permute-start.17 = (f32[128,128]{1,0:T(8,128)S(1)}, f32[128,128]{1,0:T(8,128)S(1)}, u32[]{:S(2)}, u32[]{:S(2)}) collective-permute-start(f32[128,128]{1,0:T(8,128)S(1)} %collective-permute-done.16.refs_4_), channel_id=1, source_target_pairs={{0,4},{4,8},{8,12},{12,0},{1,5},{5,9},{9,13},{13,1},{2,6},{6,10},{... | collective-permute-start | bytes 196616 | tf_op jit(solution)/shard_map/ppermute | solution.py:350
  50.0 5.5 %collective-permute-start.4 = (f32[128,256]{1,0:T(8,128)S(1)}, f32[128,256]{1,0:T(8,128)S(1)}, u32[]{:S(2)}, u32[]{:S(2)}) collective-permute-start(f32[128,256]{1,0:T(8,128)S(1)} %bitcast.20), channel_id=1, source_target_pairs={{0,1},{1,0},{2,3},{3,2},{4,5},{5,4},{6,7},{7,6},{8,9},{9,8},{10,11... | collective-permute-start | bytes 393224 | tf_op jit(solution)/shard_map/ppermute | solution.py:350
  55.7 2.0 %shard_map.93 = (f32[128,128]{1,0:T(8,128)S(1)}, f32[128,128]{1,0:T(8,128)S(1)}) custom-call(s32[4]{0:T(128)S(1)} %bitcast.27, s32[4]{0:T(128)S(1)} %collective-permute-done.far_tree, f32[128,1024]{1,0:T(8,128)S(1)} %bitcast.18, f32[128,1024]{1,0:T(8,128)S(1)} %collective-permute-done.1.far_mat, f32[128,128]{1,0:T(8,128)S(1)} %shard_map.92.refs_0_, ...), custom_call_target="tpu_custom_call" | custom-call | flops 134217728 | bytes 1572864 | tf_op jit(solution)/shard_map/pallas_call | solution.py:472
  57.7 7.4 %collective-permute-start.21 = (f32[128,128]{1,0:T(8,128)S(1)}, f32[128,128]{1,0:T(8,128)S(1)}, u32[]{:S(2)}, u32[]{:S(2)}) collective-permute-start(f32[128,128]{1,0:T(8,128)S(1)} %get-tuple-element.33), channel_id=1, source_target_pairs={{0,17},{1,16},{16,33},{17,32},{32,49},{33,48},{48,65},{49,64},{64,... | collective-permute-start | bytes 196616 | tf_op jit(solution)/shard_map/ppermute | solution.py:433
  65.1 3.1 %collective-permute-done.21.refs_2_ = f32[128,128]{1,0:T(8,128)S(1)} collective-permute-done((f32[128,128]{1,0:T(8,128)S(1)}, f32[128,128]{1,0:T(8,128)S(1)}, u32[]{:S(2)}, u32[]{:S(2)}) %collective-permute-start.21) | collective-permute-done | bytes 65568 | tf_op jit(solution)/shard_map/ppermute | solution.py:433
  68.3 1.9 %shard_map.94 = (f32[256,128]{1,0:T(8,128)S(1)}, f32[256,128]{1,0:T(8,128)S(1)}, f32[256,128]{1,0:T(8,128)S(1)}, f32[256,128]{1,0:T(8,128)S(1)}) custom-call(s32[4]{0:T(128)S(1)} %bitcast.28, s32[4]{0:T(128)S(1)} %collective-permute-done.far_tree, f32[256,128]{1,0:T(8,128)S(1)} %get-tuple-element.25.keep_ref.refs_8_, ...), custom_call_target="tpu_custom_call" | custom-call | flops 134217728 | bytes 1572864 | tf_op jit(solution)/shard_map/pallas_call | solution.py:440
  71.7 2.3 %collective-permute-done.22 = f32[256,128]{1,0:T(8,128)S(1)} collective-permute-done((f32[256,128]{1,0:T(8,128)S(1)}, f32[256,128]{1,0:T(8,128)S(1)}, u32[]{:S(2)}, u32[]{:S(2)}) %collective-permute-start.22) | collective-permute-done | bytes 131104 | tf_op jit(solution)/shard_map/ppermute | solution.py:350
  74.1 2.1 %collective-permute-done.23 = f32[256,128]{1,0:T(8,128)S(1)} collective-permute-done((f32[256,128]{1,0:T(8,128)S(1)}, f32[256,128]{1,0:T(8,128)S(1)}, u32[]{:S(2)}, u32[]{:S(2)}) %collective-permute-start.23) | collective-permute-done | bytes 131104 | tf_op jit(solution)/shard_map/ppermute | solution.py:350
  76.2 3.4 %collective-permute-done.24 = f32[256,128]{1,0:T(8,128)S(1)} collective-permute-done((f32[256,128]{1,0:T(8,128)S(1)}, f32[256,128]{1,0:T(8,128)S(1)}, u32[]{:S(2)}, u32[]{:S(2)}) %collective-permute-start.24) | collective-permute-done | bytes 131104 | tf_op jit(solution)/shard_map/ppermute | solution.py:350
  79.6 5.7 %collective-permute-start.25 = (f32[256,128]{1,0:T(8,128)S(1)}, f32[256,128]{1,0:T(8,128)S(1)}, u32[]{:S(2)}, u32[]{:S(2)}) collective-permute-start(f32[256,128]{1,0:T(8,128)S(1)} %add_add_fusion), channel_id=1, source_target_pairs={{0,2},{2,0},{1,3},{3,1},{4,6},{6,4},{5,7},{7,5},{8,10},{10,8},{9,1... | collective-permute-start | bytes 393224 | tf_op jit(solution)/shard_map/ppermute | solution.py:350
  85.3 5.1 %collective-permute-done.25 = f32[256,128]{1,0:T(8,128)S(1)} collective-permute-done((f32[256,128]{1,0:T(8,128)S(1)}, f32[256,128]{1,0:T(8,128)S(1)}, u32[]{:S(2)}, u32[]{:S(2)}) %collective-permute-start.25) | collective-permute-done | bytes 131104 | tf_op jit(solution)/shard_map/ppermute | solution.py:350
  92.0 2.3 %collective-permute-done.26.refs_1_ = f32[256,128]{1,0:T(8,128)S(1)} collective-permute-done((f32[256,128]{1,0:T(8,128)S(1)}, f32[256,128]{1,0:T(8,128)S(1)}, u32[]{:S(2)}, u32[]{:S(2)}) %collective-permute-start.26) | collective-permute-done | bytes 131104 | tf_op jit(solution)/shard_map/ppermute | solution.py:350
  94.3 1.7 %collective-permute-done.27.refs_2_ = f32[256,128]{1,0:T(8,128)S(1)} collective-permute-done((f32[256,128]{1,0:T(8,128)S(1)}, f32[256,128]{1,0:T(8,128)S(1)}, u32[]{:S(2)}, u32[]{:S(2)}) %collective-permute-start.27) | collective-permute-done | bytes 131104 | tf_op jit(solution)/shard_map/ppermute | solution.py:350
  98.9 8.7 %collective-permute-start.32 = (f32[128,128]{1,0:T(8,128)S(1)}, f32[128,128]{1,0:T(8,128)S(1)}, u32[]{:S(2)}, u32[]{:S(2)}) collective-permute-start(f32[128,128]{1,0:T(8,128)S(1)} %shard_map.95.refs_0_), channel_id=1, source_target_pairs={{0,2},{2,0},{1,3},{3,1},{4,6},{6,4},{5,7},{7,5},{8,10},{10,8},{9,1... | collective-permute-start | bytes 196616 | tf_op jit(solution)/shard_map/ppermute | solution.py:350
  109.0 1.8 %collective-permute-done.32.refs_4_ = f32[128,128]{1,0:T(8,128)S(1)} collective-permute-done((f32[128,128]{1,0:T(8,128)S(1)}, f32[128,128]{1,0:T(8,128)S(1)}, u32[]{:S(2)}, u32[]{:S(2)}) %collective-permute-start.32) | collective-permute-done | bytes 65568 | tf_op jit(solution)/shard_map/ppermute | solution.py:350
  114.0 2.1 %collective-permute-done.34.refs_6_ = f32[128,128]{1,0:T(8,128)S(1)} collective-permute-done((f32[128,128]{1,0:T(8,128)S(1)}, f32[128,128]{1,0:T(8,128)S(1)}, u32[]{:S(2)}, u32[]{:S(2)}) %collective-permute-start.34) | collective-permute-done | bytes 65568 | tf_op jit(solution)/shard_map/ppermute | solution.py:350
  117.2 1.6 %shard_map.96.own_ref = f32[256,128]{1,0:T(8,128)S(1)} custom-call(s32[4]{0:T(128)S(1)} %bitcast.29, s32[4]{0:T(128)S(1)} %collective-permute-done.far_tree, f32[128,1024]{1,0:T(8,128)S(1)} %bitcast.19, f32[128,1024]{1,0:T(8,128)S(1)} %collective-permute-done.1.far_mat, f32[128,128]{1,0:T(8,128)S(1)} %shard_map.95.refs_0_, ...), custom_call_target="tpu_custom_call" | custom-call | flops 134217728 | bytes 1572864 | tf_op jit(solution)/shard_map/pallas_call | solution.py:472
  118.8 3.9 %collective-permute-start.36 = (f32[256,128]{1,0:T(8,128)S(1)}, f32[256,128]{1,0:T(8,128)S(1)}, u32[]{:S(2)}, u32[]{:S(2)}) collective-permute-start(f32[256,128]{1,0:T(8,128)S(1)} %shard_map.96.own_ref), channel_id=1, source_target_pairs={{0,1},{1,0},{2,3},{3,2},{4,5},{5,4},{6,7},{7,6},{8,9},{9,8},{10,11... | collective-permute-start | bytes 393224 | tf_op jit(solution)/shard_map/ppermute | solution.py:350
  122.8 2.4 %shard_map.97 = (f32[512,128]{1,0:T(8,128)S(1)}, f32[512,128]{1,0:T(8,128)S(1)}, bf16[1024,256]{1,0:T(8,128)(2,1)S(1)}) custom-call(s32[4,16]{1,0:T(4,128)S(1)} %bitcast.23, f32[2,1,1024,128]{3,2,1,0:T(8,128)S(1)} %copy-done.1, f32[1024,512]{1,0:T(8,128)S(1)} %bitcast.12), custom_call_target="tpu_custom_call" | custom-call | flops 805306368 | bytes 3145728 | tf_op jit(solution)/shard_map/pallas_call | solution.py:404
  125.2 2.4 %shard_map.98 = (f32[512,128]{1,0:T(8,128)S(1)}, f32[512,128]{1,0:T(8,128)S(1)}, bf16[1024,256]{1,0:T(8,128)(2,1)S(1)}) custom-call(s32[4,16]{1,0:T(4,128)S(1)} %bitcast.24, f32[2,1,1024,128]{3,2,1,0:T(8,128)S(1)} %copy-done.1, f32[1024,512]{1,0:T(8,128)S(1)} %bitcast.13), custom_call_target="tpu_custom_call" | custom-call | flops 805306368 | bytes 3145728 | tf_op jit(solution)/shard_map/pallas_call | solution.py:404
  127.7 1.7 %field.1 = f32[2,1024,128]{2,1,0:T(8,128)} custom-call(f32[256,128]{1,0:T(8,128)S(1)} %shard_map.96.own_ref, f32[256,128]{1,0:T(8,128)S(1)} %collective-permute-done.36.came_ref, f32[512,128]{1,0:T(8,128)S(1)} %get-tuple-element.39.refs_0_, f32[512,128]{1,0:T(8,128)S(1)} %get-tuple-element.40.refs_1_, f32[512,128]{1,0:T(8,128)S(1)} %get-tuple-element.41.refs_2_, ...), custom_call_target="tpu_custom_call" | custom-call | flops 536870912 | bytes 3145728 | tf_op jit(solution)/shard_map/field/pallas_call | solution.py:483
  (74 shorter events, 23.5 us)
Async XLA Ops:
  0.0 37.1 %collective-permute-start.12 = (f32[128,4096]{1,0:T(8,128)}, f32[128,4096]{1,0:T(8,128)S(1)}, u32[]{:S(2)}, u32[]{:S(2)}) collective-permute-start(f32[128,4096]{1,0:T(8,128)} %bitcast.14), channel_id=1, source_target_pairs={{0,1},{1,0},{2,3},{3,2},{4,5},{5,4},{6,7},{7,6},{8,9},{9,8},{10,11... | collective-permute-start | bytes 6291464 | tf_op jit(solution)/shard_map/ppermute | solution.py:350
  0.7 5.0 %collective-permute-start.3 = (f32[512,256]{1,0:T(8,128)}, f32[512,256]{1,0:T(8,128)S(1)}, u32[]{:S(2)}, u32[]{:S(2)}) collective-permute-start(f32[512,256]{1,0:T(8,128)} %bitcast.30), channel_id=1, source_target_pairs={{0,1},{1,0},{2,3},{3,2},{4,5},{5,4},{6,7},{7,6},{8,9},{9,8},{10,11... | collective-permute-start | bytes 1572872 | tf_op jit(solution)/shard_map/ppermute | solution.py:350
  7.6 4.9 %collective-permute-start.5 = (f32[256,128]{1,0:T(8,128)S(1)}, f32[256,128]{1,0:T(8,128)S(1)}, u32[]{:S(2)}, u32[]{:S(2)}) collective-permute-start(f32[256,128]{1,0:T(8,128)S(1)} %get-tuple-element.29), channel_id=1, source_target_pairs={{0,4},{4,8},{8,12},{12,0},{1,5},{5,9},{9,13},{13,1},{2,6},{6,10},{... | collective-permute-start | bytes 393224 | tf_op jit(solution)/shard_map/ppermute | solution.py:350
  7.9 6.0 %collective-permute-start.6 = (f32[256,128]{1,0:T(8,128)S(1)}, f32[256,128]{1,0:T(8,128)S(1)}, u32[]{:S(2)}, u32[]{:S(2)}) collective-permute-start(f32[256,128]{1,0:T(8,128)S(1)} %get-tuple-element.30), channel_id=1, source_target_pairs={{0,8},{4,12},{8,0},{12,4},{1,9},{5,13},{9,1},{13,5},{2,10},{6,14},... | collective-permute-start | bytes 393224 | tf_op jit(solution)/shard_map/ppermute | solution.py:350
  10.0 7.1 %collective-permute-start.7 = (f32[256,128]{1,0:T(8,128)S(1)}, f32[256,128]{1,0:T(8,128)S(1)}, u32[]{:S(2)}, u32[]{:S(2)}) collective-permute-start(f32[256,128]{1,0:T(8,128)S(1)} %get-tuple-element.31), channel_id=1, source_target_pairs={{0,12},{4,0},{8,4},{12,8},{1,13},{5,1},{9,5},{13,9},{2,14},{6,2},{... | collective-permute-start | bytes 393224 | tf_op jit(solution)/shard_map/ppermute | solution.py:350
  10.0 39.1 %collective-permute-start.1 = (f32[128,1024]{1,0:T(8,128)S(1)}, f32[128,1024]{1,0:T(8,128)S(1)}, u32[]{:S(2)}, u32[]{:S(2)}) collective-permute-start(f32[128,1024]{1,0:T(8,128)S(1)} %bitcast.17), channel_id=1, source_target_pairs={{0,1},{1,0},{2,3},{3,2},{4,5},{5,4},{6,7},{7,6},{8,9},{9,8},{10,11... | collective-permute-start | bytes 1572872 | tf_op jit(solution)/shard_map/ppermute | solution.py:350
  17.1 8.9 %collective-permute-start.8 = (f32[256,128]{1,0:T(8,128)S(1)}, f32[256,128]{1,0:T(8,128)S(1)}, u32[]{:S(2)}, u32[]{:S(2)}) collective-permute-start(f32[256,128]{1,0:T(8,128)S(1)} %add_add_fusion.1), channel_id=1, source_target_pairs={{0,2},{2,0},{1,3},{3,1},{4,6},{6,4},{5,7},{7,5},{8,10},{10,8},{9,1... | collective-permute-start | bytes 393224 | tf_op jit(solution)/shard_map/ppermute | solution.py:350
  26.0 5.5 %collective-permute-start.10 = (f32[256,128]{1,0:T(8,128)S(1)}, f32[256,128]{1,0:T(8,128)S(1)}, u32[]{:S(2)}, u32[]{:S(2)}) collective-permute-start(f32[256,128]{1,0:T(8,128)S(1)} %add.27.refs_0_), channel_id=1, source_target_pairs={{0,8},{4,12},{8,0},{12,4},{1,9},{5,13},{9,1},{13,5},{2,10},{6,14},... | collective-permute-start | bytes 393224 | tf_op jit(solution)/shard_map/ppermute | solution.py:350
  27.3 9.8 %collective-permute-start.11 = (f32[256,128]{1,0:T(8,128)S(1)}, f32[256,128]{1,0:T(8,128)S(1)}, u32[]{:S(2)}, u32[]{:S(2)}) collective-permute-start(f32[256,128]{1,0:T(8,128)S(1)} %add.27.refs_0_), channel_id=1, source_target_pairs={{0,12},{4,0},{8,4},{12,8},{1,13},{5,1},{9,5},{13,9},{2,14},{6,2},{... | collective-permute-start | bytes 393224 | tf_op jit(solution)/shard_map/ppermute | solution.py:350
  27.3 9.8 %collective-permute-start.9 = (f32[256,128]{1,0:T(8,128)S(1)}, f32[256,128]{1,0:T(8,128)S(1)}, u32[]{:S(2)}, u32[]{:S(2)}) collective-permute-start(f32[256,128]{1,0:T(8,128)S(1)} %add.27.refs_0_), channel_id=1, source_target_pairs={{0,4},{4,8},{8,12},{12,0},{1,5},{5,9},{9,13},{13,1},{2,6},{6,10},{... | collective-permute-start | bytes 393224 | tf_op jit(solution)/shard_map/ppermute | solution.py:350
  31.5 14.9 %collective-permute-start.20 = (f32[128,256]{1,0:T(8,128)S(1)}, f32[128,256]{1,0:T(8,128)S(1)}, u32[]{:S(2)}, u32[]{:S(2)}) collective-permute-start(f32[128,256]{1,0:T(8,128)S(1)} %get-tuple-element.32.refs_10_), channel_id=1, source_target_pairs={{0,1},{1,0},{2,3},{3,2},{4,5},{5,4},{6,7},{7,6},{8,9},{9,8},{10,11... | collective-permute-start | bytes 393224 | tf_op jit(solution)/shard_map/ppermute | solution.py:350
  38.6 7.9 %collective-permute-start.16 = (f32[128,128]{1,0:T(8,128)S(1)}, f32[128,128]{1,0:T(8,128)S(1)}, u32[]{:S(2)}, u32[]{:S(2)}) collective-permute-start(f32[128,128]{1,0:T(8,128)S(1)} %shard_map.92.refs_0_), channel_id=1, source_target_pairs={{0,2},{2,0},{1,3},{3,1},{4,6},{6,4},{5,7},{7,5},{8,10},{10,8},{9,1... | collective-permute-start | bytes 196616 | tf_op jit(solution)/shard_map/ppermute | solution.py:350
  44.1 5.1 %collective-permute-start.13 = (f32[128,128]{1,0:T(8,128)S(1)}, f32[128,128]{1,0:T(8,128)S(1)}, u32[]{:S(2)}, u32[]{:S(2)}) collective-permute-start(f32[128,128]{1,0:T(8,128)S(1)} %shard_map.92.refs_0_), channel_id=1, source_target_pairs={{0,4},{4,8},{8,12},{12,0},{1,5},{5,9},{9,13},{13,1},{2,6},{6,10},{... | collective-permute-start | bytes 196616 | tf_op jit(solution)/shard_map/ppermute | solution.py:350
  44.7 5.2 %collective-permute-start.14 = (f32[128,128]{1,0:T(8,128)S(1)}, f32[128,128]{1,0:T(8,128)S(1)}, u32[]{:S(2)}, u32[]{:S(2)}) collective-permute-start(f32[128,128]{1,0:T(8,128)S(1)} %shard_map.92.refs_0_), channel_id=1, source_target_pairs={{0,8},{4,12},{8,0},{12,4},{1,9},{5,13},{9,1},{13,5},{2,10},{6,14},... | collective-permute-start | bytes 196616 | tf_op jit(solution)/shard_map/ppermute | solution.py:350
  46.4 9.1 %collective-permute-start.15 = (f32[128,128]{1,0:T(8,128)S(1)}, f32[128,128]{1,0:T(8,128)S(1)}, u32[]{:S(2)}, u32[]{:S(2)}) collective-permute-start(f32[128,128]{1,0:T(8,128)S(1)} %shard_map.92.refs_0_), channel_id=1, source_target_pairs={{0,12},{4,0},{8,4},{12,8},{1,13},{5,1},{9,5},{13,9},{2,14},{6,2},{... | collective-permute-start | bytes 196616 | tf_op jit(solution)/shard_map/ppermute | solution.py:350
  46.5 9.0 %collective-permute-start.17 = (f32[128,128]{1,0:T(8,128)S(1)}, f32[128,128]{1,0:T(8,128)S(1)}, u32[]{:S(2)}, u32[]{:S(2)}) collective-permute-start(f32[128,128]{1,0:T(8,128)S(1)} %collective-permute-done.16.refs_4_), channel_id=1, source_target_pairs={{0,4},{4,8},{8,12},{12,0},{1,5},{5,9},{9,13},{13,1},{2,6},{6,10},{... | collective-permute-start | bytes 196616 | tf_op jit(solution)/shard_map/ppermute | solution.py:350
  49.1 6.4 %collective-permute-start.18 = (f32[128,128]{1,0:T(8,128)S(1)}, f32[128,128]{1,0:T(8,128)S(1)}, u32[]{:S(2)}, u32[]{:S(2)}) collective-permute-start(f32[128,128]{1,0:T(8,128)S(1)} %collective-permute-done.16.refs_4_), channel_id=1, source_target_pairs={{0,8},{4,12},{8,0},{12,4},{1,9},{5,13},{9,1},{13,5},{2,10},{6,14},... | collective-permute-start | bytes 196616 | tf_op jit(solution)/shard_map/ppermute | solution.py:350
  49.2 6.5 %collective-permute-start.19 = (f32[128,128]{1,0:T(8,128)S(1)}, f32[128,128]{1,0:T(8,128)S(1)}, u32[]{:S(2)}, u32[]{:S(2)}) collective-permute-start(f32[128,128]{1,0:T(8,128)S(1)} %collective-permute-done.16.refs_4_), channel_id=1, source_target_pairs={{0,12},{4,0},{8,4},{12,8},{1,13},{5,1},{9,5},{13,9},{2,14},{6,2},{... | collective-permute-start | bytes 196616 | tf_op jit(solution)/shard_map/ppermute | solution.py:350
  50.0 15.2 %collective-permute-start.4 = (f32[128,256]{1,0:T(8,128)S(1)}, f32[128,256]{1,0:T(8,128)S(1)}, u32[]{:S(2)}, u32[]{:S(2)}) collective-permute-start(f32[128,256]{1,0:T(8,128)S(1)} %bitcast.20), channel_id=1, source_target_pairs={{0,1},{1,0},{2,3},{3,2},{4,5},{5,4},{6,7},{7,6},{8,9},{9,8},{10,11... | collective-permute-start | bytes 393224 | tf_op jit(solution)/shard_map/ppermute | solution.py:350
  57.7 10.6 %collective-permute-start.21 = (f32[128,128]{1,0:T(8,128)S(1)}, f32[128,128]{1,0:T(8,128)S(1)}, u32[]{:S(2)}, u32[]{:S(2)}) collective-permute-start(f32[128,128]{1,0:T(8,128)S(1)} %get-tuple-element.33), channel_id=1, source_target_pairs={{0,17},{1,16},{16,33},{17,32},{32,49},{33,48},{48,65},{49,64},{64,... | collective-permute-start | bytes 196616 | tf_op jit(solution)/shard_map/ppermute | solution.py:433
  70.8 5.4 %collective-permute-start.23 = (f32[256,128]{1,0:T(8,128)S(1)}, f32[256,128]{1,0:T(8,128)S(1)}, u32[]{:S(2)}, u32[]{:S(2)}) collective-permute-start(f32[256,128]{1,0:T(8,128)S(1)} %get-tuple-element.36), channel_id=1, source_target_pairs={{0,8},{4,12},{8,0},{12,4},{1,9},{5,13},{9,1},{13,5},{2,10},{6,14},... | collective-permute-start | bytes 393224 | tf_op jit(solution)/shard_map/ppermute | solution.py:350
  71.3 8.3 %collective-permute-start.24 = (f32[256,128]{1,0:T(8,128)S(1)}, f32[256,128]{1,0:T(8,128)S(1)}, u32[]{:S(2)}, u32[]{:S(2)}) collective-permute-start(f32[256,128]{1,0:T(8,128)S(1)} %get-tuple-element.37), channel_id=1, source_target_pairs={{0,12},{4,0},{8,4},{12,8},{1,13},{5,1},{9,5},{13,9},{2,14},{6,2},{... | collective-permute-start | bytes 393224 | tf_op jit(solution)/shard_map/ppermute | solution.py:350
  79.6 10.8 %collective-permute-start.25 = (f32[256,128]{1,0:T(8,128)S(1)}, f32[256,128]{1,0:T(8,128)S(1)}, u32[]{:S(2)}, u32[]{:S(2)}) collective-permute-start(f32[256,128]{1,0:T(8,128)S(1)} %add_add_fusion), channel_id=1, source_target_pairs={{0,2},{2,0},{1,3},{3,1},{4,6},{6,4},{5,7},{7,5},{8,10},{10,8},{9,1... | collective-permute-start | bytes 393224 | tf_op jit(solution)/shard_map/ppermute | solution.py:350
  90.5 5.5 %collective-permute-start.27 = (f32[256,128]{1,0:T(8,128)S(1)}, f32[256,128]{1,0:T(8,128)S(1)}, u32[]{:S(2)}, u32[]{:S(2)}) collective-permute-start(f32[256,128]{1,0:T(8,128)S(1)} %add.31.refs_0_), channel_id=1, source_target_pairs={{0,8},{4,12},{8,0},{12,4},{1,9},{5,13},{9,1},{13,5},{2,10},{6,14},... | collective-permute-start | bytes 393224 | tf_op jit(solution)/shard_map/ppermute | solution.py:350
  90.6 6.7 %collective-permute-start.28 = (f32[256,128]{1,0:T(8,128)S(1)}, f32[256,128]{1,0:T(8,128)S(1)}, u32[]{:S(2)}, u32[]{:S(2)}) collective-permute-start(f32[256,128]{1,0:T(8,128)S(1)} %add.31.refs_0_), channel_id=1, source_target_pairs={{0,12},{4,0},{8,4},{12,8},{1,13},{5,1},{9,5},{13,9},{2,14},{6,2},{... | collective-permute-start | bytes 393224 | tf_op jit(solution)/shard_map/ppermute | solution.py:350
  98.9 12.0 %collective-permute-start.32 = (f32[128,128]{1,0:T(8,128)S(1)}, f32[128,128]{1,0:T(8,128)S(1)}, u32[]{:S(2)}, u32[]{:S(2)}) collective-permute-start(f32[128,128]{1,0:T(8,128)S(1)} %shard_map.95.refs_0_), channel_id=1, source_target_pairs={{0,2},{2,0},{1,3},{3,1},{4,6},{6,4},{5,7},{7,5},{8,10},{10,8},{9,1... | collective-permute-start | bytes 196616 | tf_op jit(solution)/shard_map/ppermute | solution.py:350
  107.5 5.1 %collective-permute-start.29 = (f32[128,128]{1,0:T(8,128)S(1)}, f32[128,128]{1,0:T(8,128)S(1)}, u32[]{:S(2)}, u32[]{:S(2)}) collective-permute-start(f32[128,128]{1,0:T(8,128)S(1)} %shard_map.95.refs_0_), channel_id=1, source_target_pairs={{0,4},{4,8},{8,12},{12,0},{1,5},{5,9},{9,13},{13,1},{2,6},{6,10},{... | collective-permute-start | bytes 196616 | tf_op jit(solution)/shard_map/ppermute | solution.py:350
  107.7 5.7 %collective-permute-start.30 = (f32[128,128]{1,0:T(8,128)S(1)}, f32[128,128]{1,0:T(8,128)S(1)}, u32[]{:S(2)}, u32[]{:S(2)}) collective-permute-start(f32[128,128]{1,0:T(8,128)S(1)} %shard_map.95.refs_0_), channel_id=1, source_target_pairs={{0,8},{4,12},{8,0},{12,4},{1,9},{5,13},{9,1},{13,5},{2,10},{6,14},... | collective-permute-start | bytes 196616 | tf_op jit(solution)/shard_map/ppermute | solution.py:350
  107.9 5.6 %collective-permute-start.31 = (f32[128,128]{1,0:T(8,128)S(1)}, f32[128,128]{1,0:T(8,128)S(1)}, u32[]{:S(2)}, u32[]{:S(2)}) collective-permute-start(f32[128,128]{1,0:T(8,128)S(1)} %shard_map.95.refs_0_), channel_id=1, source_target_pairs={{0,12},{4,0},{8,4},{12,8},{1,13},{5,1},{9,5},{13,9},{2,14},{6,2},{... | collective-permute-start | bytes 196616 | tf_op jit(solution)/shard_map/ppermute | solution.py:350
  111.4 4.7 %collective-permute-start.34 = (f32[128,128]{1,0:T(8,128)S(1)}, f32[128,128]{1,0:T(8,128)S(1)}, u32[]{:S(2)}, u32[]{:S(2)}) collective-permute-start(f32[128,128]{1,0:T(8,128)S(1)} %collective-permute-done.32.refs_4_), channel_id=1, source_target_pairs={{0,8},{4,12},{8,0},{12,4},{1,9},{5,13},{9,1},{13,5},{2,10},{6,14},... | collective-permute-start | bytes 196616 | tf_op jit(solution)/shard_map/ppermute | solution.py:350
  112.6 4.6 %collective-permute-start.35 = (f32[128,128]{1,0:T(8,128)S(1)}, f32[128,128]{1,0:T(8,128)S(1)}, u32[]{:S(2)}, u32[]{:S(2)}) collective-permute-start(f32[128,128]{1,0:T(8,128)S(1)} %collective-permute-done.32.refs_4_), channel_id=1, source_target_pairs={{0,12},{4,0},{8,4},{12,8},{1,13},{5,1},{9,5},{13,9},{2,14},{6,2},{... | collective-permute-start | bytes 196616 | tf_op jit(solution)/shard_map/ppermute | solution.py:350
  118.8 8.8 %collective-permute-start.36 = (f32[256,128]{1,0:T(8,128)S(1)}, f32[256,128]{1,0:T(8,128)S(1)}, u32[]{:S(2)}, u32[]{:S(2)}) collective-permute-start(f32[256,128]{1,0:T(8,128)S(1)} %shard_map.96.own_ref), channel_id=1, source_target_pairs={{0,1},{1,0},{2,3},{3,2},{4,5},{5,4},{6,7},{7,6},{8,9},{9,8},{10,11... | collective-permute-start | bytes 393224 | tf_op jit(solution)/shard_map/ppermute | solution.py:350
  (14 other events, 200.3 us)

commit v4 on v3

--- a/solution.py
+++ b/solution.py
@@ -173,7 +173,7 @@
     c = lax.axis_index(C)
     for out, which in ((keep_ref, c), (send_ref, 1 - c)):
         out[:BND] = pair_of(half_of(drive, which), half_of(y0, which))
-        later = half_of(y1, 1 - which)
+        later = half_of(y1, which)
         out[BND:] = pair_of(later, later)
     late.wait()
 
@@ -196,8 +196,8 @@
         own_couple, far_couple, wave_ref = refs[:3]
         wave = wave_ref[...]
         drives = (
-            applied(own_couple[...], to_first(wave)) - keep_ref[BND:],
-            applied(far_couple[...], wave) - came_ref[BND:],
+            applied(own_couple[...], wave) - keep_ref[BND:],
+            applied(far_couple[...], to_first(wave)) - came_ref[BND:],
         )
     parts = [applied(own_lift[...], drives[0]), applied(far_lift[...], drives[1])]
     for copy in copies:
@@ -312,7 +312,7 @@
         came = came_ref[beat * BND : (beat + 1) * BND]
         first = is_first(own)
         z = jnp.where(
-            lax.axis_index(C) == beat,
+            lax.axis_index(C) == 0,
             jnp.where(first, own, came),
             jnp.where(first, to_first(came), to_second(own)),
         )
@@ -376,7 +376,7 @@
 
     far_tree = swapped(own_tree, C)
     far_lift = swapped(lift[0], C)
-    far_sep = swapped(own_sep, C)
+    far_sep = swapped(in_hbm(own_sep), C)
     far_spread = swapped(own_spread, C)
     far_couple = swapped(kmat, C)
 
@@ -429,8 +429,7 @@
         extra = ()
         if beat:
             devices = lax.axis_size("slab")
-            route = [(2 * i + c, 2 * i + 3 - c) for i in range(devices - 1) for c in range(2)]
-            incoming = lax.ppermute(outgoing, ("slab", C), route)
+            incoming = lax.ppermute(outgoing, "slab", [(i, i + 1) for i in range(devices - 1)])
             extra = (kmat, far_couple, incoming)
         fetched = [
             pltpu.SMEM((P_SIZE,), jnp.int32),

time: 130 us -> 132 us (1.015)
  the two profiles are of different devices: /device:TPU:39 before, /device:TPU:33 now
where the time goes in v4:
time: 132 us
  starting transfers between devices  75.4 us (57%)
  waiting for transfers between devices  30.8 us (23%)
  Pallas kernels  22.8 us (17%)
  local copies, waits for them, and re-layouts  2.05 us (2%)
    ppermute x36, starting transfers between devices, shifted(): lax.ppermute(value, axis, [(i, (i + distance) % size) for i in range(size)])  72.2 us
    ppermute x36, waiting for transfers between devices, shifted(): lax.ppermute(value, axis, [(i, (i + distance) % size) for i in range(size)])  26.9 us
    pallas_call x2, Pallas kernels, sweep(): pl.pallas_call(sep_kernel, in_specs=[VM] * (NX + 2), out_specs=VM, out_sh...  6.25 us
    pallas_call x2, Pallas kernels, sweep(): pl.pallas_call(functools.partial(bulk_kernel, step), grid=(1,), in_specs=...  5.08 us
    ppermute x1, waiting for transfers between devices, sweep(): lax.ppermute(outgoing, 'slab', [(i, i + 1) for i in range(devices - 1)])  3.9 us
    pallas_call x2, Pallas kernels, sweep(): pl.pallas_call(functools.partial(lift_kernel, beat), in_specs=[SM if beat...  3.64 us
    pallas_call x2, Pallas kernels, sweep(): pl.pallas_call(functools.partial(spread_kernel, beat), in_specs=[SM, SM]...  3.56 us
    ppermute x1, starting transfers between devices, sweep(): lax.ppermute(outgoing, 'slab', [(i, i + 1) for i in range(devices - 1)])  3.2 us
  transfers between devices with their start and end apart: 37, of which 15 were waited for; matrix products, arithmetic and copies ran while one was open for 0% of the time, Pallas kernels for 11%

profile of v4, /device:TPU:33, one launch (start us, length us, event | category | flops | bytes accessed | tf_op | source)
XLA Modules:
  0.0 131.6 jit_solution(18278900657913450778)
XLA Ops:
  1.4 2.6 %start.1 = (f32[256,128]{1,0:T(8,128)S(1)}, f32[256,128]{1,0:T(8,128)S(1)}, f32[128,256]{1,0:T(8,128)S(1)}, f32[512,256]{1,0:T(8,128)S(1)}) custom-call(s32[4,16]{1,0:T(4,128)S(1)} %bitcast.22, f32[2,1,1024,128]{3,2,1,0:T(8,128)} %src_ref.5, f32[1,1024,512]{2,1,0:T(8,128)} %g_ref.1, f32[1,128,256]{2,1,0:T(8,128)} %couple_ref.1, f32[1,128,128]{2,1,0:T(8,128)} %wave_ref.1, ...), custom_call_target="tpu_custom_call" | custom-call | flops 201326592 | bytes 2097152 | tf_op jit(solution)/shard_map/start/pallas_call | solution.py:383
  5.7 1.8 %shard_map.91 = (f32[256,128]{1,0:T(8,128)S(1)}, f32[256,128]{1,0:T(8,128)S(1)}, f32[256,128]{1,0:T(8,128)S(1)}, f32[256,128]{1,0:T(8,128)S(1)}) custom-call(s32[4]{0:T(128)} %bitcast.25, s32[4]{0:T(128)S(1)} %collective-permute-done.far_tree, f32[256,128]{1,0:T(8,128)S(1)} %get-tuple-element.25.keep_ref.refs_8_, ...), custom_call_target="tpu_custom_call" | custom-call | flops 134217728 | bytes 1572864 | tf_op jit(solution)/shard_map/pallas_call | solution.py:439
  8.9 2.5 %collective-permute-start.6 = (f32[256,128]{1,0:T(8,128)S(1)}, f32[256,128]{1,0:T(8,128)S(1)}, u32[]{:S(2)}, u32[]{:S(2)}) collective-permute-start(f32[256,128]{1,0:T(8,128)S(1)} %get-tuple-element.30), channel_id=1, source_target_pairs={{0,8},{4,12},{8,0},{12,4},{1,9},{5,13},{9,1},{13,5},{2,10},{6,14},... | collective-permute-start | bytes 393224 | tf_op jit(solution)/shard_map/ppermute | solution.py:350
  13.6 3.8 %collective-permute-done.6 = f32[256,128]{1,0:T(8,128)S(1)} collective-permute-done((f32[256,128]{1,0:T(8,128)S(1)}, f32[256,128]{1,0:T(8,128)S(1)}, u32[]{:S(2)}, u32[]{:S(2)}) %collective-permute-start.6) | collective-permute-done | bytes 131104 | tf_op jit(solution)/shard_map/ppermute | solution.py:350
  17.5 6.1 %collective-permute-start.8 = (f32[256,128]{1,0:T(8,128)S(1)}, f32[256,128]{1,0:T(8,128)S(1)}, u32[]{:S(2)}, u32[]{:S(2)}) collective-permute-start(f32[256,128]{1,0:T(8,128)S(1)} %add_add_fusion.1), channel_id=1, source_target_pairs={{0,2},{2,0},{1,3},{3,1},{4,6},{6,4},{5,7},{7,5},{8,10},{10,8},{9,1... | collective-permute-start | bytes 393224 | tf_op jit(solution)/shard_map/ppermute | solution.py:350
  23.6 2.7 %collective-permute-done.8 = f32[256,128]{1,0:T(8,128)S(1)} collective-permute-done((f32[256,128]{1,0:T(8,128)S(1)}, f32[256,128]{1,0:T(8,128)S(1)}, u32[]{:S(2)}, u32[]{:S(2)}) %collective-permute-start.8) | collective-permute-done | bytes 131104 | tf_op jit(solution)/shard_map/ppermute | solution.py:350
  26.3 1.9 %collective-permute-start.10 = (f32[256,128]{1,0:T(8,128)S(1)}, f32[256,128]{1,0:T(8,128)S(1)}, u32[]{:S(2)}, u32[]{:S(2)}) collective-permute-start(f32[256,128]{1,0:T(8,128)S(1)} %add.27.refs_0_), channel_id=1, source_target_pairs={{0,8},{4,12},{8,0},{12,4},{1,9},{5,13},{9,1},{13,5},{2,10},{6,14},... | collective-permute-start | bytes 393224 | tf_op jit(solution)/shard_map/ppermute | solution.py:350
  28.2 1.6 %collective-permute-start.11 = (f32[256,128]{1,0:T(8,128)S(1)}, f32[256,128]{1,0:T(8,128)S(1)}, u32[]{:S(2)}, u32[]{:S(2)}) collective-permute-start(f32[256,128]{1,0:T(8,128)S(1)} %add.27.refs_0_), channel_id=1, source_target_pairs={{0,12},{4,0},{8,4},{12,8},{1,13},{5,1},{9,5},{13,9},{2,14},{6,2},{... | collective-permute-start | bytes 393224 | tf_op jit(solution)/shard_map/ppermute | solution.py:350
  29.8 1.9 %collective-permute-done.10.refs_2_ = f32[256,128]{1,0:T(8,128)S(1)} collective-permute-done((f32[256,128]{1,0:T(8,128)S(1)}, f32[256,128]{1,0:T(8,128)S(1)}, u32[]{:S(2)}, u32[]{:S(2)}) %collective-permute-start.10) | collective-permute-done | bytes 131104 | tf_op jit(solution)/shard_map/ppermute | solution.py:350
  31.7 5.7 %collective-permute-start.20 = (f32[128,256]{1,0:T(8,128)S(1)}, f32[128,256]{1,0:T(8,128)S(1)}, u32[]{:S(2)}, u32[]{:S(2)}) collective-permute-start(f32[128,256]{1,0:T(8,128)S(1)} %get-tuple-element.32.refs_10_), channel_id=1, source_target_pairs={{0,1},{1,0},{2,3},{3,2},{4,5},{5,4},{6,7},{7,6},{8,9},{9,8},{10,11... | collective-permute-start | bytes 393224 | tf_op jit(solution)/shard_map/ppermute | solution.py:350
  38.8 3.1 %shard_map.92.refs_0_ = f32[128,128]{1,0:T(8,128)S(1)} custom-call(f32[256,128]{1,0:T(8,128)S(1)} %add.27.refs_0_, f32[256,128]{1,0:T(8,128)S(1)} %collective-permute-done.9.refs_1_, f32[256,128]{1,0:T(8,128)S(1)} %collective-permute-done.10.refs_2_, f32[256,128]{1,0:T(8,128)S(1)} %collective-permute-done.11.refs_3_, f32[128,4096]{1,0:T(8,128)S(1)} %bitcast.15, ...), custom_call_target="tpu_custom_call" | custom-call | flops 536870912 | bytes 5242880 | tf_op jit(solution)/shard_map/pallas_call | solution.py:460
  41.9 5.5 %collective-permute-start.16 = (f32[128,128]{1,0:T(8,128)S(1)}, f32[128,128]{1,0:T(8,128)S(1)}, u32[]{:S(2)}, u32[]{:S(2)}) collective-permute-start(f32[128,128]{1,0:T(8,128)S(1)} %shard_map.92.refs_0_), channel_id=1, source_target_pairs={{0,2},{2,0},{1,3},{3,1},{4,6},{6,4},{5,7},{7,5},{8,10},{10,8},{9,1... | collective-permute-start | bytes 196616 | tf_op jit(solution)/shard_map/ppermute | solution.py:350
  48.6 2.0 %collective-permute-start.14 = (f32[128,128]{1,0:T(8,128)S(1)}, f32[128,128]{1,0:T(8,128)S(1)}, u32[]{:S(2)}, u32[]{:S(2)}) collective-permute-start(f32[128,128]{1,0:T(8,128)S(1)} %shard_map.92.refs_0_), channel_id=1, source_target_pairs={{0,8},{4,12},{8,0},{12,4},{1,9},{5,13},{9,1},{13,5},{2,10},{6,14},... | collective-permute-start | bytes 196616 | tf_op jit(solution)/shard_map/ppermute | solution.py:350
  54.6 5.6 %collective-permute-start.4 = (f32[128,256]{1,0:T(8,128)S(1)}, f32[128,256]{1,0:T(8,128)S(1)}, u32[]{:S(2)}, u32[]{:S(2)}) collective-permute-start(f32[128,256]{1,0:T(8,128)S(1)} %bitcast.20), channel_id=1, source_target_pairs={{0,1},{1,0},{2,3},{3,2},{4,5},{5,4},{6,7},{7,6},{8,9},{9,8},{10,11... | collective-permute-start | bytes 393224 | tf_op jit(solution)/shard_map/ppermute | solution.py:350
  60.3 2.0 %shard_map.93 = (f32[128,128]{1,0:T(8,128)S(1)}, f32[128,128]{1,0:T(8,128)S(1)}) custom-call(s32[4]{0:T(128)S(1)} %bitcast.27, s32[4]{0:T(128)S(1)} %collective-permute-done.far_tree, f32[128,1024]{1,0:T(8,128)S(1)} %bitcast.18, f32[128,1024]{1,0:T(8,128)S(1)} %collective-permute-done.1.far_mat, f32[128,128]{1,0:T(8,128)S(1)} %shard_map.92.refs_0_, ...), custom_call_target="tpu_custom_call" | custom-call | flops 134217728 | bytes 1572864 | tf_op jit(solution)/shard_map/pallas_call | solution.py:471
  62.3 3.2 %collective-permute-start.21 = (f32[128,128]{1,0:T(8,128)S(1)}, f32[128,128]{1,0:T(8,128)S(1)}, u32[]{:S(2)}, u32[]{:S(2)}) collective-permute-start(f32[128,128]{1,0:T(8,128)S(1)} %get-tuple-element.33), channel_id=1, source_target_pairs={{0,16},{16,32},{32,48},{48,64},{64,80},{80,96},{96,112},{112,128},... | collective-permute-start | bytes 196616 | tf_op jit(solution)/shard_map/ppermute | solution.py:432
  65.5 3.9 %collective-permute-done.21.refs_2_ = f32[128,128]{1,0:T(8,128)S(1)} collective-permute-done((f32[128,128]{1,0:T(8,128)S(1)}, f32[128,128]{1,0:T(8,128)S(1)}, u32[]{:S(2)}, u32[]{:S(2)}) %collective-permute-start.21) | collective-permute-done | bytes 65568 | tf_op jit(solution)/shard_map/ppermute | solution.py:432
  69.4 1.8 %shard_map.94 = (f32[256,128]{1,0:T(8,128)S(1)}, f32[256,128]{1,0:T(8,128)S(1)}, f32[256,128]{1,0:T(8,128)S(1)}, f32[256,128]{1,0:T(8,128)S(1)}) custom-call(s32[4]{0:T(128)S(1)} %bitcast.28, s32[4]{0:T(128)S(1)} %collective-permute-done.far_tree, f32[256,128]{1,0:T(8,128)S(1)} %get-tuple-element.25.keep_ref.refs_8_, ...), custom_call_target="tpu_custom_call" | custom-call | flops 134217728 | bytes 1572864 | tf_op jit(solution)/shard_map/pallas_call | solution.py:439
  74.3 3.5 %collective-permute-done.22 = f32[256,128]{1,0:T(8,128)S(1)} collective-permute-done((f32[256,128]{1,0:T(8,128)S(1)}, f32[256,128]{1,0:T(8,128)S(1)}, u32[]{:S(2)}, u32[]{:S(2)}) %collective-permute-start.22) | collective-permute-done | bytes 131104 | tf_op jit(solution)/shard_map/ppermute | solution.py:350
  78.4 2.7 %collective-permute-start.25 = (f32[256,128]{1,0:T(8,128)S(1)}, f32[256,128]{1,0:T(8,128)S(1)}, u32[]{:S(2)}, u32[]{:S(2)}) collective-permute-start(f32[256,128]{1,0:T(8,128)S(1)} %add_add_fusion), channel_id=1, source_target_pairs={{0,2},{2,0},{1,3},{3,1},{4,6},{6,4},{5,7},{7,5},{8,10},{10,8},{9,1... | collective-permute-start | bytes 393224 | tf_op jit(solution)/shard_map/ppermute | solution.py:350
  81.1 6.5 %collective-permute-done.25 = f32[256,128]{1,0:T(8,128)S(1)} collective-permute-done((f32[256,128]{1,0:T(8,128)S(1)}, f32[256,128]{1,0:T(8,128)S(1)}, u32[]{:S(2)}, u32[]{:S(2)}) %collective-permute-start.25) | collective-permute-done | bytes 131104 | tf_op jit(solution)/shard_map/ppermute | solution.py:350
  88.0 3.3 %collective-permute-start.27 = (f32[256,128]{1,0:T(8,128)S(1)}, f32[256,128]{1,0:T(8,128)S(1)}, u32[]{:S(2)}, u32[]{:S(2)}) collective-permute-start(f32[256,128]{1,0:T(8,128)S(1)} %add.31.refs_0_), channel_id=1, source_target_pairs={{0,8},{4,12},{8,0},{12,4},{1,9},{5,13},{9,1},{13,5},{2,10},{6,14},... | collective-permute-start | bytes 393224 | tf_op jit(solution)/shard_map/ppermute | solution.py:350
  91.2 1.8 %collective-permute-done.26.refs_1_ = f32[256,128]{1,0:T(8,128)S(1)} collective-permute-done((f32[256,128]{1,0:T(8,128)S(1)}, f32[256,128]{1,0:T(8,128)S(1)}, u32[]{:S(2)}, u32[]{:S(2)}) %collective-permute-start.26) | collective-permute-done | bytes 131104 | tf_op jit(solution)/shard_map/ppermute | solution.py:350
  93.1 1.9 %collective-permute-done.27.refs_2_ = f32[256,128]{1,0:T(8,128)S(1)} collective-permute-done((f32[256,128]{1,0:T(8,128)S(1)}, f32[256,128]{1,0:T(8,128)S(1)}, u32[]{:S(2)}, u32[]{:S(2)}) %collective-permute-start.27) | collective-permute-done | bytes 131104 | tf_op jit(solution)/shard_map/ppermute | solution.py:350
  95.1 3.1 %shard_map.95.refs_0_ = f32[128,128]{1,0:T(8,128)S(1)} custom-call(f32[256,128]{1,0:T(8,128)S(1)} %add.31.refs_0_, f32[256,128]{1,0:T(8,128)S(1)} %collective-permute-done.26.refs_1_, f32[256,128]{1,0:T(8,128)S(1)} %collective-permute-done.27.refs_2_, f32[256,128]{1,0:T(8,128)S(1)} %collective-permute-done.28.refs_3_, f32[128,4096]{1,0:T(8,128)S(1)} %bitcast.16, ...), custom_call_target="tpu_custom_call" | custom-call | flops 536870912 | bytes 5242880 | tf_op jit(solution)/shard_map/pallas_call | solution.py:460
  98.2 2.8 %collective-permute-start.32 = (f32[128,128]{1,0:T(8,128)S(1)}, f32[128,128]{1,0:T(8,128)S(1)}, u32[]{:S(2)}, u32[]{:S(2)}) collective-permute-start(f32[128,128]{1,0:T(8,128)S(1)} %shard_map.95.refs_0_), channel_id=1, source_target_pairs={{0,2},{2,0},{1,3},{3,1},{4,6},{6,4},{5,7},{7,5},{8,10},{10,8},{9,1... | collective-permute-start | bytes 196616 | tf_op jit(solution)/shard_map/ppermute | solution.py:350
  102.1 2.5 %collective-permute-start.30 = (f32[128,128]{1,0:T(8,128)S(1)}, f32[128,128]{1,0:T(8,128)S(1)}, u32[]{:S(2)}, u32[]{:S(2)}) collective-permute-start(f32[128,128]{1,0:T(8,128)S(1)} %shard_map.95.refs_0_), channel_id=1, source_target_pairs={{0,8},{4,12},{8,0},{12,4},{1,9},{5,13},{9,1},{13,5},{2,10},{6,14},... | collective-permute-start | bytes 196616 | tf_op jit(solution)/shard_map/ppermute | solution.py:350
  106.0 2.6 %collective-permute-start.34 = (f32[128,128]{1,0:T(8,128)S(1)}, f32[128,128]{1,0:T(8,128)S(1)}, u32[]{:S(2)}, u32[]{:S(2)}) collective-permute-start(f32[128,128]{1,0:T(8,128)S(1)} %collective-permute-done.32.refs_4_), channel_id=1, source_target_pairs={{0,8},{4,12},{8,0},{12,4},{1,9},{5,13},{9,1},{13,5},{2,10},{6,14},... | collective-permute-start | bytes 196616 | tf_op jit(solution)/shard_map/ppermute | solution.py:350
  113.3 11.3 %collective-permute-start.36 = (f32[256,128]{1,0:T(8,128)S(1)}, f32[256,128]{1,0:T(8,128)S(1)}, u32[]{:S(2)}, u32[]{:S(2)}) collective-permute-start(f32[256,128]{1,0:T(8,128)S(1)} %shard_map.96.own_ref), channel_id=1, source_target_pairs={{0,1},{1,0},{2,3},{3,2},{4,5},{5,4},{6,7},{7,6},{8,9},{9,8},{10,11... | collective-permute-start | bytes 393224 | tf_op jit(solution)/shard_map/ppermute | solution.py:350
  124.5 2.5 %shard_map.97 = (f32[512,128]{1,0:T(8,128)S(1)}, f32[512,128]{1,0:T(8,128)S(1)}, bf16[1024,256]{1,0:T(8,128)(2,1)S(1)}) custom-call(s32[4,16]{1,0:T(4,128)S(1)} %bitcast.23, f32[2,1,1024,128]{3,2,1,0:T(8,128)S(1)} %copy-done.1, f32[1024,512]{1,0:T(8,128)S(1)} %bitcast.12), custom_call_target="tpu_custom_call" | custom-call | flops 805306368 | bytes 3145728 | tf_op jit(solution)/shard_map/pallas_call | solution.py:404
  127.1 2.6 %shard_map.98 = (f32[512,128]{1,0:T(8,128)S(1)}, f32[512,128]{1,0:T(8,128)S(1)}, bf16[1024,256]{1,0:T(8,128)(2,1)S(1)}) custom-call(s32[4,16]{1,0:T(4,128)S(1)} %bitcast.24, f32[2,1,1024,128]{3,2,1,0:T(8,128)S(1)} %copy-done.1, f32[1024,512]{1,0:T(8,128)S(1)} %bitcast.13), custom_call_target="tpu_custom_call" | custom-call | flops 805306368 | bytes 3145728 | tf_op jit(solution)/shard_map/pallas_call | solution.py:404
  129.6 1.7 %field.1 = f32[2,1024,128]{2,1,0:T(8,128)} custom-call(f32[256,128]{1,0:T(8,128)S(1)} %shard_map.96.own_ref, f32[256,128]{1,0:T(8,128)S(1)} %collective-permute-done.36.came_ref, f32[512,128]{1,0:T(8,128)S(1)} %get-tuple-element.39.refs_0_, f32[512,128]{1,0:T(8,128)S(1)} %get-tuple-element.40.refs_1_, f32[512,128]{1,0:T(8,128)S(1)} %get-tuple-element.41.refs_2_, ...), custom_call_target="tpu_custom_call" | custom-call | flops 536870912 | bytes 3145728 | tf_op jit(solution)/shard_map/field/pallas_call | solution.py:482
  (76 shorter events, 24.6 us)
Async XLA Ops:
  0.0 37.5 %collective-permute-start.12 = (f32[128,4096]{1,0:T(8,128)}, f32[128,4096]{1,0:T(8,128)S(1)}, u32[]{:S(2)}, u32[]{:S(2)}) collective-permute-start(f32[128,4096]{1,0:T(8,128)} %bitcast.14), channel_id=1, source_target_pairs={{0,1},{1,0},{2,3},{3,2},{4,5},{5,4},{6,7},{7,6},{8,9},{9,8},{10,11... | collective-permute-start | bytes 6291464 | tf_op jit(solution)/shard_map/ppermute | solution.py:350
  0.7 5.0 %collective-permute-start.3 = (f32[512,256]{1,0:T(8,128)}, f32[512,256]{1,0:T(8,128)S(1)}, u32[]{:S(2)}, u32[]{:S(2)}) collective-permute-start(f32[512,256]{1,0:T(8,128)} %bitcast.30), channel_id=1, source_target_pairs={{0,1},{1,0},{2,3},{3,2},{4,5},{5,4},{6,7},{7,6},{8,9},{9,8},{10,11... | collective-permute-start | bytes 1572872 | tf_op jit(solution)/shard_map/ppermute | solution.py:350
  7.6 6.1 %collective-permute-start.5 = (f32[256,128]{1,0:T(8,128)S(1)}, f32[256,128]{1,0:T(8,128)S(1)}, u32[]{:S(2)}, u32[]{:S(2)}) collective-permute-start(f32[256,128]{1,0:T(8,128)S(1)} %get-tuple-element.29), channel_id=1, source_target_pairs={{0,4},{4,8},{8,12},{12,0},{1,5},{5,9},{9,13},{13,1},{2,6},{6,10},{... | collective-permute-start | bytes 393224 | tf_op jit(solution)/shard_map/ppermute | solution.py:350
  8.9 8.6 %collective-permute-start.6 = (f32[256,128]{1,0:T(8,128)S(1)}, f32[256,128]{1,0:T(8,128)S(1)}, u32[]{:S(2)}, u32[]{:S(2)}) collective-permute-start(f32[256,128]{1,0:T(8,128)S(1)} %get-tuple-element.30), channel_id=1, source_target_pairs={{0,8},{4,12},{8,0},{12,4},{1,9},{5,13},{9,1},{13,5},{2,10},{6,14},... | collective-permute-start | bytes 393224 | tf_op jit(solution)/shard_map/ppermute | solution.py:350
  11.3 6.1 %collective-permute-start.7 = (f32[256,128]{1,0:T(8,128)S(1)}, f32[256,128]{1,0:T(8,128)S(1)}, u32[]{:S(2)}, u32[]{:S(2)}) collective-permute-start(f32[256,128]{1,0:T(8,128)S(1)} %get-tuple-element.31), channel_id=1, source_target_pairs={{0,12},{4,0},{8,4},{12,8},{1,13},{5,1},{9,5},{13,9},{2,14},{6,2},{... | collective-permute-start | bytes 393224 | tf_op jit(solution)/shard_map/ppermute | solution.py:350
  12.5 39.7 %collective-permute-start.1 = (f32[128,1024]{1,0:T(8,128)S(1)}, f32[128,1024]{1,0:T(8,128)S(1)}, u32[]{:S(2)}, u32[]{:S(2)}) collective-permute-start(f32[128,1024]{1,0:T(8,128)S(1)} %bitcast.17), channel_id=1, source_target_pairs={{0,1},{1,0},{2,3},{3,2},{4,5},{5,4},{6,7},{7,6},{8,9},{9,8},{10,11... | collective-permute-start | bytes 1572872 | tf_op jit(solution)/shard_map/ppermute | solution.py:350
  17.5 8.8 %collective-permute-start.8 = (f32[256,128]{1,0:T(8,128)S(1)}, f32[256,128]{1,0:T(8,128)S(1)}, u32[]{:S(2)}, u32[]{:S(2)}) collective-permute-start(f32[256,128]{1,0:T(8,128)S(1)} %add_add_fusion.1), channel_id=1, source_target_pairs={{0,2},{2,0},{1,3},{3,1},{4,6},{6,4},{5,7},{7,5},{8,10},{10,8},{9,1... | collective-permute-start | bytes 393224 | tf_op jit(solution)/shard_map/ppermute | solution.py:350
  26.3 5.4 %collective-permute-start.10 = (f32[256,128]{1,0:T(8,128)S(1)}, f32[256,128]{1,0:T(8,128)S(1)}, u32[]{:S(2)}, u32[]{:S(2)}) collective-permute-start(f32[256,128]{1,0:T(8,128)S(1)} %add.27.refs_0_), channel_id=1, source_target_pairs={{0,8},{4,12},{8,0},{12,4},{1,9},{5,13},{9,1},{13,5},{2,10},{6,14},... | collective-permute-start | bytes 393224 | tf_op jit(solution)/shard_map/ppermute | solution.py:350
  28.2 9.3 %collective-permute-start.11 = (f32[256,128]{1,0:T(8,128)S(1)}, f32[256,128]{1,0:T(8,128)S(1)}, u32[]{:S(2)}, u32[]{:S(2)}) collective-permute-start(f32[256,128]{1,0:T(8,128)S(1)} %add.27.refs_0_), channel_id=1, source_target_pairs={{0,12},{4,0},{8,4},{12,8},{1,13},{5,1},{9,5},{13,9},{2,14},{6,2},{... | collective-permute-start | bytes 393224 | tf_op jit(solution)/shard_map/ppermute | solution.py:350
  29.8 7.7 %collective-permute-start.9 = (f32[256,128]{1,0:T(8,128)S(1)}, f32[256,128]{1,0:T(8,128)S(1)}, u32[]{:S(2)}, u32[]{:S(2)}) collective-permute-start(f32[256,128]{1,0:T(8,128)S(1)} %add.27.refs_0_), channel_id=1, source_target_pairs={{0,4},{4,8},{8,12},{12,0},{1,5},{5,9},{9,13},{13,1},{2,6},{6,10},{... | collective-permute-start | bytes 393224 | tf_op jit(solution)/shard_map/ppermute | solution.py:350
  31.7 18.9 %collective-permute-start.20 = (f32[128,256]{1,0:T(8,128)S(1)}, f32[128,256]{1,0:T(8,128)S(1)}, u32[]{:S(2)}, u32[]{:S(2)}) collective-permute-start(f32[128,256]{1,0:T(8,128)S(1)} %get-tuple-element.32.refs_10_), channel_id=1, source_target_pairs={{0,1},{1,0},{2,3},{3,2},{4,5},{5,4},{6,7},{7,6},{8,9},{9,8},{10,11... | collective-permute-start | bytes 393224 | tf_op jit(solution)/shard_map/ppermute | solution.py:350
  41.9 9.9 %collective-permute-start.16 = (f32[128,128]{1,0:T(8,128)S(1)}, f32[128,128]{1,0:T(8,128)S(1)}, u32[]{:S(2)}, u32[]{:S(2)}) collective-permute-start(f32[128,128]{1,0:T(8,128)S(1)} %shard_map.92.refs_0_), channel_id=1, source_target_pairs={{0,2},{2,0},{1,3},{3,1},{4,6},{6,4},{5,7},{7,5},{8,10},{10,8},{9,1... | collective-permute-start | bytes 196616 | tf_op jit(solution)/shard_map/ppermute | solution.py:350
  47.5 5.7 %collective-permute-start.13 = (f32[128,128]{1,0:T(8,128)S(1)}, f32[128,128]{1,0:T(8,128)S(1)}, u32[]{:S(2)}, u32[]{:S(2)}) collective-permute-start(f32[128,128]{1,0:T(8,128)S(1)} %shard_map.92.refs_0_), channel_id=1, source_target_pairs={{0,4},{4,8},{8,12},{12,0},{1,5},{5,9},{9,13},{13,1},{2,6},{6,10},{... | collective-permute-start | bytes 196616 | tf_op jit(solution)/shard_map/ppermute | solution.py:350
  48.6 6.0 %collective-permute-start.14 = (f32[128,128]{1,0:T(8,128)S(1)}, f32[128,128]{1,0:T(8,128)S(1)}, u32[]{:S(2)}, u32[]{:S(2)}) collective-permute-start(f32[128,128]{1,0:T(8,128)S(1)} %shard_map.92.refs_0_), channel_id=1, source_target_pairs={{0,8},{4,12},{8,0},{12,4},{1,9},{5,13},{9,1},{13,5},{2,10},{6,14},... | collective-permute-start | bytes 196616 | tf_op jit(solution)/shard_map/ppermute | solution.py:350
  50.7 9.6 %collective-permute-start.15 = (f32[128,128]{1,0:T(8,128)S(1)}, f32[128,128]{1,0:T(8,128)S(1)}, u32[]{:S(2)}, u32[]{:S(2)}) collective-permute-start(f32[128,128]{1,0:T(8,128)S(1)} %shard_map.92.refs_0_), channel_id=1, source_target_pairs={{0,12},{4,0},{8,4},{12,8},{1,13},{5,1},{9,5},{13,9},{2,14},{6,2},{... | collective-permute-start | bytes 196616 | tf_op jit(solution)/shard_map/ppermute | solution.py:350
  51.9 8.4 %collective-permute-start.17 = (f32[128,128]{1,0:T(8,128)S(1)}, f32[128,128]{1,0:T(8,128)S(1)}, u32[]{:S(2)}, u32[]{:S(2)}) collective-permute-start(f32[128,128]{1,0:T(8,128)S(1)} %collective-permute-done.16.refs_4_), channel_id=1, source_target_pairs={{0,4},{4,8},{8,12},{12,0},{1,5},{5,9},{9,13},{13,1},{2,6},{6,10},{... | collective-permute-start | bytes 196616 | tf_op jit(solution)/shard_map/ppermute | solution.py:350
  52.1 8.2 %collective-permute-start.18 = (f32[128,128]{1,0:T(8,128)S(1)}, f32[128,128]{1,0:T(8,128)S(1)}, u32[]{:S(2)}, u32[]{:S(2)}) collective-permute-start(f32[128,128]{1,0:T(8,128)S(1)} %collective-permute-done.16.refs_4_), channel_id=1, source_target_pairs={{0,8},{4,12},{8,0},{12,4},{1,9},{5,13},{9,1},{13,5},{2,10},{6,14},... | collective-permute-start | bytes 196616 | tf_op jit(solution)/shard_map/ppermute | solution.py:350
  53.1 7.2 %collective-permute-start.19 = (f32[128,128]{1,0:T(8,128)S(1)}, f32[128,128]{1,0:T(8,128)S(1)}, u32[]{:S(2)}, u32[]{:S(2)}) collective-permute-start(f32[128,128]{1,0:T(8,128)S(1)} %collective-permute-done.16.refs_4_), channel_id=1, source_target_pairs={{0,12},{4,0},{8,4},{12,8},{1,13},{5,1},{9,5},{13,9},{2,14},{6,2},{... | collective-permute-start | bytes 196616 | tf_op jit(solution)/shard_map/ppermute | solution.py:350
  54.6 10.9 %collective-permute-start.4 = (f32[128,256]{1,0:T(8,128)S(1)}, f32[128,256]{1,0:T(8,128)S(1)}, u32[]{:S(2)}, u32[]{:S(2)}) collective-permute-start(f32[128,256]{1,0:T(8,128)S(1)} %bitcast.20), channel_id=1, source_target_pairs={{0,1},{1,0},{2,3},{3,2},{4,5},{5,4},{6,7},{7,6},{8,9},{9,8},{10,11... | collective-permute-start | bytes 393224 | tf_op jit(solution)/shard_map/ppermute | solution.py:350
  62.3 7.1 %collective-permute-start.21 = (f32[128,128]{1,0:T(8,128)S(1)}, f32[128,128]{1,0:T(8,128)S(1)}, u32[]{:S(2)}, u32[]{:S(2)}) collective-permute-start(f32[128,128]{1,0:T(8,128)S(1)} %get-tuple-element.33), channel_id=1, source_target_pairs={{0,16},{16,32},{32,48},{48,64},{64,80},{80,96},{96,112},{112,128},... | collective-permute-start | bytes 196616 | tf_op jit(solution)/shard_map/ppermute | solution.py:432
  71.2 6.5 %collective-permute-start.22 = (f32[256,128]{1,0:T(8,128)S(1)}, f32[256,128]{1,0:T(8,128)S(1)}, u32[]{:S(2)}, u32[]{:S(2)}) collective-permute-start(f32[256,128]{1,0:T(8,128)S(1)} %get-tuple-element.35), channel_id=1, source_target_pairs={{0,4},{4,8},{8,12},{12,0},{1,5},{5,9},{9,13},{13,1},{2,6},{6,10},{... | collective-permute-start | bytes 393224 | tf_op jit(solution)/shard_map/ppermute | solution.py:350
  71.8 6.0 %collective-permute-start.23 = (f32[256,128]{1,0:T(8,128)S(1)}, f32[256,128]{1,0:T(8,128)S(1)}, u32[]{:S(2)}, u32[]{:S(2)}) collective-permute-start(f32[256,128]{1,0:T(8,128)S(1)} %get-tuple-element.36), channel_id=1, source_target_pairs={{0,8},{4,12},{8,0},{12,4},{1,9},{5,13},{9,1},{13,5},{2,10},{6,14},... | collective-permute-start | bytes 393224 | tf_op jit(solution)/shard_map/ppermute | solution.py:350
  73.3 5.1 %collective-permute-start.24 = (f32[256,128]{1,0:T(8,128)S(1)}, f32[256,128]{1,0:T(8,128)S(1)}, u32[]{:S(2)}, u32[]{:S(2)}) collective-permute-start(f32[256,128]{1,0:T(8,128)S(1)} %get-tuple-element.37), channel_id=1, source_target_pairs={{0,12},{4,0},{8,4},{12,8},{1,13},{5,1},{9,5},{13,9},{2,14},{6,2},{... | collective-permute-start | bytes 393224 | tf_op jit(solution)/shard_map/ppermute | solution.py:350
  78.4 9.2 %collective-permute-start.25 = (f32[256,128]{1,0:T(8,128)S(1)}, f32[256,128]{1,0:T(8,128)S(1)}, u32[]{:S(2)}, u32[]{:S(2)}) collective-permute-start(f32[256,128]{1,0:T(8,128)S(1)} %add_add_fusion), channel_id=1, source_target_pairs={{0,2},{2,0},{1,3},{3,1},{4,6},{6,4},{5,7},{7,5},{8,10},{10,8},{9,1... | collective-permute-start | bytes 393224 | tf_op jit(solution)/shard_map/ppermute | solution.py:350
  87.7 5.4 %collective-permute-start.26 = (f32[256,128]{1,0:T(8,128)S(1)}, f32[256,128]{1,0:T(8,128)S(1)}, u32[]{:S(2)}, u32[]{:S(2)}) collective-permute-start(f32[256,128]{1,0:T(8,128)S(1)} %add.31.refs_0_), channel_id=1, source_target_pairs={{0,4},{4,8},{8,12},{12,0},{1,5},{5,9},{9,13},{13,1},{2,6},{6,10},{... | collective-permute-start | bytes 393224 | tf_op jit(solution)/shard_map/ppermute | solution.py:350
  88.0 7.0 %collective-permute-start.27 = (f32[256,128]{1,0:T(8,128)S(1)}, f32[256,128]{1,0:T(8,128)S(1)}, u32[]{:S(2)}, u32[]{:S(2)}) collective-permute-start(f32[256,128]{1,0:T(8,128)S(1)} %add.31.refs_0_), channel_id=1, source_target_pairs={{0,8},{4,12},{8,0},{12,4},{1,9},{5,13},{9,1},{13,5},{2,10},{6,14},... | collective-permute-start | bytes 393224 | tf_op jit(solution)/shard_map/ppermute | solution.py:350
  98.2 7.2 %collective-permute-start.32 = (f32[128,128]{1,0:T(8,128)S(1)}, f32[128,128]{1,0:T(8,128)S(1)}, u32[]{:S(2)}, u32[]{:S(2)}) collective-permute-start(f32[128,128]{1,0:T(8,128)S(1)} %shard_map.95.refs_0_), channel_id=1, source_target_pairs={{0,2},{2,0},{1,3},{3,1},{4,6},{6,4},{5,7},{7,5},{8,10},{10,8},{9,1... | collective-permute-start | bytes 196616 | tf_op jit(solution)/shard_map/ppermute | solution.py:350
  101.0 7.6 %collective-permute-start.29 = (f32[128,128]{1,0:T(8,128)S(1)}, f32[128,128]{1,0:T(8,128)S(1)}, u32[]{:S(2)}, u32[]{:S(2)}) collective-permute-start(f32[128,128]{1,0:T(8,128)S(1)} %shard_map.95.refs_0_), channel_id=1, source_target_pairs={{0,4},{4,8},{8,12},{12,0},{1,5},{5,9},{9,13},{13,1},{2,6},{6,10},{... | collective-permute-start | bytes 196616 | tf_op jit(solution)/shard_map/ppermute | solution.py:350
  102.1 6.8 %collective-permute-start.30 = (f32[128,128]{1,0:T(8,128)S(1)}, f32[128,128]{1,0:T(8,128)S(1)}, u32[]{:S(2)}, u32[]{:S(2)}) collective-permute-start(f32[128,128]{1,0:T(8,128)S(1)} %shard_map.95.refs_0_), channel_id=1, source_target_pairs={{0,8},{4,12},{8,0},{12,4},{1,9},{5,13},{9,1},{13,5},{2,10},{6,14},... | collective-permute-start | bytes 196616 | tf_op jit(solution)/shard_map/ppermute | solution.py:350
  104.5 4.3 %collective-permute-start.31 = (f32[128,128]{1,0:T(8,128)S(1)}, f32[128,128]{1,0:T(8,128)S(1)}, u32[]{:S(2)}, u32[]{:S(2)}) collective-permute-start(f32[128,128]{1,0:T(8,128)S(1)} %shard_map.95.refs_0_), channel_id=1, source_target_pairs={{0,12},{4,0},{8,4},{12,8},{1,13},{5,1},{9,5},{13,9},{2,14},{6,2},{... | collective-permute-start | bytes 196616 | tf_op jit(solution)/shard_map/ppermute | solution.py:350
  106.0 4.9 %collective-permute-start.34 = (f32[128,128]{1,0:T(8,128)S(1)}, f32[128,128]{1,0:T(8,128)S(1)}, u32[]{:S(2)}, u32[]{:S(2)}) collective-permute-start(f32[128,128]{1,0:T(8,128)S(1)} %collective-permute-done.32.refs_4_), channel_id=1, source_target_pairs={{0,8},{4,12},{8,0},{12,4},{1,9},{5,13},{9,1},{13,5},{2,10},{6,14},... | collective-permute-start | bytes 196616 | tf_op jit(solution)/shard_map/ppermute | solution.py:350
  113.3 16.4 %collective-permute-start.36 = (f32[256,128]{1,0:T(8,128)S(1)}, f32[256,128]{1,0:T(8,128)S(1)}, u32[]{:S(2)}, u32[]{:S(2)}) collective-permute-start(f32[256,128]{1,0:T(8,128)S(1)} %shard_map.96.own_ref), channel_id=1, source_target_pairs={{0,1},{1,0},{2,3},{3,2},{4,5},{5,4},{6,7},{7,6},{8,9},{9,8},{10,11... | collective-permute-start | bytes 393224 | tf_op jit(solution)/shard_map/ppermute | solution.py:350
  (15 other events, 228.7 us)
